TPU v7x, 32 devices: a whole 2x2x4 slice. The times are simulated.
32 devices in a mesh: groups: 2 (over y), feat: 4 (over z), pts: 2 (over x), sub: 2 (over core).
Axes of the slice: x: 2, y: 2, z: 4, core: 2. Of those that a mesh axis runs over, the one named last changes fastest.
Arguments:
- points: bfloat16 [256, 256], P(('groups', 'pts')), parts along dimension 0, may hold values from -6 to 6
- freqs: bfloat16 [256, 65536], P(None, ('feat', 'sub')), may hold values from -0.75 to 0.75
- phases: float32 [65536], P(('feat', 'sub')), may hold values from 0 to 6.283
- basis: bfloat16 [131072, 1024], P(('groups', 'feat', 'sub'), 'pts'), parts along dimension 0, may hold values from -0.0203125 to 0.0203125
Outputs:
- coefs: float32 [2048, 128], P('groups', 'pts'), parts along dimension 0
- new_basis: float32 [131072, 128], P(('groups', 'feat', 'sub'), 'pts'), parts along dimension 0
- factor: float32 [256, 128], P(('groups', 'pts')), parts along dimension 0
There are 2 independent parts, one for each index of `groups`. A program takes and returns all parts, laid end to end along the dimension named above; an argument that names none is the same for every part. Nothing has to cross between parts.
All inputs are finite; a program needn't handle non-finite values.
Results may differ from a plain program's by a relative error of at most 0.00055.
Values may be sent and summed in bfloat16 or wider, within the bound.
No kernel may reach another device: no remote copies, remote signals or barrier semaphores. Data moves between devices by JAX's collectives and lax.ppermute only.
A program may use at most 128 MiB of HBM per device.

v0:
```python
import jax
import jax.numpy as jnp
from jax import lax
from jax.sharding import PartitionSpec as P

FEATS = 65536


def on_device(points, freqs, phases, basis):
    highest = lax.Precision.HIGHEST
    phase_in = jnp.einsum("pd,df->fp", points, freqs, preferred_element_type=jnp.float32)
    features = jnp.cos(phase_in + phases[:, None])
    point_cols = features.shape[1]
    whole_basis = lax.all_gather(basis, "pts", axis=1, tiled=True).astype(jnp.float32)
    partial_value = jnp.einsum("fk,fp->kp", whole_basis, features, precision=highest)
    coefs = lax.psum(partial_value, ("feat", "sub"))
    fitted = jnp.dot(whole_basis, coefs, precision=highest)
    residual = features - fitted
    spread = lax.all_gather(residual, "pts", axis=1, tiled=True)
    block = jnp.einsum("fq,fp->qp", spread, residual, precision=highest)
    total_pts = block.shape[0]
    block = lax.psum(block, ("feat", "sub")) / FEATS
    gram = lax.all_gather(block, "pts", axis=1, tiled=True)
    factor = jnp.linalg.cholesky(gram)
    eye_mat = jnp.eye(total_pts, dtype=jnp.float32)
    inverse = jax.scipy.linalg.solve_triangular(factor, eye_mat, lower=True)
    offset = lax.axis_index("pts") * point_cols
    factor_rows = lax.dynamic_slice_in_dim(factor, offset, point_cols, 0)
    inv_rows = lax.dynamic_slice_in_dim(inverse, offset, point_cols, 0)
    new_basis = jnp.einsum("fq,pq->fp", spread, inv_rows, precision=highest)
    return (coefs, new_basis, factor_rows)


def solution(mesh):
    return jax.shard_map(
        on_device,
        mesh=mesh,
        in_specs=(
            P(("groups", "pts"), None),
            P(None, ("feat", "sub")),
            P(("feat", "sub")),
            P(("groups", "feat", "sub"), "pts"),
        ),
        out_specs=(
            P("groups", "pts"),
            P(("groups", "feat", "sub"), "pts"),
            P(("groups", "pts"), None),
        ),
        check_vma=False,
    )
```

profile of v0, /device:TPU:0, one launch (start us, length us, event | category | flops | bytes accessed | tf_op | source)
XLA Modules:
  0.0 432.8 jit_solution(4371246499104111773)
XLA Ops:
  7.2 0.0 copy-start
  7.2 0.0 copy-start.2
  7.2 0.0 all-gather.3.cloned.1.call-start
  7.2 0.7 all-gather.3.cloned.1.call-update
  7.9 0.0 all-reduce.2.cloned.1.call-start
  8.0 0.0 copy-done
  8.0 0.0 copy-done.2
  8.0 8.7 %fusion = f32[8192,64]{0,1:T(8,128)S(1)} fusion(bf16[64,256]{1,0:T(8,128)(2,1)S(1)} %copy-done, bf16[256,8192]{1,0:T(8,128)(2,1)} %param.5, f32[8192]{0:T(1024)S(1)} %copy-done.2), kind=kOutput, calls=%fused_computation.1 | convolution fusion | flops 268959744 | bytes 6356992 | tf_op jit(solution)/shard_map/pd,df->fp/dot_general | solution.py:11
  16.7 194.4 %all-gather.3.cloned.1.call-done = bf16[8192,1024]{1,0:T(8,128)(2,1)} async-done(((bf16[8192,512]{1,0:T(8,128)(2,1)}), bf16[8192,1024]{1,0:T(8,128)(2,1)}) %all-gather.3.cloned.1.call-update) | async-done | bytes 16777232 | tf_op jit(solution)/shard_map/all_gather | solution.py:14
  211.2 13.1 %convolution_bitcast_fusion.1 = f32[1024,64]{0,1:T(8,128)} fusion(f32[8192,64]{0,1:T(8,128)S(1)} %fusion, bf16[8192,1024]{1,0:T(8,128)(2,1)} %all-gather.3.cloned.1.call-done), kind=kOutput, calls=%fused_computation.4 | convolution fusion | flops 6442450944 | bytes 19136512 | tf_op jit(solution)/shard_map/fk,fp->kp/dot_general | solution.py:15
  224.3 0.0 all-reduce.2.cloned.1.call-update
  224.3 0.2 all-gather.5.cloned.1.call-start
  224.5 54.8 %all-reduce.2.cloned.1.call-done = f32[1024,64]{0,1:T(8,128)} async-done(((f32[1024,64]{0,1:T(8,128)}), f32[1024,64]{0,1:T(8,128)}) %all-reduce.2.cloned.1.call-update) | async-done | bytes 262160 | tf_op jit(solution)/shard_map/psum | solution.py:16
  279.4 19.7 %fusion.1 = f32[8192,64]{0,1:T(8,128)} fusion(f32[8192,64]{0,1:T(8,128)S(1)} %fusion, f32[1024,64]{0,1:T(8,128)} %all-reduce.2.cloned.1.call-done, bf16[8192,1024]{1,0:T(8,128)(2,1)} %all-gather.3.cloned.1.call-done), kind=kOutput, calls=%fused_computation.3 | convolution fusion | flops 6442975232 | bytes 21233664 | tf_op jit(solution)/shard_map/dot_general | solution.py:17
  299.1 0.0 all-gather.5.cloned.1.call-update
  299.1 55.9 %all-gather.5.cloned.1.call-done = f32[8192,128]{0,1:T(8,128)} async-done(((f32[8192,64]{0,1:T(8,128)}), f32[8192,128]{0,1:T(8,128)}) %all-gather.5.cloned.1.call-update) | async-done | bytes 4194320 | tf_op jit(solution)/shard_map/all_gather | solution.py:19
  355.0 7.3 %fusion.8 = f32[128,64]{0,1:T(8,128)S(1)} fusion(f32[8192,128]{0,1:T(8,128)} %all-gather.5.cloned.1.call-done, f32[8192,64]{0,1:T(8,128)} %fusion.1), kind=kOutput, calls=%fused_computation.20 | convolution fusion | flops 805306368 | bytes 6324224 | tf_op jit(solution)/shard_map/fq,fp->qp/dot_general | solution.py:20
  362.3 0.0 copy-start.1
  362.3 28.7 %psum.15 = f32[128,64]{0,1:T(8,128)S(1)} all-reduce(f32[128,64]{0,1:T(8,128)S(1)} %fusion.8), channel_id=1, replica_groups=mesh['groups'=2,'feat'=4,'pts'=2,'sub'=2] {'feat','sub'}, use_global_device_ids=true, to_apply=%region_1.0 | all-reduce | flops 8192 | bytes 65536 | tf_op jit(solution)/shard_map/psum | solution.py:22
  391.0 4.8 %all_gather.11 = f32[128,128]{0,1:T(8,128)S(1)} all-gather(f32[128,64]{0,1:T(8,128)S(1)} %broadcast_multiply_fusion), channel_id=1, replica_groups=mesh['groups'=2,'feat'=4,'pts'=2,'sub'=2] {'pts'}, dimensions={1}, use_global_device_ids=true | all-gather | bytes 98304 | tf_op jit(solution)/shard_map/all_gather | solution.py:23
  395.8 0.1 copy.7
  395.9 11.7 %cholesky.17 = f32[128,128]{1,0:T(8,128)S(1)} custom-call(f32[128,128]{1,0:T(8,128)S(1)} %fusion.4), custom_call_target="Cholesky" | custom-call | tf_op jit(solution)/shard_map/jit(cholesky)/cholesky | solution.py:24
  407.7 0.6 compare_reduce_fusion
  408.3 0.7 select_bitcast_fusion
  409.0 9.8 %custom-call.7 = f32[1,128,128]{1,2,0:T(8,128)S(1)} custom-call(f32[1,128,128]{2,1,0:T(8,128)S(1)} %get-tuple-element.3), custom_call_target="InvertDiagBlocksLowerTriangular" | custom-call | tf_op jit(solution)/shard_map/jit(_solve_triangular)/triangular_solve | solution.py:26
  418.8 0.2 fusion.2
  419.0 0.6 constant_dynamic-slice_fusion
  419.7 5.9 %fusion.5 = f32[8192,64]{0,1:T(8,128)} fusion(f32[8192,128]{0,1:T(8,128)} %all-gather.5.cloned.1.call-done, f32[128,128]{1,0:T(8,128)S(1)} %fusion.2, s32[]{:T(128)S(6)} %select_n.9), kind=kOutput, calls=%fused_computation.14 | convolution fusion | flops 805306368 | bytes 6324228 | tf_op jit(solution)/shard_map/fq,pq->fp/dot_general | solution.py:30
  425.6 0.0 copy-done.1
  425.6 0.7 copy.9
  (3 shorter events, 0.1 us)
Async XLA Ops:
  7.2 0.8 copy-start
  7.2 0.8 copy-start.2
  7.2 204.0 %all-gather.3.cloned.1.call-start = ((), (), s32[]{:S(2)}) async-start(), calls=%async_computation | async-start | bytes 25165824 | tf_op jit(solution)/shard_map/all_gather | solution.py:14
  7.9 271.5 %all-reduce.2.cloned.1.call-start = ((), (), s32[]{:S(2)}) async-start(), calls=%async_computation.1 | async-start | bytes 524288 | tf_op jit(solution)/shard_map/psum | solution.py:16
  224.3 130.7 %all-gather.5.cloned.1.call-start = ((), (), s32[]{:S(2)}) async-start(), calls=%async_computation.2 | async-start | bytes 6291456 | tf_op jit(solution)/shard_map/all_gather | solution.py:19
  362.3 63.3 %copy-start.1 = (f32[1024,64]{0,1:T(8,128)S(1)}, f32[1024,64]{0,1:T(8,128)}, u32[]{:S(2)}) copy-start(f32[1024,64]{0,1:T(8,128)} %all-reduce.2.cloned.1.call-done) | copy-start | bytes 786436
Sparse Core Ops, SparseCore 0:
  9.6 201.5 all-gather.2
  224.4 54.9 all-reduce.1
  299.3 55.7 all-gather.4
where the time goes:
time: 433 us
  waiting for transfers between devices  306 us (71%)
  matrix products  55 us (13%)
  blocking collectives  33.5 us (8%)
  other arithmetic  22.9 us (5%)
  between operations  13.8 us (3%)
    all_gather x1, waiting for transfers between devices, on_device(): lax.all_gather(basis, 'pts', axis=1, tiled=True).astype(jnp.float32)  194 us
    all_gather x1, waiting for transfers between devices, on_device(): spread = lax.all_gather(residual, 'pts', axis=1, tiled=True)  55.9 us
    psum x1, waiting for transfers between devices, on_device(): coefs = lax.psum(partial_value, ('feat', 'sub'))  54.8 us
    psum x1, blocking collectives, on_device(): block = lax.psum(block, ('feat', 'sub')) / FEATS  28.7 us
    dot_general x1, matrix products, on_device(): fitted = jnp.dot(whole_basis, coefs, precision=highest)  19.7 us
    dot_general x1, matrix products, on_device(): jnp.einsum('fk,fp->kp', whole_basis, features, precision=highest)  13.1 us
    another operation x3, other arithmetic, on_device(): factor = jnp.linalg.cholesky(gram)  12.4 us
    another operation x2, other arithmetic, on_device(): inverse = jax.scipy.linalg.solve_triangular(factor, eye_mat, lower=True)  10.5 us
  transfers between devices with their start and end apart: 3, of which 3 were waited for; matrix products, arithmetic and copies ran while one was open for 2% of the time, Pallas kernels for 0%

commit v1 on v0

v1 whole, which is shorter than its diff:
```python
import functools

import jax
import jax.numpy as jnp
from jax import lax
from jax.experimental import pallas as pl
from jax.experimental.pallas import tpu as pltpu
from jax.sharding import PartitionSpec as P

BF16, F32, WIRE = jnp.bfloat16, jnp.float32, jnp.float16

COS = (
    0.9999999889369959,
    -0.4999998901135819,
    0.041666488148010265,
    -0.0013887798934755957,
    2.4769791619676175e-05,
    -2.7078195310289617e-07,
    1.7242244242579268e-09,
)
TURN_HEAD = 6.28125
TURN_REST = 0.0019353071795864769


def cosine(x):
    turns = jnp.round(x * 0.15915494309189535)
    x = (x - turns * TURN_HEAD) - turns * TURN_REST
    t = x * x
    y = COS[-1]
    for c in COS[-2::-1]:
        y = y * t + c
    return y


def split(x):
    high = x.astype(BF16)
    return high, (x - high.astype(F32)).astype(BF16)


def dot_nt(a, b):
    return lax.dot_general(a, b, (((1,), (1,)), ((), ())), preferred_element_type=F32)


def estimate(flops, moved):
    return pl.CostEstimate(flops=int(flops), bytes_accessed=int(moved), transcendentals=0)


def coef_kernel(place, points, freqs, phases, basis, feats, keep, send, total):
    step = pl.program_id(0)
    count = points.shape[0]
    half = keep.shape[0]
    x = jnp.dot(points[...], freqs[...], preferred_element_type=F32) + phases[...]
    value = cosine(x)
    feats[...] = value
    both = jnp.concatenate(split(value), axis=0)
    part = jnp.dot(both, basis[...], preferred_element_type=F32)
    part = part[:count] + part[count:]

    @pl.when(step == 0)
    def _():
        total[...] = part

    @pl.when(step > 0)
    def _():
        total[...] += part

    @pl.when(step == pl.num_programs(0) - 1)
    def _():
        sub = place[1]
        keep[...] = total[pl.ds(pl.multiple_of(sub * half, half), half), :]
        send[...] = total[pl.ds(pl.multiple_of((1 - sub) * half, half), half), :]


def partial_coefs(place, points, freqs, phases, basis, block=1024):
    count, dims = points.shape
    width, rank = basis.shape
    half = count // 2
    return pl.pallas_call(
        coef_kernel,
        grid_spec=pltpu.PrefetchScalarGridSpec(
            num_scalar_prefetch=1,
            grid=(width // block,),
            in_specs=[
                pl.BlockSpec((count, dims), lambda i, p: (0, 0)),
                pl.BlockSpec((dims, block), lambda i, p: (0, i)),
                pl.BlockSpec((1, block), lambda i, p: (0, i)),
                pl.BlockSpec((block, rank), lambda i, p: (i, 0)),
            ],
            out_specs=[
                pl.BlockSpec((count, block), lambda i, p: (0, i)),
                pl.BlockSpec((half, rank), lambda i, p: (0, 0)),
                pl.BlockSpec((half, rank), lambda i, p: (0, 0)),
            ],
            scratch_shapes=[pltpu.VMEM((count, rank), F32)],
        ),
        out_shape=[
            jax.ShapeDtypeStruct((count, width), F32),
            jax.ShapeDtypeStruct((half, rank), F32),
            jax.ShapeDtypeStruct((half, rank), F32),
        ],
        cost_estimate=estimate(
            2 * count * width * (dims + 2 * rank), width * (2 * dims + 2 * rank + 4 * count)
        ),
        name="coefs",
    )(place, points, freqs, phases, basis)


def fit_kernel(flip, place, own_a, got_a, own_b, got_b, feats_a, feats_b, basis, left, fit, coef_a, coef_b, parts):
    step = pl.program_id(0)
    half, rank = own_a.shape
    count = 4 * half

    @pl.when(step == 0)
    def _():
        sub = place[1]
        for base, own, got, coef in ((0, own_a, got_a, coef_a), (2 * half, own_b, got_b, coef_b)):
            mine = pl.ds(pl.multiple_of(sub * half, half), half)
            other = pl.ds(pl.multiple_of((1 - sub) * half, half), half)
            coef[mine, :] = own[...]
            coef[other, :] = got[...]
            high, low = split(coef[...])
            parts[base : base + 2 * half, :] = high
            parts[count + base : count + base + 2 * half, :] = low

    value = dot_nt(parts[...], basis[...])
    value = value[:count] + value[count:]
    fit[...] = value
    left[: 2 * half, :] = feats_a[...] - value[: 2 * half]
    left[2 * half :, :] = feats_b[...] - value[2 * half :]


def fitted(place, coefs, feats_a, feats_b, basis, flip, block=1024):
    half, rank = coefs[0].shape
    count = 4 * half
    width = basis.shape[0]
    blocks = width // 2 // block

    def at(i, p):
        side = 1 - p[0] if flip else p[0]
        return side * blocks + i

    small = pl.BlockSpec((half, rank), lambda i, p: (0, 0))
    return pl.pallas_call(
        functools.partial(fit_kernel, flip),
        grid_spec=pltpu.PrefetchScalarGridSpec(
            num_scalar_prefetch=1,
            grid=(blocks,),
            in_specs=[
                small,
                small,
                small,
                small,
                pl.BlockSpec((2 * half, block), lambda i, p: (0, at(i, p))),
                pl.BlockSpec((2 * half, block), lambda i, p: (0, at(i, p))),
                pl.BlockSpec((block, rank), lambda i, p: (at(i, p), 0)),
            ],
            out_specs=[
                pl.BlockSpec((count, block), lambda i, p: (0, i)),
                pl.BlockSpec((count, block), lambda i, p: (0, i)),
                pl.BlockSpec((2 * half, rank), lambda i, p: (0, 0)),
                pl.BlockSpec((2 * half, rank), lambda i, p: (0, 0)),
            ],
            scratch_shapes=[pltpu.VMEM((2 * count, rank), BF16)],
        ),
        out_shape=[
            jax.ShapeDtypeStruct((count, width // 2), F32),
            jax.ShapeDtypeStruct((count, width // 2), F32),
            jax.ShapeDtypeStruct((2 * half, rank), F32),
            jax.ShapeDtypeStruct((2 * half, rank), F32),
        ],
        cost_estimate=estimate(2 * count * width * rank, width * (rank + 6 * count)),
        name="fit",
    )(place, *coefs, feats_a, feats_b, basis)


def gram_kernel(place, resid, keep, send, total):
    step = pl.program_id(0)
    count = resid.shape[0]
    half = count // 2
    both = jnp.concatenate(split(resid[...]), axis=0)
    part = dot_nt(both, both)
    part = (part[:count, :count] + part[count:, count:]) + (part[:count, count:] + part[count:, :count])

    @pl.when(step == 0)
    def _():
        total[...] = part

    @pl.when(step > 0)
    def _():
        total[...] += part

    @pl.when(step == pl.num_programs(0) - 1)
    def _():
        sub = place[1]
        own = place[0] == 0

        def rows(start):
            value = total[pl.ds(pl.multiple_of(start * half, half), half), :]
            swapped = jnp.concatenate([value[:, half:], value[:, :half]], axis=1)
            return jnp.where(own, value, swapped)

        mine = jnp.where(own, sub, 1 - sub)
        keep[...] = rows(mine)
        send[...] = rows(1 - mine)


def partial_gram(place, resid, block=1024):
    count, width = resid.shape
    half = count // 2
    return pl.pallas_call(
        gram_kernel,
        grid_spec=pltpu.PrefetchScalarGridSpec(
            num_scalar_prefetch=1,
            grid=(width // block,),
            in_specs=[pl.BlockSpec((count, block), lambda i, p: (0, i))],
            out_specs=[
                pl.BlockSpec((half, count), lambda i, p: (0, 0)),
                pl.BlockSpec((half, count), lambda i, p: (0, 0)),
            ],
            scratch_shapes=[pltpu.VMEM((count, count), F32)],
        ),
        out_shape=[jax.ShapeDtypeStruct((half, count), F32)] * 2,
        cost_estimate=estimate(8 * count * count * width, 4 * width * count),
        name="gram",
    )(place, resid)


def basis_kernel(place, weights, mine, theirs, out):
    first = pl.program_id(0) < pl.num_programs(0) // 2

    @pl.when(first)
    def _():
        out[...] = finish(weights[...], mine[...])

    @pl.when(jnp.logical_not(first))
    def _():
        out[...] = finish(weights[...], theirs[...])


def finish(weights, resid):
    high, low = split(weights)
    lhs = jnp.concatenate(
        [jnp.concatenate([high, high], axis=1), jnp.concatenate([low, low], axis=1)], axis=0
    )
    value = jnp.dot(lhs, jnp.concatenate(split(resid), axis=0), preferred_element_type=F32)
    rows = weights.shape[0]
    return value[:rows] + value[rows:]


def new_rows(place, weights, mine, theirs, block=1024):
    rows, count = weights.shape
    half_width = mine.shape[1]
    blocks = half_width // block
    return pl.pallas_call(
        basis_kernel,
        grid_spec=pltpu.PrefetchScalarGridSpec(
            num_scalar_prefetch=1,
            grid=(2 * blocks,),
            in_specs=[
                pl.BlockSpec((rows, count), lambda i, p: (0, 0)),
                pl.BlockSpec((count, block), lambda i, p: (0, jnp.minimum(i, blocks - 1))),
                pl.BlockSpec((count, block), lambda i, p: (0, jnp.maximum(i - blocks, 0))),
            ],
            out_specs=pl.BlockSpec(
                (rows, block),
                lambda i, p: (0, jnp.where(i < blocks, p[0], 1 - p[0]) * blocks + lax.rem(i, blocks)),
            ),
        ),
        out_shape=jax.ShapeDtypeStruct((rows, 2 * half_width), F32),
        cost_estimate=estimate(8 * rows * count * 2 * half_width, 4 * half_width * (2 * count + 2 * rows)),
        name="new_basis",
    )(place, weights, mine, theirs)


def swap(x, axis):
    return lax.ppermute(x, axis, [(0, 1), (1, 0)])


def sum_over(x, axis, size):
    terms = [x] + [lax.ppermute(x, axis, [(i, i ^ m) for i in range(size)]) for m in range(1, size)]
    while len(terms) > 1:
        terms = [a + b for a, b in zip(terms[::2], terms[1::2])]
    return terms[0]


def paired(feat, feats_total, points, freqs, phases, basis):
    count = points.shape[0]
    place = jnp.stack([lax.axis_index("pts"), lax.axis_index("sub")]).astype(jnp.int32)
    phases = phases[None, :]
    others = swap(points, "pts")
    feats, coefs = [], []
    for chunk in (points, others):
        values, keep, send = partial_coefs(place, chunk, freqs, phases, basis)
        own = sum_over(keep + swap(send, "sub"), "feat", feat)
        feats.append(values)
        coefs += [own, swap(own, "sub")]

    left_far, fit_far, coef_a, coef_b = fitted(place, coefs, *feats, basis, 1)
    left_near, fit_near, _, _ = fitted(place, coefs, *feats, basis, 0)

    def received(left, fit):
        got = swap(fit.astype(WIRE), "pts").astype(F32)
        return left - jnp.concatenate([got[count:], got[:count]], axis=0)

    near = received(left_near, fit_far)
    keep, send = partial_gram(place, near)
    gram = keep + swap(send, "sub")
    gram = gram + swap(gram, "pts")
    gram = sum_over(gram, "feat", feat)
    far_gram = swap(gram, "sub")
    first = lax.axis_index("sub") == 0
    gram = jnp.where(
        first, jnp.concatenate([gram, far_gram], 0), jnp.concatenate([far_gram, gram], 0)
    ) / feats_total
    factor = jnp.linalg.cholesky(gram)
    inverse = jax.scipy.linalg.solve_triangular(factor, jnp.eye(2 * count, dtype=F32), lower=True)

    start = lax.axis_index("pts") * count
    factor_rows = lax.dynamic_slice_in_dim(factor, start, count, 0)
    weights = lax.dynamic_slice_in_dim(inverse, start, count, 0)
    swapped = jnp.concatenate([weights[:, count:], weights[:, :count]], axis=1)
    weights = jnp.where(lax.axis_index("pts") == 0, weights, swapped)
    far = received(left_far, fit_near)
    new_basis = new_rows(place, weights, near, far)

    got = swap(coef_b, "pts")
    coefs = jnp.where(
        lax.axis_index("pts") == 0,
        jnp.concatenate([coef_a, got], axis=1),
        jnp.concatenate([got, coef_a], axis=1),
    )
    return coefs.T, new_basis.T, factor_rows


def general(feats_total, points, freqs, phases, basis):
    highest = lax.Precision.HIGHEST
    phase_in = jnp.einsum("pd,df->fp", points, freqs, preferred_element_type=F32)
    features = jnp.cos(phase_in + phases[:, None])
    point_cols = features.shape[1]
    whole_basis = lax.all_gather(basis, "pts", axis=1, tiled=True).astype(F32)
    partial_value = jnp.einsum("fk,fp->kp", whole_basis, features, precision=highest)
    coefs = lax.psum(partial_value, ("feat", "sub"))
    residual = features - jnp.dot(whole_basis, coefs, precision=highest)
    spread = lax.all_gather(residual, "pts", axis=1, tiled=True)
    block = jnp.einsum("fq,fp->qp", spread, residual, precision=highest)
    total_pts = block.shape[0]
    block = lax.psum(block, ("feat", "sub")) / feats_total
    gram = lax.all_gather(block, "pts", axis=1, tiled=True)
    factor = jnp.linalg.cholesky(gram)
    inverse = jax.scipy.linalg.solve_triangular(factor, jnp.eye(total_pts, dtype=F32), lower=True)
    offset = lax.axis_index("pts") * point_cols
    factor_rows = lax.dynamic_slice_in_dim(factor, offset, point_cols, 0)
    inv_rows = lax.dynamic_slice_in_dim(inverse, offset, point_cols, 0)
    new_basis = jnp.einsum("fq,pq->fp", spread, inv_rows, precision=highest)
    return coefs, new_basis, factor_rows


def solution(mesh):
    sizes = dict(mesh.shape)
    feat, pts, sub = sizes["feat"], sizes["pts"], sizes["sub"]

    def on_device(points, freqs, phases, basis):
        feats_total = phases.shape[0] * feat * sub
        if pts == 2 and sub == 2 and feat in (1, 2, 4, 8):
            return paired(feat, feats_total, points, freqs, phases, basis)
        return general(feats_total, points, freqs, phases, basis)

    return jax.shard_map(
        on_device,
        mesh=mesh,
        in_specs=(
            P(("groups", "pts"), None),
            P(None, ("feat", "sub")),
            P(("feat", "sub")),
            P(("groups", "feat", "sub"), "pts"),
        ),
        out_specs=(
            P("groups", "pts"),
            P(("groups", "feat", "sub"), "pts"),
            P(("groups", "pts"), None),
        ),
        check_vma=False,
    )
```

time: 433 us -> 149 us (0.34)
  waiting for transfers between devices: 306 us -> 39.8 us
  matrix products: 55 us -> 0.25 us
  Pallas kernels: 0 us -> 47 us
  blocking collectives: 33.5 us -> 0 us
  starting transfers between devices: 0.3 us -> 20.5 us
  between operations: 13.8 us -> 0.93 us
  other arithmetic: 22.9 us -> 34 us
    all_gather x2 -> x0, waiting for transfers between devices: 250 us -> none  [the longest x1 194 us: on_device(): lax.all_gather(basis, 'pts', axis=1, tiled=True).astype(jnp.float32)]
    psum x1 -> x0, waiting for transfers between devices: 54.8 us -> none  [on_device(): coefs = lax.psum(partial_value, ('feat', 'sub'))]
    dot_general x5 -> x0, matrix products: 54.8 us -> none  [the longest x1 19.7 us: on_device(): fitted = jnp.dot(whole_basis, coefs, precision=highest)]
    pallas_call x0 -> x6, Pallas kernels: none -> 47 us  [the longest x2 21 us: partial_coefs(): pl.pallas_call(coef_kernel, grid_spec=pltpu.PrefetchScalarGridSpec(num_sc...]
    ppermute x0 -> x20, waiting for transfers between devices: none -> 39.8 us  [the longest x11 29.6 us: swap(): return lax.ppermute(x, axis, [(0, 1), (1, 0)])]
    psum x1 -> x0, blocking collectives: 28.7 us -> none  [on_device(): block = lax.psum(block, ('feat', 'sub')) / FEATS]
    ppermute x0 -> x20, starting transfers between devices: none -> 20.5 us  [the longest x9 13.4 us: sum_over(): lax.ppermute(x, axis, [(i, i ^ m) for i in range(size)])]
    convert_element_type x0 -> x4, other arithmetic: none -> 4.97 us  [received(): got = swap(fit.astype(WIRE), 'pts').astype(F32)]
  transfers between devices with their start and end apart: 3 -> 20, of which waited for: 3 -> 10; matrix products, arithmetic and copies ran while one was open for 2% -> 7% of each run, Pallas kernels for 0% -> 22%
where the time goes in v1:
time: 149 us; the launch traced here: 148 us
  Pallas kernels  47 us (32%)
  waiting for transfers between devices  39.8 us (27%)
  other arithmetic  34 us (23%)
  starting transfers between devices  20.5 us (14%)
  local copies, waits for them, and re-layouts  5.45 us (4%)
    ppermute x11, waiting for transfers between devices, swap(): return lax.ppermute(x, axis, [(0, 1), (1, 0)])  29.6 us
    pallas_call x2, Pallas kernels, partial_coefs(): pl.pallas_call(coef_kernel, grid_spec=pltpu.PrefetchScalarGridSpec(num_sc...  21 us
    pallas_call x2, Pallas kernels, fitted(): pl.pallas_call(functools.partial(fit_kernel, flip), grid_spec=pltpu.Prefe...  13.6 us
    ppermute x9, starting transfers between devices, sum_over(): lax.ppermute(x, axis, [(i, i ^ m) for i in range(size)])  13.4 us
    another operation x3, other arithmetic, paired(): factor = jnp.linalg.cholesky(gram)  12.4 us
    another operation x2, other arithmetic, paired(): jax.scipy.linalg.solve_triangular(factor, jnp.eye(2 * count, dtype=F32),...  10.5 us
    ppermute x9, waiting for transfers between devices, sum_over(): lax.ppermute(x, axis, [(i, i ^ m) for i in range(size)])  10.2 us
    pallas_call x1, Pallas kernels, new_rows(): pl.pallas_call(basis_kernel, grid_spec=pltpu.PrefetchScalarGridSpec(num_s...  7.67 us
  transfers between devices with their start and end apart: 20, of which 10 were waited for; matrix products, arithmetic and copies ran while one was open for 7% of the time, Pallas kernels for 22%

profile of v1, /device:TPU:0, one launch (start us, length us, event | category | flops | bytes accessed | tf_op | source)
XLA Modules:
  0.0 147.9 jit_solution(7841880114488011863)
XLA Ops:
  0.6 3.0 %collective-permute-start.5 = (bf16[64,256]{1,0:T(8,128)(2,1)}, bf16[64,256]{1,0:T(8,128)(2,1)S(1)}, u32[]{:S(2)}, u32[]{:S(2)}) collective-permute-start(bf16[64,256]{1,0:T(8,128)(2,1)} %points.1), channel_id=1, source_target_pairs={{0,2},{2,0},{1,3},{3,1},{4,6},{6,4},{5,7},{7,5},{8,10},{10,8},{9,1... | collective-permute-start | bytes 98312 | tf_op jit(solution)/shard_map/ppermute | solution.py:276
  3.6 0.6 pad_add_fusion.place
  4.2 10.5 %coefs.2 = (f32[64,8192]{1,0:T(8,128)}, f32[32,512]{1,0:T(8,128)}, f32[32,512]{1,0:T(8,128)}) custom-call(s32[2]{0:T(128)} %pad_add_fusion.place, bf16[64,256]{1,0:T(8,128)(2,1)} %points.1, bf16[256,8192]{1,0:T(8,128)(2,1)} %freqs.3, f32[1,8192]{1,0:T(1,128)} %bitcast.16, bf16[8192,512]{1,0:T(8,128)(2,1)} %basis.7), custom_call_target="tpu_custom_call" | custom-call | flops 1342177280 | bytes 14680064 | tf_op jit(solution)/shard_map/coefs/pallas_call | solution.py:78
  14.8 0.6 copy-done.8
  15.4 10.5 %coefs.3 = (f32[64,8192]{1,0:T(8,128)}, f32[32,512]{1,0:T(8,128)}, f32[32,512]{1,0:T(8,128)}) custom-call(s32[2]{0:T(128)} %pad_add_fusion.place, bf16[64,256]{1,0:T(8,128)(2,1)} %copy-done.8, bf16[256,8192]{1,0:T(8,128)(2,1)} %freqs.3, f32[1,8192]{1,0:T(1,128)} %bitcast.17, bf16[8192,512]{1,0:T(8,128)(2,1)} %basis.7), custom_call_target="tpu_custom_call" | custom-call | flops 1342177280 | bytes 14680064 | tf_op jit(solution)/shard_map/coefs/pallas_call | solution.py:78
  25.9 0.5 collective-permute-start.6
  26.4 1.6 %collective-permute-start.1 = (f32[32,512]{1,0:T(8,128)S(1)}, f32[32,512]{1,0:T(8,128)S(1)}, u32[]{:S(2)}, u32[]{:S(2)}) collective-permute-start(f32[32,512]{1,0:T(8,128)S(1)} %add.55), channel_id=1, source_target_pairs={{0,4},{4,0},{8,12},{12,8},{1,5},{5,1},{9,13},{13,9},{2,6},{6,2},{1... | collective-permute-start | bytes 196616 | tf_op jit(solution)/shard_map/ppermute | solution.py:280
  28.1 2.6 %collective-permute-start.2 = (f32[32,512]{1,0:T(8,128)S(1)}, f32[32,512]{1,0:T(8,128)S(1)}, u32[]{:S(2)}, u32[]{:S(2)}) collective-permute-start(f32[32,512]{1,0:T(8,128)S(1)} %add.55), channel_id=1, source_target_pairs={{0,8},{4,12},{8,0},{12,4},{1,9},{5,13},{9,1},{13,5},{2,10},{6,14},... | collective-permute-start | bytes 196616 | tf_op jit(solution)/shard_map/ppermute | solution.py:280
  30.9 0.9 add.59
  31.7 0.7 collective-permute-start.7
  32.5 3.5 %collective-permute-start.8 = (f32[32,512]{1,0:T(8,128)S(1)}, f32[32,512]{1,0:T(8,128)S(1)}, u32[]{:S(2)}, u32[]{:S(2)}) collective-permute-start(f32[32,512]{1,0:T(8,128)S(1)} %add.59), channel_id=1, source_target_pairs={{0,8},{4,12},{8,0},{12,4},{1,9},{5,13},{9,1},{13,5},{2,10},{6,14},... | collective-permute-start | bytes 196616 | tf_op jit(solution)/shard_map/ppermute | solution.py:280
  36.2 1.2 collective-permute-done.3
  37.5 3.5 %collective-permute-done.8 = f32[32,512]{1,0:T(8,128)S(1)} collective-permute-done((f32[32,512]{1,0:T(8,128)S(1)}, f32[32,512]{1,0:T(8,128)S(1)}, u32[]{:S(2)}, u32[]{:S(2)}) %collective-permute-start.8) | collective-permute-done | bytes 65568 | tf_op jit(solution)/shard_map/ppermute | solution.py:280
  41.0 1.1 collective-permute-done.9
  42.3 1.2 collective-permute-done.10.got_b
  43.5 0.6 copy-done.5
  44.1 6.8 %fit.2 = (f32[128,4096]{1,0:T(8,128)}, f32[128,4096]{1,0:T(8,128)}, f32[64,512]{1,0:T(8,128)}, f32[64,512]{1,0:T(8,128)}) custom-call(s32[2]{0:T(128)} %pad_add_fusion.place, f32[32,512]{1,0:T(8,128)} %copy-done.2, f32[32,512]{1,0:T(8,128)} %copy-done.4, f32[32,512]{1,0:T(8,128)} %copy-done.3, f32[32,512]{1,0:T(8,128)} %copy-done.5, ...), custom_call_target="tpu_custom_call" | custom-call | flops 1073741824 | bytes 10485760 | tf_op jit(solution)/shard_map/fit/pallas_call | solution.py:143
  50.9 1.7 %convert_element_type.13 = f16[128,4096]{1,0:T(8,128)(2,1)S(1)} convert(f32[128,4096]{1,0:T(8,128)} %get-tuple-element.26) | non-fusion elementwise | flops 524288 | bytes 3145728 | tf_op jit(solution)/shard_map/convert_element_type | solution.py:302
  52.6 0.6 collective-permute-start.12
  53.2 6.8 %fit.3 = (f32[128,4096]{1,0:T(8,128)}, f32[128,4096]{1,0:T(8,128)}, f32[64,512]{1,0:T(8,128)}, f32[64,512]{1,0:T(8,128)}) custom-call(s32[2]{0:T(128)} %pad_add_fusion.place, f32[32,512]{1,0:T(8,128)} %copy-done.2, f32[32,512]{1,0:T(8,128)} %copy-done.4, f32[32,512]{1,0:T(8,128)} %copy-done.3, f32[32,512]{1,0:T(8,128)} %copy-done.5, ...), custom_call_target="tpu_custom_call" | custom-call | flops 1073741824 | bytes 10485760 | tf_op jit(solution)/shard_map/fit/pallas_call | solution.py:143
  60.0 1.7 %convert_element_type.15 = f16[128,4096]{1,0:T(8,128)(2,1)S(1)} convert(f32[128,4096]{1,0:T(8,128)} %get-tuple-element.30) | non-fusion elementwise | flops 524288 | bytes 3145728 | tf_op jit(solution)/shard_map/convert_element_type | solution.py:302
  61.8 1.6 %collective-permute-start.19 = (f16[128,4096]{1,0:T(8,128)(2,1)S(1)}, f16[128,4096]{1,0:T(8,128)(2,1)S(1)}, u32[]{:S(2)}, u32[]{:S(2)}) collective-permute-start(f16[128,4096]{1,0:T(8,128)(2,1)S(1)} %convert_element_type.15), channel_id=1, source_target_pairs={{0,2},{2,0},{1,3},{3,1},{4,6},{6,4},{5,7},{7,5},{8,10},{10,8},{9,1... | collective-permute-start | bytes 3145736 | tf_op jit(solution)/shard_map/ppermute | solution.py:276
  63.4 0.5 collective-permute-start.11
  63.9 14.9 %collective-permute-done.12 = f16[128,4096]{1,0:T(8,128)(2,1)} collective-permute-done((f16[128,4096]{1,0:T(8,128)(2,1)S(1)}, f16[128,4096]{1,0:T(8,128)(2,1)}, u32[]{:S(2)}, u32[]{:S(2)}) %collective-permute-start.12) | collective-permute-done | bytes 1048608 | tf_op jit(solution)/shard_map/ppermute | solution.py:276
  78.8 1.4 convert_element_type.14
  80.3 1.4 copy-done.1
  81.8 1.5 %maximum_subtract_fusion.resid.mine = f32[128,4096]{1,0:T(8,128)} fusion(f32[128,4096]{1,0:T(8,128)S(1)} %copy-done.1, f32[64,4096]{1,0:T(8,128)S(1)} %get-tuple-element.36, f32[64,4096]{1,0:T(8,128)S(1)} %get-tuple-element.35), kind=kLoop, calls=%fused_computation | loop fusion | flops 1048576 | bytes 6291456 | tf_op jit(solution)/shard_map/sub | solution.py:303
  83.3 4.7 %gram.1 = (f32[64,128]{1,0:T(8,128)}, f32[64,128]{1,0:T(8,128)}) custom-call(s32[2]{0:T(128)} %pad_add_fusion.place, f32[128,4096]{1,0:T(8,128)} %maximum_subtract_fusion.resid.mine), custom_call_target="tpu_custom_call" | custom-call | flops 536870912 | bytes 2097152 | tf_op jit(solution)/shard_map/gram/pallas_call | solution.py:210
  88.0 0.8 copy.7
  89.0 0.8 copy.8
  89.8 0.4 collective-permute-done.13
  90.2 0.6 collective-permute-start.14
  90.8 13.1 %collective-permute-done.11 = f32[64,512]{1,0:T(8,128)S(1)} collective-permute-done((f32[64,512]{1,0:T(8,128)S(1)}, f32[64,512]{1,0:T(8,128)S(1)}, u32[]{:S(2)}, u32[]{:S(2)}) %collective-permute-start.11) | collective-permute-done | bytes 131104 | tf_op jit(solution)/shard_map/ppermute | solution.py:276
  103.9 0.7 fusion
  104.8 1.1 collective-permute-start.15
  105.9 1.7 %collective-permute-start.16 = (f32[64,128]{0,1:T(8,128)S(1)}, f32[64,128]{0,1:T(8,128)S(1)}, u32[]{:S(2)}, u32[]{:S(2)}) collective-permute-start(f32[64,128]{0,1:T(8,128)S(1)} %add.64), channel_id=1, source_target_pairs={{0,8},{4,12},{8,0},{12,4},{1,9},{5,13},{9,1},{13,5},{2,10},{6,14},... | collective-permute-start | bytes 98312 | tf_op jit(solution)/shard_map/ppermute | solution.py:280
  107.6 1.6 %collective-permute-start.17 = (f32[64,128]{0,1:T(8,128)S(1)}, f32[64,128]{0,1:T(8,128)S(1)}, u32[]{:S(2)}, u32[]{:S(2)}) collective-permute-start(f32[64,128]{0,1:T(8,128)S(1)} %add.64), channel_id=1, source_target_pairs={{0,12},{4,8},{8,4},{12,0},{1,13},{5,9},{9,5},{13,1},{2,14},{6,10},... | collective-permute-start | bytes 98312 | tf_op jit(solution)/shard_map/ppermute | solution.py:280
  109.5 3.0 %collective-permute-done.16 = f32[64,128]{0,1:T(8,128)S(1)} collective-permute-done((f32[64,128]{0,1:T(8,128)S(1)}, f32[64,128]{0,1:T(8,128)S(1)}, u32[]{:S(2)}, u32[]{:S(2)}) %collective-permute-start.16) | collective-permute-done | bytes 32800 | tf_op jit(solution)/shard_map/ppermute | solution.py:280
  112.5 1.3 collective-permute-done.17
  113.9 1.6 %maximum_subtract_fusion.1.theirs = f32[128,4096]{1,0:T(8,128)} fusion(f32[128,4096]{1,0:T(8,128)S(1)} %copy-done, f32[64,4096]{1,0:T(8,128)S(1)} %get-tuple-element.34, f32[64,4096]{1,0:T(8,128)S(1)} %get-tuple-element.33), kind=kLoop, calls=%fused_computation.1 | loop fusion | flops 1048576 | bytes 6291456 | tf_op jit(solution)/shard_map/sub | solution.py:303
  115.7 11.7 %cholesky.17 = f32[128,128]{1,0:T(8,128)S(1)} custom-call(f32[128,128]{1,0:T(8,128)S(1)} %fusion.4), custom_call_target="Cholesky" | custom-call | tf_op jit(solution)/shard_map/jit(cholesky)/cholesky | solution.py:315
  127.5 0.6 compare_reduce_fusion
  128.1 0.7 select_bitcast_fusion
  128.8 9.8 %custom-call.7 = f32[1,128,128]{1,2,0:T(8,128)S(1)} custom-call(f32[1,128,128]{2,1,0:T(8,128)S(1)} %get-tuple-element.31), custom_call_target="InvertDiagBlocksLowerTriangular" | custom-call | tf_op jit(solution)/shard_map/jit(_solve_triangular)/triangular_solve | solution.py:316
  138.6 0.2 fusion.2
  138.8 0.6 constant_dynamic-slice_fusion.1
  139.6 0.7 maximum_select_fusion.2.weights
  140.2 7.7 %new_basis.1 = f32[64,8192]{1,0:T(8,128)} custom-call(s32[2]{0:T(128)} %pad_add_fusion.place, f32[64,128]{1,0:T(8,128)} %maximum_select_fusion.2.weights, f32[128,4096]{1,0:T(8,128)} %maximum_subtract_fusion.resid.mine, f32[128,4096]{1,0:T(8,128)} %maximum_subtract_fusion.1.theirs), custom_call_target="tpu_custom_call" | custom-call | flops 536870912 | bytes 6291456 | tf_op jit(solution)/shard_map/new_basis/pallas_call | solution.py:254
  (49 shorter events, 1.8 us)
Async XLA Ops:
  0.6 14.1 %collective-permute-start.5 = (bf16[64,256]{1,0:T(8,128)(2,1)}, bf16[64,256]{1,0:T(8,128)(2,1)S(1)}, u32[]{:S(2)}, u32[]{:S(2)}) collective-permute-start(bf16[64,256]{1,0:T(8,128)(2,1)} %points.1), channel_id=1, source_target_pairs={{0,2},{2,0},{1,3},{3,1},{4,6},{6,4},{5,7},{7,5},{8,10},{10,8},{9,1... | collective-permute-start | bytes 98312 | tf_op jit(solution)/shard_map/ppermute | solution.py:276
  14.7 11.7 %copy-start.7 = (f32[32,512]{1,0:T(8,128)S(1)}, f32[32,512]{1,0:T(8,128)}, u32[]{:S(2)}) copy-start(f32[32,512]{1,0:T(8,128)} %get-tuple-element.17) | copy-start | bytes 196612
  14.7 11.7 %collective-permute-start = (f32[32,512]{1,0:T(8,128)}, f32[32,512]{1,0:T(8,128)S(1)}, u32[]{:S(2)}, u32[]{:S(2)}) collective-permute-start(f32[32,512]{1,0:T(8,128)} %get-tuple-element.18), channel_id=1, source_target_pairs={{0,1},{1,0},{2,3},{3,2},{4,5},{5,4},{6,7},{7,6},{8,9},{9,8},{10,11... | collective-permute-start | bytes 196616 | tf_op jit(solution)/shard_map/ppermute | solution.py:276
  14.8 0.6 copy-start.8
  25.9 5.0 %collective-permute-start.6 = (f32[32,512]{1,0:T(8,128)}, f32[32,512]{1,0:T(8,128)S(1)}, u32[]{:S(2)}, u32[]{:S(2)}) collective-permute-start(f32[32,512]{1,0:T(8,128)} %get-tuple-element.20), channel_id=1, source_target_pairs={{0,1},{1,0},{2,3},{3,2},{4,5},{5,4},{6,7},{7,6},{8,9},{9,8},{10,11... | collective-permute-start | bytes 196616 | tf_op jit(solution)/shard_map/ppermute | solution.py:276
  26.4 9.5 %collective-permute-start.1 = (f32[32,512]{1,0:T(8,128)S(1)}, f32[32,512]{1,0:T(8,128)S(1)}, u32[]{:S(2)}, u32[]{:S(2)}) collective-permute-start(f32[32,512]{1,0:T(8,128)S(1)} %add.55), channel_id=1, source_target_pairs={{0,4},{4,0},{8,12},{12,8},{1,5},{5,1},{9,13},{13,9},{2,6},{6,2},{1... | collective-permute-start | bytes 196616 | tf_op jit(solution)/shard_map/ppermute | solution.py:280
  28.1 8.1 %collective-permute-start.2 = (f32[32,512]{1,0:T(8,128)S(1)}, f32[32,512]{1,0:T(8,128)S(1)}, u32[]{:S(2)}, u32[]{:S(2)}) collective-permute-start(f32[32,512]{1,0:T(8,128)S(1)} %add.55), channel_id=1, source_target_pairs={{0,8},{4,12},{8,0},{12,4},{1,9},{5,13},{9,1},{13,5},{2,10},{6,14},... | collective-permute-start | bytes 196616 | tf_op jit(solution)/shard_map/ppermute | solution.py:280
  30.7 6.7 %collective-permute-start.3 = (f32[32,512]{1,0:T(8,128)S(1)}, f32[32,512]{1,0:T(8,128)S(1)}, u32[]{:S(2)}, u32[]{:S(2)}) collective-permute-start(f32[32,512]{1,0:T(8,128)S(1)} %add.55), channel_id=1, source_target_pairs={{0,12},{4,8},{8,4},{12,0},{1,13},{5,9},{9,5},{13,1},{2,14},{6,10},... | collective-permute-start | bytes 196616 | tf_op jit(solution)/shard_map/ppermute | solution.py:280
  31.7 5.7 %collective-permute-start.7 = (f32[32,512]{1,0:T(8,128)S(1)}, f32[32,512]{1,0:T(8,128)S(1)}, u32[]{:S(2)}, u32[]{:S(2)}) collective-permute-start(f32[32,512]{1,0:T(8,128)S(1)} %add.59), channel_id=1, source_target_pairs={{0,4},{4,0},{8,12},{12,8},{1,5},{5,1},{9,13},{13,9},{2,6},{6,2},{1... | collective-permute-start | bytes 196616 | tf_op jit(solution)/shard_map/ppermute | solution.py:280
  32.5 8.5 %collective-permute-start.8 = (f32[32,512]{1,0:T(8,128)S(1)}, f32[32,512]{1,0:T(8,128)S(1)}, u32[]{:S(2)}, u32[]{:S(2)}) collective-permute-start(f32[32,512]{1,0:T(8,128)S(1)} %add.59), channel_id=1, source_target_pairs={{0,8},{4,12},{8,0},{12,4},{1,9},{5,13},{9,1},{13,5},{2,10},{6,14},... | collective-permute-start | bytes 196616 | tf_op jit(solution)/shard_map/ppermute | solution.py:280
  36.0 6.2 %collective-permute-start.9 = (f32[32,512]{1,0:T(8,128)S(1)}, f32[32,512]{1,0:T(8,128)S(1)}, u32[]{:S(2)}, u32[]{:S(2)}) collective-permute-start(f32[32,512]{1,0:T(8,128)S(1)} %add.59), channel_id=1, source_target_pairs={{0,12},{4,8},{8,4},{12,0},{1,13},{5,9},{9,5},{13,1},{2,14},{6,10},... | collective-permute-start | bytes 196616 | tf_op jit(solution)/shard_map/ppermute | solution.py:280
  37.4 6.1 %copy-start.2 = (f32[32,512]{1,0:T(8,128)}, f32[32,512]{1,0:T(8,128)S(1)}, u32[]{:S(2)}) copy-start(f32[32,512]{1,0:T(8,128)S(1)} %add_add_fusion.2.own_a) | copy-start | bytes 196612
  37.4 4.9 %collective-permute-start.4 = (f32[32,512]{1,0:T(8,128)S(1)}, f32[32,512]{1,0:T(8,128)S(1)}, u32[]{:S(2)}, u32[]{:S(2)}) collective-permute-start(f32[32,512]{1,0:T(8,128)S(1)} %add_add_fusion.2.own_a), channel_id=1, source_target_pairs={{0,1},{1,0},{2,3},{3,2},{4,5},{5,4},{6,7},{7,6},{8,9},{9,8},{10,11... | collective-permute-start | bytes 196616 | tf_op jit(solution)/shard_map/ppermute | solution.py:276
  42.2 1.3 copy-start.3
  42.2 1.3 collective-permute-start.10
  42.3 1.2 copy-start.4
  43.5 0.6 copy-start.5
  52.6 26.2 %collective-permute-start.12 = (f16[128,4096]{1,0:T(8,128)(2,1)S(1)}, f16[128,4096]{1,0:T(8,128)(2,1)}, u32[]{:S(2)}, u32[]{:S(2)}) collective-permute-start(f16[128,4096]{1,0:T(8,128)(2,1)S(1)} %convert_element_type.13), channel_id=1, source_target_pairs={{0,2},{2,0},{1,3},{3,1},{4,6},{6,4},{5,7},{7,5},{8,10},{10,8},{9,1... | collective-permute-start | bytes 3145736 | tf_op jit(solution)/shard_map/ppermute | solution.py:276
  60.0 3.3 %copy-start.9 = (f32[64,512]{1,0:T(8,128)S(1)}, f32[64,512]{1,0:T(8,128)}, u32[]{:S(2)}) copy-start(f32[64,512]{1,0:T(8,128)} %get-tuple-element.24) | copy-start | bytes 393220
  61.8 42.8 %collective-permute-start.19 = (f16[128,4096]{1,0:T(8,128)(2,1)S(1)}, f16[128,4096]{1,0:T(8,128)(2,1)S(1)}, u32[]{:S(2)}, u32[]{:S(2)}) collective-permute-start(f16[128,4096]{1,0:T(8,128)(2,1)S(1)} %convert_element_type.15), channel_id=1, source_target_pairs={{0,2},{2,0},{1,3},{3,1},{4,6},{6,4},{5,7},{7,5},{8,10},{10,8},{9,1... | collective-permute-start | bytes 3145736 | tf_op jit(solution)/shard_map/ppermute | solution.py:276
  63.4 40.5 %collective-permute-start.11 = (f32[64,512]{1,0:T(8,128)S(1)}, f32[64,512]{1,0:T(8,128)S(1)}, u32[]{:S(2)}, u32[]{:S(2)}) collective-permute-start(f32[64,512]{1,0:T(8,128)S(1)} %copy-done.9), channel_id=1, source_target_pairs={{0,2},{2,0},{1,3},{3,1},{4,6},{6,4},{5,7},{7,5},{8,10},{10,8},{9,1... | collective-permute-start | bytes 393224 | tf_op jit(solution)/shard_map/ppermute | solution.py:276
  80.2 1.6 %copy-start.1 = (f32[128,4096]{1,0:T(8,128)S(1)}, f32[128,4096]{1,0:T(8,128)}, u32[]{:S(2)}) copy-start(f32[128,4096]{1,0:T(8,128)} %get-tuple-element.25) | copy-start | bytes 6291460
  83.3 20.6 %copy-start.6 = (f32[64,512]{1,0:T(8,128)S(1)}, f32[64,512]{1,0:T(8,128)}, u32[]{:S(2)}) copy-start(f32[64,512]{1,0:T(8,128)} %get-tuple-element.23) | copy-start | bytes 393220
  88.9 1.3 collective-permute-start.13
  90.2 14.6 %collective-permute-start.14 = (f32[64,128]{0,1:T(8,128)S(1)}, f32[64,128]{0,1:T(8,128)S(1)}, u32[]{:S(2)}, u32[]{:S(2)}) collective-permute-start(f32[64,128]{0,1:T(8,128)S(1)} %add.63), channel_id=1, source_target_pairs={{0,2},{2,0},{1,3},{3,1},{4,6},{6,4},{5,7},{7,5},{8,10},{10,8},{9,1... | collective-permute-start | bytes 98312 | tf_op jit(solution)/shard_map/ppermute | solution.py:276
  104.8 9.1 %copy-start = (f32[128,4096]{1,0:T(8,128)S(1)}, f32[128,4096]{1,0:T(8,128)}, u32[]{:S(2)}) copy-start(f32[128,4096]{1,0:T(8,128)} %get-tuple-element.29) | copy-start | bytes 6291460
  104.8 4.7 %collective-permute-start.15 = (f32[64,128]{0,1:T(8,128)S(1)}, f32[64,128]{0,1:T(8,128)S(1)}, u32[]{:S(2)}, u32[]{:S(2)}) collective-permute-start(f32[64,128]{0,1:T(8,128)S(1)} %add.64), channel_id=1, source_target_pairs={{0,4},{4,0},{8,12},{12,8},{1,5},{5,1},{9,13},{13,9},{2,6},{6,2},{1... | collective-permute-start | bytes 98312 | tf_op jit(solution)/shard_map/ppermute | solution.py:280
  105.9 6.6 %collective-permute-start.16 = (f32[64,128]{0,1:T(8,128)S(1)}, f32[64,128]{0,1:T(8,128)S(1)}, u32[]{:S(2)}, u32[]{:S(2)}) collective-permute-start(f32[64,128]{0,1:T(8,128)S(1)} %add.64), channel_id=1, source_target_pairs={{0,8},{4,12},{8,0},{12,4},{1,9},{5,13},{9,1},{13,5},{2,10},{6,14},... | collective-permute-start | bytes 98312 | tf_op jit(solution)/shard_map/ppermute | solution.py:280
  107.6 6.2 %collective-permute-start.17 = (f32[64,128]{0,1:T(8,128)S(1)}, f32[64,128]{0,1:T(8,128)S(1)}, u32[]{:S(2)}, u32[]{:S(2)}) collective-permute-start(f32[64,128]{0,1:T(8,128)S(1)} %add.64), channel_id=1, source_target_pairs={{0,12},{4,8},{8,4},{12,0},{1,13},{5,9},{9,5},{13,1},{2,14},{6,10},... | collective-permute-start | bytes 98312 | tf_op jit(solution)/shard_map/ppermute | solution.py:280
  113.8 1.7 %collective-permute-start.18 = (f32[64,128]{0,1:T(8,128)S(1)}, f32[64,128]{0,1:T(8,128)S(1)}, u32[]{:S(2)}, u32[]{:S(2)}) collective-permute-start(f32[64,128]{0,1:T(8,128)S(1)} %add_add_fusion), channel_id=1, source_target_pairs={{0,1},{1,0},{2,3},{3,2},{4,5},{5,4},{6,7},{7,6},{8,9},{9,8},{10,11... | collective-permute-start | bytes 98312 | tf_op jit(solution)/shard_map/ppermute | solution.py:276

commit v2 on v0

v2 whole, which is shorter than its diff:
```python
import functools

import jax
import jax.numpy as jnp
from jax import lax
from jax.experimental import pallas as pl
from jax.experimental.pallas import tpu as pltpu
from jax.sharding import PartitionSpec as P

BF16, F32, WIRE = jnp.bfloat16, jnp.float32, jnp.float16

COS = (
    0.9999999889369959,
    -0.4999998901135819,
    0.041666488148010265,
    -0.0013887798934755957,
    2.4769791619676175e-05,
    -2.7078195310289617e-07,
    1.7242244242579268e-09,
)
TURN_HEAD = 6.28125
TURN_REST = 0.0019353071795864769


def cosine(x):
    turns = jnp.round(x * 0.15915494309189535)
    x = (x - turns * TURN_HEAD) - turns * TURN_REST
    t = x * x
    y = COS[-1]
    for c in COS[-2::-1]:
        y = y * t + c
    return y


def split(x):
    high = x.astype(BF16)
    return high, (x - high.astype(F32)).astype(BF16)


def dot_nt(a, b):
    return lax.dot_general(a, b, (((1,), (1,)), ((), ())), preferred_element_type=F32)


LONG = pl.CostEstimate(flops=1000, bytes_accessed=20_000_000, transcendentals=0)
COST = pl.CostEstimate(flops=1000, bytes_accessed=1000, transcendentals=0)


def on_chip(kernel, name, out_shape, scalars=0, cost=COST, **extra):
    out_shape = [jax.ShapeDtypeStruct(*out) for out in out_shape]
    vmem = pl.BlockSpec(memory_space=pltpu.VMEM)
    smem = pl.BlockSpec(memory_space=pltpu.SMEM)

    def call(*args):
        return pl.pallas_call(
            kernel,
            in_specs=[smem] * scalars + [vmem] * (len(args) - scalars),
            out_specs=[vmem] * len(out_shape),
            out_shape=out_shape,
            cost_estimate=cost,
            compiler_params=pltpu.CompilerParams(vmem_limit_bytes=16 << 20),
            name=name,
            **extra,
        )(*args)

    return call


def half_rows(index, half):
    return pl.ds(pl.multiple_of(index * half, half), half)


def make_features(points, freqs, phases, feats, parts, at):
    count = points.shape[0]
    x = jnp.dot(points[...], freqs[:, at], preferred_element_type=F32) + phases[:, at]
    value = cosine(x)
    feats[:, at] = value
    parts[:count, at], parts[count:, at] = split(value)


def own_coefs(points, freqs, phases, basis, block=1024):
    count, width, rank = points.shape[0], freqs.shape[1], basis.shape[1]
    blocks = width // block
    spans = [pl.ds(i * block, block) for i in range(blocks)]

    def kernel(points, freqs, phases, basis, feats, coefs, freqs_in, phases_in, basis_in, points_in, parts, sems):
        first = [
            pltpu.make_async_copy(points, points_in, sems.at[0]),
            pltpu.make_async_copy(phases, phases_in, sems.at[1]),
        ]
        second = [
            pltpu.make_async_copy(freqs.at[:, at], freqs_in.at[:, at], sems.at[2 + i])
            for i, at in enumerate(spans)
        ]
        third = [
            pltpu.make_async_copy(basis.at[at, :], basis_in.at[at, :], sems.at[2 + blocks + i])
            for i, at in enumerate(spans)
        ]
        for copy in first + second + third:
            copy.start()
        for copy in first:
            copy.wait()
        for copy, at in zip(second, spans):
            copy.wait()
            make_features(points_in, freqs_in, phases_in, feats, parts, at)
        total = None
        for copy, at in zip(third, spans):
            copy.wait()
            value = jnp.dot(parts[:, at], basis_in[at, :], preferred_element_type=F32)
            total = value if total is None else total + value
        coefs[...] = total[:count] + total[count:]

    vmem = pl.BlockSpec(memory_space=pltpu.VMEM)
    hbm = pl.BlockSpec(memory_space=pltpu.HBM)
    return pl.pallas_call(
        kernel,
        in_specs=[hbm] * 4,
        out_specs=[vmem] * 5,
        out_shape=[
            jax.ShapeDtypeStruct((count, width), F32),
            jax.ShapeDtypeStruct((count, rank), F32),
            jax.ShapeDtypeStruct(freqs.shape, freqs.dtype),
            jax.ShapeDtypeStruct(phases.shape, phases.dtype),
            jax.ShapeDtypeStruct(basis.shape, basis.dtype),
        ],
        scratch_shapes=[
            pltpu.VMEM(points.shape, points.dtype),
            pltpu.VMEM((2 * count, width), BF16),
            pltpu.SemaphoreType.DMA((2 + 2 * blocks,)),
        ],
        cost_estimate=COST,
        compiler_params=pltpu.CompilerParams(vmem_limit_bytes=16 << 20),
        name="own_coefs",
    )(*(pltpu.with_memory_space_constraint(x, pltpu.HBM) for x in (points, freqs, phases, basis)))


def other_coefs(place, points, freqs, phases, basis, coefs, block=1024):
    count, width = points.shape[0], freqs.shape[1]

    def kernel(place, points, freqs, phases, basis, coefs, feats, keep, send, parts):
        for start in range(0, width, block):
            make_features(points, freqs, phases, feats, parts, pl.ds(start, block))
        total = jnp.dot(parts[...], basis[...], preferred_element_type=F32)
        others = total[:count] + total[count:]
        keep[...] = jnp.where(place[1] == 0, coefs[...], others)
        send[...] = jnp.where(place[1] == 0, others, coefs[...])

    return on_chip(
        kernel,
        "other_coefs",
        [((count, width), F32), (coefs.shape, F32), (coefs.shape, F32)],
        scalars=1,
        scratch_shapes=[pltpu.VMEM((2 * count, width), BF16)],
    )(place, points, freqs, phases, basis, coefs)


def own_columns(place, own, theirs, passed):
    count, rank = own.shape

    def kernel(place, own, theirs, passed, out):
        other = jnp.where(place[1] == 1, theirs[...], passed[...])
        first = place[0] == 0
        out[:, :rank] = jnp.where(first, own[...], other)
        out[:, rank:] = jnp.where(first, other, own[...])

    return on_chip(kernel, "own_columns", [((count, 2 * rank), F32)], scalars=1)(
        place, own, theirs, passed
    )[0]


def fit_body(place, parts, feats_a, feats_b, basis, fit, left, flip, offset):
    count, size = fit.shape
    half, width = count // 2, basis.shape[0]
    side = 1 - place[0] if flip else place[0]
    at = pl.ds(pl.multiple_of(side * (width // 2) + offset, 128), size)
    value = dot_nt(parts[...], basis[at, :])
    value = value[:count] + value[count:]
    fit[...] = value
    left[:half, :] = feats_b[:, at] - value[half:]
    left[half:, :] = feats_a[:, at] - value[:half]


def first_fit(place, kept, got, feats_a, feats_b, basis, flip, offset, size):
    count, rank = kept.shape

    def kernel(place, kept, got, feats_a, feats_b, basis, fit, left, own, parts):
        first = place[1] == 0
        own[...] = jnp.where(first, kept[...], got[...])
        other = jnp.where(first, got[...], kept[...])
        parts[:count, :], parts[2 * count : 3 * count, :] = split(own[...])
        parts[count : 2 * count, :], parts[3 * count :, :] = split(other)
        fit_body(place, parts, feats_a, feats_b, basis, fit, left, flip, offset)

    return on_chip(
        kernel,
        "first_fit",
        [((2 * count, size), F32)] * 2 + [((count, rank), F32), ((4 * count, rank), BF16)],
        scalars=1,
    )(place, kept, got, feats_a, feats_b, basis)


def fitted(place, parts, feats_a, feats_b, basis, flip, offset, size):
    def kernel(place, parts, feats_a, feats_b, basis, fit, left):
        fit_body(place, parts, feats_a, feats_b, basis, fit, left, flip, offset)

    return on_chip(kernel, "fit", [((parts.shape[0] // 2, size), F32)] * 2, scalars=1)(
        place, parts, feats_a, feats_b, basis
    )


def halves(x):
    return jnp.concatenate(split(x), axis=0)


def overlap(pieces, spans, span):
    start, size = span
    found = []
    for piece, (first, length) in zip(pieces, spans):
        low, high = max(start, first), min(start + size, first + length)
        if low < high:
            found.append((piece, low - first, high - first))
    return [x[0] for x in found], [x[1:] for x in found]


def residual(refs, cuts, got):
    left = [ref[:, low:high] for ref, (low, high) in zip(refs, cuts)]
    return halves(jnp.concatenate(left, axis=1) - got[...])


def add_gram(left, got, total=None):
    pieces, cuts = left
    count, size = got.shape

    def kernel(*refs):
        both = residual(refs, cuts, refs[len(cuts)])
        refs[-2][...] = both
        value = dot_nt(both, both)
        refs[-1][...] = value if total is None else refs[len(cuts) + 1][...] + value

    args = (*pieces, got) if total is None else (*pieces, got, total)
    return on_chip(
        kernel, "gram", [((2 * count, size), BF16), ((2 * count, 2 * count), F32)]
    )(*args)


def gram_halves(place, left, got, total):
    pieces, cuts = left
    count, size = got.shape
    half = count // 2

    def kernel(place, *refs):
        refs, (got, total, parts, keep, send, whole) = refs[:-6], refs[-6:]
        both = residual(refs, cuts, got)
        parts[...] = both
        value = total[...] + dot_nt(both, both)
        whole[...] = (value[:count, :count] + value[count:, count:]) + (
            value[:count, count:] + value[count:, :count]
        )
        ordered = place[0] == 1

        def rows(start):
            value = whole[half_rows(start, half), :]
            swapped = jnp.concatenate([value[:, half:], value[:, :half]], axis=1)
            return jnp.where(ordered, value, swapped)

        mine = jnp.where(ordered, place[1], 1 - place[1])
        keep[...] = rows(mine)
        send[...] = rows(1 - mine)

    return on_chip(
        kernel,
        "gram_halves",
        [((2 * count, size), BF16), ((half, count), F32), ((half, count), F32)],
        scalars=1,
        scratch_shapes=[pltpu.VMEM((count, count), F32)],
    )(place, *pieces, got, total)


def residual_parts(left, got):
    pieces, cuts = left
    count, size = got.shape

    def kernel(*refs):
        refs[-1][...] = residual(refs, cuts, refs[-2])

    return on_chip(kernel, "residual", [((2 * count, size), BF16)])(*pieces, got)[0]


ROWS = 8


def eliminate(matrix):
    size = matrix.shape[0]
    lane = lax.broadcasted_iota(jnp.int32, (ROWS, size), 1)
    row = lax.broadcasted_iota(jnp.int32, (ROWS, size), 0)
    count = size // ROWS
    upper = [matrix[ROWS * i : ROWS * (i + 1), :] for i in range(count)]
    lower = [jnp.where(lane == row + ROWS * i, 1.0, 0.0) for i in range(count)]

    def row_of(x, k):
        return jnp.broadcast_to(x[k : k + 1, :], (ROWS, size))

    def column_of(x, k):
        return jnp.broadcast_to(x[:, k : k + 1], (ROWS, size))

    pivots = []
    for p in range(count):
        columns = [column_of(upper[p], ROWS * p + k) for k in range(ROWS)]
        a, b = upper[p], lower[p]
        inverse, above = [], {}
        pivot = None
        for k in range(ROWS):
            d = row_of(columns[k], k)
            inverse.append(1.0 / d)
            pivot = d if pivot is None else jnp.where(row == k, d, pivot)
            if k < ROWS - 1:
                factor = jnp.where(row > k, columns[k] * inverse[k], 0.0)
                for j in range(k + 1, ROWS):
                    above[k, j] = row_of(columns[j], k)
                    columns[j] = columns[j] - factor * above[k, j]
                a = a - factor * row_of(a, k)
                b = b - factor * row_of(b, k)
        upper[p], lower[p] = a, b
        pivots.append(pivot)
        rows_a = [row_of(a, k) for k in range(ROWS)]
        rows_b = [row_of(b, k) for k in range(ROWS)]
        for i in range(p + 1, count):
            factors = []
            for k in range(ROWS):
                column = column_of(upper[i], ROWS * p + k)
                for j in range(k):
                    column = column - factors[j] * above[j, k]
                factors.append(column * inverse[k])
            for k in range(ROWS):
                upper[i] = upper[i] - factors[k] * rows_a[k]
                lower[i] = lower[i] - factors[k] * rows_b[k]
    return upper, lower, pivots


def factorize(place, kept, got, feats_total):
    half, size = kept.shape

    def kernel(place, kept, got, factor, weights, whole, inverse):
        first = place[1] == 0
        gram = jnp.concatenate(
            [jnp.where(first, kept[...], got[...]), jnp.where(first, got[...], kept[...])], axis=0
        ) * (1.0 / feats_total)
        upper, lower, pivots = eliminate(gram)
        lane = lax.broadcasted_iota(jnp.int32, (ROWS, size), 1)
        row = lax.broadcasted_iota(jnp.int32, (ROWS, size), 0)
        rows = []
        for i, pivot in enumerate(pivots):
            scale = 1.0 / jnp.sqrt(pivot)
            rows.append(jnp.where(lane >= row + ROWS * i, upper[i] * scale, 0.0))
            inverse[ROWS * i : ROWS * (i + 1), :] = lower[i] * scale
        whole[...] = jnp.concatenate(rows, axis=0).T
        factor[...] = whole[half_rows(place[0], half), :]
        own = inverse[half_rows(place[0], half), :]
        swapped = jnp.concatenate([own[:, half:], own[:, :half]], axis=1)
        weights[...] = jnp.where(place[0] == 1, own, swapped)

    return on_chip(
        kernel,
        "factorize",
        [((half, size), F32)] * 2,
        scalars=1,
        cost=LONG,
        scratch_shapes=[pltpu.VMEM((size, size), F32), pltpu.VMEM((size, size), F32)],
    )(place, kept, got)


def new_columns(place, weights, near, far):
    rows = weights.shape[0]
    sizes = [part.shape[1] for part in near + far]
    half = sum(sizes) // 2
    starts = [sum(sizes[:i]) % half for i in range(len(sizes))]

    def kernel(place, weights, *refs):
        parts, (out, whole, sems) = refs[:-3], refs[-3:]
        high, low = split(weights[...])
        lhs = jnp.concatenate(
            [jnp.concatenate([high, high], axis=1), jnp.concatenate([low, low], axis=1)], axis=0
        )
        copies = []
        for index, (start, size) in enumerate(zip(starts, sizes)):
            value = jnp.dot(lhs, parts[index][...], preferred_element_type=F32)
            side = place[0] if index < len(near) else 1 - place[0]
            at = pl.ds(pl.multiple_of(side * half + start, 128), size)
            whole[:, at] = value[:rows] + value[rows:]
            copies.append(pltpu.make_async_copy(whole.at[:, at], out.at[:, at], sems.at[index]))
            copies[-1].start()
        for copy in copies:
            copy.wait()

    vmem = pl.BlockSpec(memory_space=pltpu.VMEM)
    hbm = pl.BlockSpec(memory_space=pltpu.HBM)
    return pl.pallas_call(
        kernel,
        in_specs=[pl.BlockSpec(memory_space=pltpu.SMEM)] + [vmem] * (1 + len(sizes)),
        out_specs=hbm,
        out_shape=jax.ShapeDtypeStruct((rows, 2 * half), F32),
        scratch_shapes=[
            pltpu.VMEM((rows, 2 * half), F32),
            pltpu.SemaphoreType.DMA((len(sizes),)),
        ],
        cost_estimate=COST,
        compiler_params=pltpu.CompilerParams(vmem_limit_bytes=16 << 20),
        name="new_basis",
    )(place, weights, *near, *far)


def swap(x, axis):
    return lax.ppermute(x, axis, [(0, 1), (1, 0)])


def sum_over(x, axis, size):
    terms = [x] + [lax.ppermute(x, axis, [(i, i ^ m) for i in range(size)]) for m in range(1, size)]
    terms = [term.astype(F32) for term in terms]
    while len(terms) > 1:
        terms = [a + b for a, b in zip(terms[::2], terms[1::2])]
    return terms[0]


NEAR = (8, 8, 8, 8)
FAR = (8, 24)


def parted(total, shares):
    cuts = [total * sum(shares[: i + 1]) // sum(shares) // 128 * 128 for i in range(len(shares))]
    return [(start, stop - start) for start, stop in zip([0] + cuts, cuts)]


def paired(feat, feats_total, points, freqs, phases, basis):
    place = jnp.stack([lax.axis_index("pts"), lax.axis_index("sub")]).astype(jnp.int32)
    others = swap(points, "pts")
    feats_a, coefs, freqs, phases, basis = own_coefs(points, freqs, phases[None, :], basis)
    feats_b, keep, send = other_coefs(place, others, freqs, phases, basis, coefs)
    kept = sum_over((keep + swap(send, "sub")).astype(WIRE), "feat", feat)

    half = basis.shape[0] // 2
    near, far = parted(half, NEAR), parted(half, FAR)
    fit, rest, own, parts = first_fit(
        place, kept, swap(kept, "sub"), feats_a, feats_b, basis, 1, *near[0]
    )
    theirs = lax.ppermute(kept, ("pts", "sub"), [(1, 3), (3, 1)])

    def fill(flip, span):
        return fitted(place, parts, feats_a, feats_b, basis, flip, *span)

    fits_away, left_far = zip((fit, rest), *(fill(1, span) for span in near[1:]))
    parts, theirs = lax.optimization_barrier((parts, theirs))
    fits_back, left_near = zip(*(fill(0, span) for span in far))
    fits_away = [fit.astype(WIRE) for fit in fits_away]
    first_back, *fits_back = [fit.astype(WIRE) for fit in fits_back]

    def arrived(fit):
        return swap(fit, "pts").astype(F32)

    got = [arrived(fit) for fit in fits_away]
    total, resids = None, []
    for span, value in zip(near[:-1], got):
        value, total = add_gram(overlap(left_near, far, span), value, total)
        resids.append(value)
    first_got = arrived(first_back)
    total, *fits_back = lax.optimization_barrier((total, *fits_back))
    value, keep, send = gram_halves(place, overlap(left_near, far, near[-1]), got[-1], total)
    resids.append(value)
    gram = keep + swap(send, "sub")
    gram = gram + swap(gram, "pts")
    away = [residual_parts(overlap(left_far, near, far[0]), first_got)]
    gram, away[0], *fits_back = lax.optimization_barrier((gram, away[0], *fits_back))
    away += [
        residual_parts(overlap(left_far, near, span), arrived(fit))
        for span, fit in zip(far[1:], fits_back)
    ]
    gram = sum_over(gram, "feat", feat)
    factor, weights = factorize(place, gram, swap(gram, "sub"), feats_total)
    weights, theirs = lax.optimization_barrier((weights, theirs))
    coefs = own_columns(place, own, theirs, swap(theirs, "sub"))
    coefs, away[-1] = lax.optimization_barrier((coefs, away[-1]))
    new_basis = new_columns(place, weights, resids, away)
    return coefs.T, new_basis.T, factor


def general(feats_total, points, freqs, phases, basis):
    highest = lax.Precision.HIGHEST
    phase_in = jnp.einsum("pd,df->fp", points, freqs, preferred_element_type=F32)
    features = jnp.cos(phase_in + phases[:, None])
    point_cols = features.shape[1]
    whole_basis = lax.all_gather(basis, "pts", axis=1, tiled=True).astype(F32)
    partial_value = jnp.einsum("fk,fp->kp", whole_basis, features, precision=highest)
    coefs = lax.psum(partial_value, ("feat", "sub"))
    residual = features - jnp.dot(whole_basis, coefs, precision=highest)
    spread = lax.all_gather(residual, "pts", axis=1, tiled=True)
    block = jnp.einsum("fq,fp->qp", spread, residual, precision=highest)
    total_pts = block.shape[0]
    block = lax.psum(block, ("feat", "sub")) / feats_total
    gram = lax.all_gather(block, "pts", axis=1, tiled=True)
    factor = jnp.linalg.cholesky(gram)
    inverse = jax.scipy.linalg.solve_triangular(factor, jnp.eye(total_pts, dtype=F32), lower=True)
    offset = lax.axis_index("pts") * point_cols
    factor_rows = lax.dynamic_slice_in_dim(factor, offset, point_cols, 0)
    inv_rows = lax.dynamic_slice_in_dim(inverse, offset, point_cols, 0)
    new_basis = jnp.einsum("fq,pq->fp", spread, inv_rows, precision=highest)
    return coefs, new_basis, factor_rows


def solution(mesh):
    sizes = dict(mesh.shape)
    feat, pts, sub = sizes["feat"], sizes["pts"], sizes["sub"]

    def on_device(points, freqs, phases, basis):
        feats_total = phases.shape[0] * feat * sub
        if pts == 2 and sub == 2 and feat in (1, 2, 4, 8):
            return paired(feat, feats_total, points, freqs, phases, basis)
        return general(feats_total, points, freqs, phases, basis)

    return jax.shard_map(
        on_device,
        mesh=mesh,
        in_specs=(
            P(("groups", "pts"), None),
            P(None, ("feat", "sub")),
            P(("feat", "sub")),
            P(("groups", "feat", "sub"), "pts"),
        ),
        out_specs=(
            P("groups", "pts"),
            P(("groups", "feat", "sub"), "pts"),
            P(("groups", "pts"), None),
        ),
        check_vma=False,
    )
```

time: 433 us -> 82.1 us (0.19)
  waiting for transfers between devices: 306 us -> 31.4 us
  matrix products: 55 us -> 0 us
  blocking collectives: 33.5 us -> 0 us
  Pallas kernels: 0 us -> 27.1 us
  other arithmetic: 22.9 us -> 0.68 us
  starting transfers between devices: 0.3 us -> 21.7 us
  between operations: 13.8 us -> 1.05 us
    all_gather x2 -> x0, waiting for transfers between devices: 250 us -> none  [the longest x1 194 us: on_device(): lax.all_gather(basis, 'pts', axis=1, tiled=True).astype(jnp.float32)]
    psum x1 -> x0, waiting for transfers between devices: 54.8 us -> none  [on_device(): coefs = lax.psum(partial_value, ('feat', 'sub'))]
    dot_general x5 -> x0, matrix products: 54.8 us -> none  [the longest x1 19.7 us: on_device(): fitted = jnp.dot(whole_basis, coefs, precision=highest)]
    ppermute x0 -> x20, waiting for transfers between devices: none -> 31.4 us  [the longest x13 21.5 us: swap(): return lax.ppermute(x, axis, [(0, 1), (1, 0)])]
    psum x1 -> x0, blocking collectives: 28.7 us -> none  [on_device(): block = lax.psum(block, ('feat', 'sub')) / FEATS]
    pallas_call x0 -> x17, Pallas kernels: none -> 27.1 us  [the longest x15 19 us: call(): pl.pallas_call(kernel, in_specs=[smem] * scalars + [vmem] * (len(args) -...]
    another operation x5 -> x1, other arithmetic: 22.9 us -> 0.07 us  [paired(): jnp.stack([lax.axis_index('pts'), lax.axis_index('sub')]).astype(jnp.int32)]
    ppermute x0 -> x20, starting transfers between devices: none -> 21.7 us  [the longest x13 12 us: swap(): return lax.ppermute(x, axis, [(0, 1), (1, 0)])]
  transfers between devices with their start and end apart: 3 -> 20, of which waited for: 3 -> 15; matrix products, arithmetic and copies ran while one was open for 2% -> 1% of each run, Pallas kernels for 0% -> 26%
where the time goes in v2:
time: 82.1 us; the launch traced here: 81.9 us
  waiting for transfers between devices  31.4 us (38%)
  Pallas kernels  27.1 us (33%)
  starting transfers between devices  21.7 us (26%)
  between operations  1.05 us (1%)
    ppermute x13, waiting for transfers between devices, swap(): return lax.ppermute(x, axis, [(0, 1), (1, 0)])  21.5 us
    pallas_call x15, Pallas kernels, call(): pl.pallas_call(kernel, in_specs=[smem] * scalars + [vmem] * (len(args) -...  19 us
    ppermute x13, starting transfers between devices, swap(): return lax.ppermute(x, axis, [(0, 1), (1, 0)])  12 us
    ppermute x6, waiting for transfers between devices, sum_over(): lax.ppermute(x, axis, [(i, i ^ m) for i in range(size)])  9.85 us
    ppermute x6, starting transfers between devices, sum_over(): lax.ppermute(x, axis, [(i, i ^ m) for i in range(size)])  8.84 us
    pallas_call x1, Pallas kernels, own_coefs(): pl.pallas_call(kernel, in_specs=[hbm] * 4, out_specs=[vmem] * 5, out_shap...  5.91 us
    pallas_call x1, Pallas kernels, new_columns(): pl.pallas_call(kernel, in_specs=[pl.BlockSpec(memory_space=pltpu.SMEM)] +...  2.19 us
  transfers between devices with their start and end apart: 20, of which 15 were waited for; matrix products, arithmetic and copies ran while one was open for 1% of the time, Pallas kernels for 26%

profile of v2, /device:TPU:0, one launch (start us, length us, event | category | flops | bytes accessed | tf_op | source)
XLA Modules:
  0.0 81.9 jit_solution(578502567159993337)
XLA Ops:
  0.6 3.0 %collective-permute-start = (bf16[64,256]{1,0:T(8,128)(2,1)}, bf16[64,256]{1,0:T(8,128)(2,1)S(1)}, u32[]{:S(2)}, u32[]{:S(2)}) collective-permute-start(bf16[64,256]{1,0:T(8,128)(2,1)} %points.1), channel_id=1, source_target_pairs={{0,2},{2,0},{1,3},{3,1},{4,6},{6,4},{5,7},{7,5},{8,10},{10,8},{9,1... | collective-permute-start | bytes 98312 | tf_op jit(solution)/shard_map/ppermute | solution.py:412
  3.7 5.9 %own_coefs.1 = (f32[64,8192]{1,0:T(8,128)S(1)}, f32[64,512]{1,0:T(8,128)S(1)}, bf16[256,8192]{1,0:T(8,128)(2,1)S(1)}, f32[1,8192]{1,0:T(1,128)S(1)}, bf16[8192,512]{1,0:T(8,128)(2,1)S(1)}) custom-call(bf16[64,256]{1,0:T(8,128)(2,1)} %points.1, bf16[256,8192]{1,0:T(8,128)(2,1)} %freqs.1, f32[1,8192]{1,0:T(1,128)} %bitcast.7, bf16[8192,512]{1,0:T(8,128)(2,1)} %basis.1), custom_call_target="tpu_custom_call" | custom-call | flops 1000 | bytes 1000 | tf_op jit(solution)/shard_map/own_coefs/pallas_call | solution.py:114
  9.6 3.4 %other_coefs.1 = (f32[64,8192]{1,0:T(8,128)S(1)}, f32[64,512]{1,0:T(8,128)S(1)}, f32[64,512]{1,0:T(8,128)S(1)}) custom-call(s32[2]{0:T(128)S(1)} %pad_add_fusion.place, bf16[64,256]{1,0:T(8,128)(2,1)S(1)} %collective-permute-done.points, bf16[256,8192]{1,0:T(8,128)(2,1)S(1)} %get-tuple-element.47.freqs, f32[1,8192]{1,0:T(1,128)S(1)} %get-tuple-element.48.phases, ...), custom_call_target="tpu_custom_call" | custom-call | flops 1000 | bytes 1000 | tf_op jit(solution)/shard_map/other_coefs/pallas_call | solution.py:54
  13.1 1.3 %collective-permute-done.1 = f32[64,512]{1,0:T(8,128)S(1)} collective-permute-done((f32[64,512]{1,0:T(8,128)S(1)}, f32[64,512]{1,0:T(8,128)S(1)}, u32[]{:S(2)}, u32[]{:S(2)}) %collective-permute-start.1) | collective-permute-done | bytes 131104 | tf_op jit(solution)/shard_map/ppermute | solution.py:412
  14.5 1.6 %collective-permute-start.2 = (f16[64,512]{1,0:T(8,128)(2,1)S(1)}, f16[64,512]{1,0:T(8,128)(2,1)S(1)}, u32[]{:S(2)}, u32[]{:S(2)}) collective-permute-start(f16[64,512]{1,0:T(8,128)(2,1)S(1)} %add_convert_fusion), channel_id=1, source_target_pairs={{0,4},{4,0},{8,12},{12,8},{1,5},{5,1},{9,13},{13,9},{2,6},{6,2},{1... | collective-permute-start | bytes 196616 | tf_op jit(solution)/shard_map/ppermute | solution.py:416
  16.1 2.6 %collective-permute-start.3 = (f16[64,512]{1,0:T(8,128)(2,1)S(1)}, f16[64,512]{1,0:T(8,128)(2,1)S(1)}, u32[]{:S(2)}, u32[]{:S(2)}) collective-permute-start(f16[64,512]{1,0:T(8,128)(2,1)S(1)} %add_convert_fusion), channel_id=1, source_target_pairs={{0,8},{4,12},{8,0},{12,4},{1,9},{5,13},{9,1},{13,5},{2,10},{6,14},... | collective-permute-start | bytes 196616 | tf_op jit(solution)/shard_map/ppermute | solution.py:416
  18.7 0.2 collective-permute-start.4
  18.9 4.7 %collective-permute-done.3 = f16[64,512]{1,0:T(8,128)(2,1)S(1)} collective-permute-done((f16[64,512]{1,0:T(8,128)(2,1)S(1)}, f16[64,512]{1,0:T(8,128)(2,1)S(1)}, u32[]{:S(2)}, u32[]{:S(2)}) %collective-permute-start.3) | collective-permute-done | bytes 65568 | tf_op jit(solution)/shard_map/ppermute | solution.py:416
  23.7 1.2 %collective-permute-done.4 = f16[64,512]{1,0:T(8,128)(2,1)S(1)} collective-permute-done((f16[64,512]{1,0:T(8,128)(2,1)S(1)}, f16[64,512]{1,0:T(8,128)(2,1)S(1)}, u32[]{:S(2)}, u32[]{:S(2)}) %collective-permute-start.4) | collective-permute-done | bytes 65568 | tf_op jit(solution)/shard_map/ppermute | solution.py:416
  25.0 0.8 %collective-permute-start.6 = (f32[64,512]{1,0:T(8,128)S(1)}, f32[64,512]{1,0:T(8,128)S(1)}, u32[]{:S(2)}, u32[]{:S(2)}) collective-permute-start(f32[64,512]{1,0:T(8,128)S(1)} %add_add_fusion.kept), channel_id=1, source_target_pairs={{1,3},{3,1},{5,7},{7,5},{9,11},{11,9},{13,15},{15,13},{17,19},{19,... | collective-permute-start | bytes 393224 | tf_op jit(solution)/shard_map/ppermute | solution.py:444
  25.9 0.5 collective-permute-done.5.got
  26.4 1.0 %first_fit.1 = (f32[128,1024]{1,0:T(8,128)S(1)}, f32[128,1024]{1,0:T(8,128)S(1)}, f32[64,512]{1,0:T(8,128)S(1)}, bf16[256,512]{1,0:T(8,128)(2,1)S(1)}) custom-call(s32[2]{0:T(128)S(1)} %pad_add_fusion.place, f32[64,512]{1,0:T(8,128)S(1)} %add_add_fusion.kept, f32[64,512]{1,0:T(8,128)S(1)} %collective-permute-done.5.got, ...), custom_call_target="tpu_custom_call" | custom-call | flops 1000 | bytes 1000 | tf_op jit(solution)/shard_map/first_fit/pallas_call | solution.py:54
  27.4 0.6 collective-permute-start.10
  28.0 1.0 %fit.8 = (f32[128,1024]{1,0:T(8,128)S(1)}, f32[128,1024]{1,0:T(8,128)S(1)}) custom-call(s32[2]{0:T(128)S(1)} %pad_add_fusion.place, bf16[256,512]{1,0:T(8,128)(2,1)S(1)} %get-tuple-element.57.parts, f32[64,8192]{1,0:T(8,128)S(1)} %get-tuple-element.53.feats_a, f32[64,8192]{1,0:T(8,128)S(1)} %get-tuple-element.54.feats_b, ...), custom_call_target="tpu_custom_call" | custom-call | flops 1000 | bytes 1000 | tf_op jit(solution)/shard_map/fit/pallas_call | solution.py:54
  29.1 1.6 %collective-permute-start.9 = (f16[128,1024]{1,0:T(8,128)(2,1)S(1)}, f16[128,1024]{1,0:T(8,128)(2,1)S(1)}, u32[]{:S(2)}, u32[]{:S(2)}) collective-permute-start(f16[128,1024]{1,0:T(8,128)(2,1)S(1)} %convert_element_type.60), channel_id=1, source_target_pairs={{0,2},{2,0},{1,3},{3,1},{4,6},{6,4},{5,7},{7,5},{8,10},{10,8},{9,1... | collective-permute-start | bytes 786440 | tf_op jit(solution)/shard_map/ppermute | solution.py:412
  30.6 1.0 %fit.7 = (f32[128,1024]{1,0:T(8,128)S(1)}, f32[128,1024]{1,0:T(8,128)S(1)}) custom-call(s32[2]{0:T(128)S(1)} %pad_add_fusion.place, bf16[256,512]{1,0:T(8,128)(2,1)S(1)} %get-tuple-element.57.parts, f32[64,8192]{1,0:T(8,128)S(1)} %get-tuple-element.53.feats_a, f32[64,8192]{1,0:T(8,128)S(1)} %get-tuple-element.54.feats_b, ...), custom_call_target="tpu_custom_call" | custom-call | flops 1000 | bytes 1000 | tf_op jit(solution)/shard_map/fit/pallas_call | solution.py:54
  31.7 0.6 collective-permute-start.8
  32.3 1.0 %fit.6 = (f32[128,1024]{1,0:T(8,128)S(1)}, f32[128,1024]{1,0:T(8,128)S(1)}) custom-call(s32[2]{0:T(128)S(1)} %pad_add_fusion.place, bf16[256,512]{1,0:T(8,128)(2,1)S(1)} %get-tuple-element.57.parts, f32[64,8192]{1,0:T(8,128)S(1)} %get-tuple-element.53.feats_a, f32[64,8192]{1,0:T(8,128)S(1)} %get-tuple-element.54.feats_b, ...), custom_call_target="tpu_custom_call" | custom-call | flops 1000 | bytes 1000 | tf_op jit(solution)/shard_map/fit/pallas_call | solution.py:54
  33.3 1.6 %collective-permute-start.7 = (f16[128,1024]{1,0:T(8,128)(2,1)S(1)}, f16[128,1024]{1,0:T(8,128)(2,1)S(1)}, u32[]{:S(2)}, u32[]{:S(2)}) collective-permute-start(f16[128,1024]{1,0:T(8,128)(2,1)S(1)} %convert_element_type.56), channel_id=1, source_target_pairs={{0,2},{2,0},{1,3},{3,1},{4,6},{6,4},{5,7},{7,5},{8,10},{10,8},{9,1... | collective-permute-start | bytes 786440 | tf_op jit(solution)/shard_map/ppermute | solution.py:412
  34.9 1.0 %fit.9 = (f32[128,1024]{1,0:T(8,128)S(1)}, f32[128,1024]{1,0:T(8,128)S(1)}) custom-call(s32[2]{0:T(128)S(1)} %pad_add_fusion.place, bf16[256,512]{1,0:T(8,128)(2,1)S(1)} %get-tuple-element.57.parts, f32[64,8192]{1,0:T(8,128)S(1)} %get-tuple-element.53.feats_a, f32[64,8192]{1,0:T(8,128)S(1)} %get-tuple-element.54.feats_b, ...), custom_call_target="tpu_custom_call" | custom-call | flops 1000 | bytes 1000 | tf_op jit(solution)/shard_map/fit/pallas_call | solution.py:54
  36.0 0.6 collective-permute-start.13
  36.6 1.6 %fit.5 = (f32[128,3072]{1,0:T(8,128)S(1)}, f32[128,3072]{1,0:T(8,128)S(1)}) custom-call(s32[2]{0:T(128)S(1)} %pad_add_fusion.place, bf16[256,512]{1,0:T(8,128)(2,1)S(1)} %get-tuple-element.57.parts, f32[64,8192]{1,0:T(8,128)S(1)} %get-tuple-element.53.feats_a, f32[64,8192]{1,0:T(8,128)S(1)} %get-tuple-element.54.feats_b, ...), custom_call_target="tpu_custom_call" | custom-call | flops 1000 | bytes 1000 | tf_op jit(solution)/shard_map/fit/pallas_call | solution.py:54
  38.4 0.4 gram.3
  38.7 3.6 %collective-permute-done.9 = f16[128,1024]{1,0:T(8,128)(2,1)S(1)} collective-permute-done((f16[128,1024]{1,0:T(8,128)(2,1)S(1)}, f16[128,1024]{1,0:T(8,128)(2,1)S(1)}, u32[]{:S(2)}, u32[]{:S(2)}) %collective-permute-start.9) | collective-permute-done | bytes 262176 | tf_op jit(solution)/shard_map/ppermute | solution.py:412
  42.3 0.4 gram.4
  42.7 5.2 %collective-permute-done.8 = f16[128,1024]{1,0:T(8,128)(2,1)S(1)} collective-permute-done((f16[128,1024]{1,0:T(8,128)(2,1)S(1)}, f16[128,1024]{1,0:T(8,128)(2,1)S(1)}, u32[]{:S(2)}, u32[]{:S(2)}) %collective-permute-start.8) | collective-permute-done | bytes 262176 | tf_op jit(solution)/shard_map/ppermute | solution.py:412
  48.0 0.4 gram.5
  48.3 5.2 %collective-permute-done.7 = f16[128,1024]{1,0:T(8,128)(2,1)S(1)} collective-permute-done((f16[128,1024]{1,0:T(8,128)(2,1)S(1)}, f16[128,1024]{1,0:T(8,128)(2,1)S(1)}, u32[]{:S(2)}, u32[]{:S(2)}) %collective-permute-start.7) | collective-permute-done | bytes 262176 | tf_op jit(solution)/shard_map/ppermute | solution.py:412
  53.6 1.0 %gram_halves.1 = (bf16[256,1024]{1,0:T(8,128)(2,1)S(1)}, f32[64,128]{1,0:T(8,128)S(1)}, f32[64,128]{1,0:T(8,128)S(1)}) custom-call(s32[2]{0:T(128)S(1)} %pad_add_fusion.place, f32[128,3072]{1,0:T(8,128)S(1)} %get-tuple-element.58.refs_0_, f32[128,1024]{1,0:T(8,128)S(1)} %convert_element_type.57.refs_1_, f32[256,256]{1,0:T(8,128)S(1)} %get-tuple-element.68.refs_2_), custom_call_target="tpu_custom_call" | custom-call | flops 1000 | bytes 1000 | tf_op jit(solution)/shard_map/gram_halves/pallas_call | solution.py:54
  54.6 0.9 %collective-permute-start.11 = (f32[64,128]{1,0:T(8,128)S(1)}, f32[64,128]{1,0:T(8,128)S(1)}, u32[]{:S(2)}, u32[]{:S(2)}) collective-permute-start(f32[64,128]{1,0:T(8,128)S(1)} %get-tuple-element.70), channel_id=1, source_target_pairs={{0,1},{1,0},{2,3},{3,2},{4,5},{5,4},{6,7},{7,6},{8,9},{9,8},{10,11... | collective-permute-start | bytes 98312 | tf_op jit(solution)/shard_map/ppermute | solution.py:412
  55.4 0.9 %collective-permute-done.11 = f32[64,128]{1,0:T(8,128)S(1)} collective-permute-done((f32[64,128]{1,0:T(8,128)S(1)}, f32[64,128]{1,0:T(8,128)S(1)}, u32[]{:S(2)}, u32[]{:S(2)}) %collective-permute-start.11) | collective-permute-done | bytes 32800 | tf_op jit(solution)/shard_map/ppermute | solution.py:412
  56.3 1.4 %collective-permute-start.12 = (f32[64,128]{1,0:T(8,128)S(1)}, f32[64,128]{1,0:T(8,128)S(1)}, u32[]{:S(2)}, u32[]{:S(2)}) collective-permute-start(f32[64,128]{1,0:T(8,128)S(1)} %add.31), channel_id=1, source_target_pairs={{0,2},{2,0},{1,3},{3,1},{4,6},{6,4},{5,7},{7,5},{8,10},{10,8},{9,1... | collective-permute-start | bytes 98312 | tf_op jit(solution)/shard_map/ppermute | solution.py:412
  57.7 1.4 %collective-permute-done.13 = f16[128,1024]{1,0:T(8,128)(2,1)S(1)} collective-permute-done((f16[128,1024]{1,0:T(8,128)(2,1)S(1)}, f16[128,1024]{1,0:T(8,128)(2,1)S(1)}, u32[]{:S(2)}, u32[]{:S(2)}) %collective-permute-start.13) | collective-permute-done | bytes 262176 | tf_op jit(solution)/shard_map/ppermute | solution.py:412
  59.3 0.9 %collective-permute-done.12 = f32[64,128]{1,0:T(8,128)S(1)} collective-permute-done((f32[64,128]{1,0:T(8,128)S(1)}, f32[64,128]{1,0:T(8,128)S(1)}, u32[]{:S(2)}, u32[]{:S(2)}) %collective-permute-start.12) | collective-permute-done | bytes 32800 | tf_op jit(solution)/shard_map/ppermute | solution.py:412
  60.2 1.4 %collective-permute-start.19 = (f16[128,3072]{1,0:T(8,128)(2,1)S(1)}, f16[128,3072]{1,0:T(8,128)(2,1)S(1)}, u32[]{:S(2)}, u32[]{:S(2)}) collective-permute-start(f16[128,3072]{1,0:T(8,128)(2,1)S(1)} %convert_element_type.64), channel_id=1, source_target_pairs={{0,2},{2,0},{1,3},{3,1},{4,6},{6,4},{5,7},{7,5},{8,10},{10,8},{9,1... | collective-permute-start | bytes 2359304 | tf_op jit(solution)/shard_map/ppermute | solution.py:412
  61.6 0.8 %collective-permute-start.14 = (f32[64,128]{1,0:T(8,128)S(1)}, f32[64,128]{1,0:T(8,128)S(1)}, u32[]{:S(2)}, u32[]{:S(2)}) collective-permute-start(f32[64,128]{1,0:T(8,128)S(1)} %add.32), channel_id=1, source_target_pairs={{0,4},{4,0},{8,12},{12,8},{1,5},{5,1},{9,13},{13,9},{2,6},{6,2},{1... | collective-permute-start | bytes 98312 | tf_op jit(solution)/shard_map/ppermute | solution.py:416
  62.5 1.7 %collective-permute-start.15 = (f32[64,128]{1,0:T(8,128)S(1)}, f32[64,128]{1,0:T(8,128)S(1)}, u32[]{:S(2)}, u32[]{:S(2)}) collective-permute-start(f32[64,128]{1,0:T(8,128)S(1)} %add.32), channel_id=1, source_target_pairs={{0,8},{4,12},{8,0},{12,4},{1,9},{5,13},{9,1},{13,5},{2,10},{6,14},... | collective-permute-start | bytes 98312 | tf_op jit(solution)/shard_map/ppermute | solution.py:416
  64.2 1.8 %collective-permute-start.16 = (f32[64,128]{1,0:T(8,128)S(1)}, f32[64,128]{1,0:T(8,128)S(1)}, u32[]{:S(2)}, u32[]{:S(2)}) collective-permute-start(f32[64,128]{1,0:T(8,128)S(1)} %add.32), channel_id=1, source_target_pairs={{0,12},{4,8},{8,4},{12,0},{1,13},{5,9},{9,5},{13,1},{2,14},{6,10},... | collective-permute-start | bytes 98312 | tf_op jit(solution)/shard_map/ppermute | solution.py:416
  66.0 2.0 %collective-permute-done.15 = f32[64,128]{1,0:T(8,128)S(1)} collective-permute-done((f32[64,128]{1,0:T(8,128)S(1)}, f32[64,128]{1,0:T(8,128)S(1)}, u32[]{:S(2)}, u32[]{:S(2)}) %collective-permute-start.15) | collective-permute-done | bytes 32800 | tf_op jit(solution)/shard_map/ppermute | solution.py:416
  68.0 1.9 %collective-permute-done.16 = f32[64,128]{1,0:T(8,128)S(1)} collective-permute-done((f32[64,128]{1,0:T(8,128)S(1)}, f32[64,128]{1,0:T(8,128)S(1)}, u32[]{:S(2)}, u32[]{:S(2)}) %collective-permute-start.16) | collective-permute-done | bytes 32800 | tf_op jit(solution)/shard_map/ppermute | solution.py:416
  70.0 1.2 %collective-permute-done.17.got = f32[64,128]{1,0:T(8,128)S(1)} collective-permute-done((f32[64,128]{1,0:T(8,128)S(1)}, f32[64,128]{1,0:T(8,128)S(1)}, u32[]{:S(2)}, u32[]{:S(2)}) %collective-permute-start.17) | collective-permute-done | bytes 32800 | tf_op jit(solution)/shard_map/ppermute | solution.py:412
  71.2 5.1 %factorize.1 = (f32[64,128]{1,0:T(8,128)}, f32[64,128]{1,0:T(8,128)S(1)}) custom-call(s32[2]{0:T(128)S(1)} %pad_add_fusion.place, f32[64,128]{1,0:T(8,128)S(1)} %add_add_fusion.1.kept, f32[64,128]{1,0:T(8,128)S(1)} %collective-permute-done.17.got), custom_call_target="tpu_custom_call" | custom-call | flops 1000 | bytes 20000000 | tf_op jit(solution)/shard_map/factorize/pallas_call | solution.py:54
  76.3 0.2 collective-permute-start.18
  76.5 1.2 %collective-permute-done.18.passed = f32[64,512]{1,0:T(8,128)S(1)} collective-permute-done((f32[64,512]{1,0:T(8,128)S(1)}, f32[64,512]{1,0:T(8,128)S(1)}, u32[]{:S(2)}, u32[]{:S(2)}) %collective-permute-start.18) | collective-permute-done | bytes 131104 | tf_op jit(solution)/shard_map/ppermute | solution.py:412
  77.7 1.3 %own_columns.1 = f32[64,1024]{1,0:T(8,128)} custom-call(s32[2]{0:T(128)S(1)} %pad_add_fusion.place, f32[64,512]{1,0:T(8,128)S(1)} %get-tuple-element.55.own, f32[64,512]{1,0:T(8,128)S(1)} %collective-permute-done.6.theirs, f32[64,512]{1,0:T(8,128)S(1)} %collective-permute-done.18.passed), custom_call_target="tpu_custom_call" | custom-call | flops 1000 | bytes 1000 | tf_op jit(solution)/shard_map/own_columns/pallas_call | solution.py:54
  78.9 0.2 collective-permute-done.19
  79.2 0.3 residual.3.refs_5_
  79.6 2.2 %new_basis.1 = f32[64,8192]{1,0:T(8,128)} custom-call(s32[2]{0:T(128)S(1)} %pad_add_fusion.place, f32[64,128]{1,0:T(8,128)S(1)} %get-tuple-element.83.weights, bf16[256,1024]{1,0:T(8,128)(2,1)S(1)} %get-tuple-element.84.refs_0_, bf16[256,1024]{1,0:T(8,128)(2,1)S(1)} %get-tuple-element.85.refs_1_, bf16[256,1024]{1,0:T(8,128)(2,1)S(1)} %get-tuple-element.86.refs_2_, ...), custom_call_target="tpu_custom_call" | custom-call | flops 1000 | bytes 1000 | tf_op jit(solution)/shard_map/new_basis/pallas_call | solution.py:396
  (27 shorter events, 1.0 us)
Async XLA Ops:
  0.6 9.0 %collective-permute-start = (bf16[64,256]{1,0:T(8,128)(2,1)}, bf16[64,256]{1,0:T(8,128)(2,1)S(1)}, u32[]{:S(2)}, u32[]{:S(2)}) collective-permute-start(bf16[64,256]{1,0:T(8,128)(2,1)} %points.1), channel_id=1, source_target_pairs={{0,2},{2,0},{1,3},{3,1},{4,6},{6,4},{5,7},{7,5},{8,10},{10,8},{9,1... | collective-permute-start | bytes 98312 | tf_op jit(solution)/shard_map/ppermute | solution.py:412
  13.0 1.4 %collective-permute-start.1 = (f32[64,512]{1,0:T(8,128)S(1)}, f32[64,512]{1,0:T(8,128)S(1)}, u32[]{:S(2)}, u32[]{:S(2)}) collective-permute-start(f32[64,512]{1,0:T(8,128)S(1)} %get-tuple-element.52), channel_id=1, source_target_pairs={{0,1},{1,0},{2,3},{3,2},{4,5},{5,4},{6,7},{7,6},{8,9},{9,8},{10,11... | collective-permute-start | bytes 393224 | tf_op jit(solution)/shard_map/ppermute | solution.py:412
  14.5 4.5 %collective-permute-start.2 = (f16[64,512]{1,0:T(8,128)(2,1)S(1)}, f16[64,512]{1,0:T(8,128)(2,1)S(1)}, u32[]{:S(2)}, u32[]{:S(2)}) collective-permute-start(f16[64,512]{1,0:T(8,128)(2,1)S(1)} %add_convert_fusion), channel_id=1, source_target_pairs={{0,4},{4,0},{8,12},{12,8},{1,5},{5,1},{9,13},{13,9},{2,6},{6,2},{1... | collective-permute-start | bytes 196616 | tf_op jit(solution)/shard_map/ppermute | solution.py:416
  16.1 7.5 %collective-permute-start.3 = (f16[64,512]{1,0:T(8,128)(2,1)S(1)}, f16[64,512]{1,0:T(8,128)(2,1)S(1)}, u32[]{:S(2)}, u32[]{:S(2)}) collective-permute-start(f16[64,512]{1,0:T(8,128)(2,1)S(1)} %add_convert_fusion), channel_id=1, source_target_pairs={{0,8},{4,12},{8,0},{12,4},{1,9},{5,13},{9,1},{13,5},{2,10},{6,14},... | collective-permute-start | bytes 196616 | tf_op jit(solution)/shard_map/ppermute | solution.py:416
  18.7 6.2 %collective-permute-start.4 = (f16[64,512]{1,0:T(8,128)(2,1)S(1)}, f16[64,512]{1,0:T(8,128)(2,1)S(1)}, u32[]{:S(2)}, u32[]{:S(2)}) collective-permute-start(f16[64,512]{1,0:T(8,128)(2,1)S(1)} %add_convert_fusion), channel_id=1, source_target_pairs={{0,12},{4,8},{8,4},{12,0},{1,13},{5,9},{9,5},{13,1},{2,14},{6,10},... | collective-permute-start | bytes 196616 | tf_op jit(solution)/shard_map/ppermute | solution.py:416
  24.9 1.4 %collective-permute-start.5 = (f32[64,512]{1,0:T(8,128)S(1)}, f32[64,512]{1,0:T(8,128)S(1)}, u32[]{:S(2)}, u32[]{:S(2)}) collective-permute-start(f32[64,512]{1,0:T(8,128)S(1)} %add_add_fusion.kept), channel_id=1, source_target_pairs={{0,1},{1,0},{2,3},{3,2},{4,5},{5,4},{6,7},{7,6},{8,9},{9,8},{10,11... | collective-permute-start | bytes 393224 | tf_op jit(solution)/shard_map/ppermute | solution.py:412
  25.0 9.9 %collective-permute-start.6 = (f32[64,512]{1,0:T(8,128)S(1)}, f32[64,512]{1,0:T(8,128)S(1)}, u32[]{:S(2)}, u32[]{:S(2)}) collective-permute-start(f32[64,512]{1,0:T(8,128)S(1)} %add_add_fusion.kept), channel_id=1, source_target_pairs={{1,3},{3,1},{5,7},{7,5},{9,11},{11,9},{13,15},{15,13},{17,19},{19,... | collective-permute-start | bytes 393224 | tf_op jit(solution)/shard_map/ppermute | solution.py:444
  27.4 10.9 %collective-permute-start.10 = (f16[128,1024]{1,0:T(8,128)(2,1)S(1)}, f16[128,1024]{1,0:T(8,128)(2,1)S(1)}, u32[]{:S(2)}, u32[]{:S(2)}) collective-permute-start(f16[128,1024]{1,0:T(8,128)(2,1)S(1)} %convert_element_type.62), channel_id=1, source_target_pairs={{0,2},{2,0},{1,3},{3,1},{4,6},{6,4},{5,7},{7,5},{8,10},{10,8},{9,1... | collective-permute-start | bytes 786440 | tf_op jit(solution)/shard_map/ppermute | solution.py:412
  29.1 13.2 %collective-permute-start.9 = (f16[128,1024]{1,0:T(8,128)(2,1)S(1)}, f16[128,1024]{1,0:T(8,128)(2,1)S(1)}, u32[]{:S(2)}, u32[]{:S(2)}) collective-permute-start(f16[128,1024]{1,0:T(8,128)(2,1)S(1)} %convert_element_type.60), channel_id=1, source_target_pairs={{0,2},{2,0},{1,3},{3,1},{4,6},{6,4},{5,7},{7,5},{8,10},{10,8},{9,1... | collective-permute-start | bytes 786440 | tf_op jit(solution)/shard_map/ppermute | solution.py:412
  31.7 16.2 %collective-permute-start.8 = (f16[128,1024]{1,0:T(8,128)(2,1)S(1)}, f16[128,1024]{1,0:T(8,128)(2,1)S(1)}, u32[]{:S(2)}, u32[]{:S(2)}) collective-permute-start(f16[128,1024]{1,0:T(8,128)(2,1)S(1)} %convert_element_type.58), channel_id=1, source_target_pairs={{0,2},{2,0},{1,3},{3,1},{4,6},{6,4},{5,7},{7,5},{8,10},{10,8},{9,1... | collective-permute-start | bytes 786440 | tf_op jit(solution)/shard_map/ppermute | solution.py:412
  33.3 20.2 %collective-permute-start.7 = (f16[128,1024]{1,0:T(8,128)(2,1)S(1)}, f16[128,1024]{1,0:T(8,128)(2,1)S(1)}, u32[]{:S(2)}, u32[]{:S(2)}) collective-permute-start(f16[128,1024]{1,0:T(8,128)(2,1)S(1)} %convert_element_type.56), channel_id=1, source_target_pairs={{0,2},{2,0},{1,3},{3,1},{4,6},{6,4},{5,7},{7,5},{8,10},{10,8},{9,1... | collective-permute-start | bytes 786440 | tf_op jit(solution)/shard_map/ppermute | solution.py:412
  36.0 23.2 %collective-permute-start.13 = (f16[128,1024]{1,0:T(8,128)(2,1)S(1)}, f16[128,1024]{1,0:T(8,128)(2,1)S(1)}, u32[]{:S(2)}, u32[]{:S(2)}) collective-permute-start(f16[128,1024]{1,0:T(8,128)(2,1)S(1)} %convert_element_type.65), channel_id=1, source_target_pairs={{0,2},{2,0},{1,3},{3,1},{4,6},{6,4},{5,7},{7,5},{8,10},{10,8},{9,1... | collective-permute-start | bytes 786440 | tf_op jit(solution)/shard_map/ppermute | solution.py:412
  54.6 1.7 %collective-permute-start.11 = (f32[64,128]{1,0:T(8,128)S(1)}, f32[64,128]{1,0:T(8,128)S(1)}, u32[]{:S(2)}, u32[]{:S(2)}) collective-permute-start(f32[64,128]{1,0:T(8,128)S(1)} %get-tuple-element.70), channel_id=1, source_target_pairs={{0,1},{1,0},{2,3},{3,2},{4,5},{5,4},{6,7},{7,6},{8,9},{9,8},{10,11... | collective-permute-start | bytes 98312 | tf_op jit(solution)/shard_map/ppermute | solution.py:412
  56.3 3.9 %collective-permute-start.12 = (f32[64,128]{1,0:T(8,128)S(1)}, f32[64,128]{1,0:T(8,128)S(1)}, u32[]{:S(2)}, u32[]{:S(2)}) collective-permute-start(f32[64,128]{1,0:T(8,128)S(1)} %add.31), channel_id=1, source_target_pairs={{0,2},{2,0},{1,3},{3,1},{4,6},{6,4},{5,7},{7,5},{8,10},{10,8},{9,1... | collective-permute-start | bytes 98312 | tf_op jit(solution)/shard_map/ppermute | solution.py:412
  60.2 18.9 %collective-permute-start.19 = (f16[128,3072]{1,0:T(8,128)(2,1)S(1)}, f16[128,3072]{1,0:T(8,128)(2,1)S(1)}, u32[]{:S(2)}, u32[]{:S(2)}) collective-permute-start(f16[128,3072]{1,0:T(8,128)(2,1)S(1)} %convert_element_type.64), channel_id=1, source_target_pairs={{0,2},{2,0},{1,3},{3,1},{4,6},{6,4},{5,7},{7,5},{8,10},{10,8},{9,1... | collective-permute-start | bytes 2359304 | tf_op jit(solution)/shard_map/ppermute | solution.py:412
  61.6 4.4 %collective-permute-start.14 = (f32[64,128]{1,0:T(8,128)S(1)}, f32[64,128]{1,0:T(8,128)S(1)}, u32[]{:S(2)}, u32[]{:S(2)}) collective-permute-start(f32[64,128]{1,0:T(8,128)S(1)} %add.32), channel_id=1, source_target_pairs={{0,4},{4,0},{8,12},{12,8},{1,5},{5,1},{9,13},{13,9},{2,6},{6,2},{1... | collective-permute-start | bytes 98312 | tf_op jit(solution)/shard_map/ppermute | solution.py:416
  62.5 5.5 %collective-permute-start.15 = (f32[64,128]{1,0:T(8,128)S(1)}, f32[64,128]{1,0:T(8,128)S(1)}, u32[]{:S(2)}, u32[]{:S(2)}) collective-permute-start(f32[64,128]{1,0:T(8,128)S(1)} %add.32), channel_id=1, source_target_pairs={{0,8},{4,12},{8,0},{12,4},{1,9},{5,13},{9,1},{13,5},{2,10},{6,14},... | collective-permute-start | bytes 98312 | tf_op jit(solution)/shard_map/ppermute | solution.py:416
  64.2 5.7 %collective-permute-start.16 = (f32[64,128]{1,0:T(8,128)S(1)}, f32[64,128]{1,0:T(8,128)S(1)}, u32[]{:S(2)}, u32[]{:S(2)}) collective-permute-start(f32[64,128]{1,0:T(8,128)S(1)} %add.32), channel_id=1, source_target_pairs={{0,12},{4,8},{8,4},{12,0},{1,13},{5,9},{9,5},{13,1},{2,14},{6,10},... | collective-permute-start | bytes 98312 | tf_op jit(solution)/shard_map/ppermute | solution.py:416
  69.9 1.3 %collective-permute-start.17 = (f32[64,128]{1,0:T(8,128)S(1)}, f32[64,128]{1,0:T(8,128)S(1)}, u32[]{:S(2)}, u32[]{:S(2)}) collective-permute-start(f32[64,128]{1,0:T(8,128)S(1)} %add_add_fusion.1.kept), channel_id=1, source_target_pairs={{0,1},{1,0},{2,3},{3,2},{4,5},{5,4},{6,7},{7,6},{8,9},{9,8},{10,11... | collective-permute-start | bytes 98312 | tf_op jit(solution)/shard_map/ppermute | solution.py:412
  76.3 1.3 %collective-permute-start.18 = (f32[64,512]{1,0:T(8,128)S(1)}, f32[64,512]{1,0:T(8,128)S(1)}, u32[]{:S(2)}, u32[]{:S(2)}) collective-permute-start(f32[64,512]{1,0:T(8,128)S(1)} %collective-permute-done.6.theirs), channel_id=1, source_target_pairs={{0,1},{1,0},{2,3},{3,2},{4,5},{5,4},{6,7},{7,6},{8,9},{9,8},{10,11... | collective-permute-start | bytes 393224 | tf_op jit(solution)/shard_map/ppermute | solution.py:412

commit v3 on v2

--- a/solution.py
+++ b/solution.py
@@ -368,22 +368,29 @@
     )(place, kept, got)
 
 
-def new_columns(place, weights, near, far):
+def new_columns(place, weights, near, far, left, got):
     rows = weights.shape[0]
-    sizes = [part.shape[1] for part in near + far]
-    half = sum(sizes) // 2
-    starts = [sum(sizes[:i]) % half for i in range(len(sizes))]
+    pieces, cuts = left
+    half = sum(part.shape[1] for part in near)
+    tasks = []
+    for flip, group in ((0, near), (1, far + [got])):
+        start = 0
+        for part in group:
+            tasks.append((flip, start, part.shape[1]))
+            start += part.shape[1]
 
     def kernel(place, weights, *refs):
-        parts, (out, whole, sems) = refs[:-3], refs[-3:]
+        refs, (out, whole, sems) = refs[:-3], refs[-3:]
+        parts, lefts, got = refs[: len(tasks) - 1], refs[len(tasks) - 1 : -1], refs[-1]
         high, low = split(weights[...])
         lhs = jnp.concatenate(
             [jnp.concatenate([high, high], axis=1), jnp.concatenate([low, low], axis=1)], axis=0
         )
         copies = []
-        for index, (start, size) in enumerate(zip(starts, sizes)):
-            value = jnp.dot(lhs, parts[index][...], preferred_element_type=F32)
-            side = place[0] if index < len(near) else 1 - place[0]
+        for index, (flip, start, size) in enumerate(tasks):
+            part = parts[index][...] if index < len(parts) else residual(lefts, cuts, got)
+            value = jnp.dot(lhs, part, preferred_element_type=F32)
+            side = 1 - place[0] if flip else place[0]
             at = pl.ds(pl.multiple_of(side * half + start, 128), size)
             whole[:, at] = value[:rows] + value[rows:]
             copies.append(pltpu.make_async_copy(whole.at[:, at], out.at[:, at], sems.at[index]))
@@ -393,19 +400,20 @@
 
     vmem = pl.BlockSpec(memory_space=pltpu.VMEM)
     hbm = pl.BlockSpec(memory_space=pltpu.HBM)
+    args = (weights, *near, *far, *pieces, got)
     return pl.pallas_call(
         kernel,
-        in_specs=[pl.BlockSpec(memory_space=pltpu.SMEM)] + [vmem] * (1 + len(sizes)),
+        in_specs=[pl.BlockSpec(memory_space=pltpu.SMEM)] + [vmem] * len(args),
         out_specs=hbm,
         out_shape=jax.ShapeDtypeStruct((rows, 2 * half), F32),
         scratch_shapes=[
             pltpu.VMEM((rows, 2 * half), F32),
-            pltpu.SemaphoreType.DMA((len(sizes),)),
+            pltpu.SemaphoreType.DMA((len(tasks),)),
         ],
         cost_estimate=COST,
         compiler_params=pltpu.CompilerParams(vmem_limit_bytes=16 << 20),
         name="new_basis",
-    )(place, weights, *near, *far)
+    )(place, *args)
 
 
 def swap(x, axis):
@@ -421,7 +429,7 @@
 
 
 NEAR = (8, 8, 8, 8)
-FAR = (8, 24)
+FAR = (8, 8, 16)
 
 
 def parted(total, shares):
@@ -465,19 +473,21 @@
     value, keep, send = gram_halves(place, overlap(left_near, far, near[-1]), got[-1], total)
     resids.append(value)
     gram = keep + swap(send, "sub")
+    gram, fits_back[0] = lax.optimization_barrier((gram, fits_back[0]))
     gram = gram + swap(gram, "pts")
     away = [residual_parts(overlap(left_far, near, far[0]), first_got)]
-    gram, away[0], *fits_back = lax.optimization_barrier((gram, away[0], *fits_back))
+    gram, away[0], *fits_back[1:] = lax.optimization_barrier((gram, away[0], *fits_back[1:]))
     away += [
         residual_parts(overlap(left_far, near, span), arrived(fit))
-        for span, fit in zip(far[1:], fits_back)
+        for span, fit in zip(far[1:-1], fits_back)
     ]
+    last = overlap(left_far, near, far[-1]), arrived(fits_back[-1])
     gram = sum_over(gram, "feat", feat)
     factor, weights = factorize(place, gram, swap(gram, "sub"), feats_total)
     weights, theirs = lax.optimization_barrier((weights, theirs))
     coefs = own_columns(place, own, theirs, swap(theirs, "sub"))
     coefs, away[-1] = lax.optimization_barrier((coefs, away[-1]))
-    new_basis = new_columns(place, weights, resids, away)
+    new_basis = new_columns(place, weights, resids, away, *last)
     return coefs.T, new_basis.T, factor
 
 

time: 82.1 us -> 81 us (0.987)
  waiting for transfers between devices: 31.4 us -> 29.2 us
    ppermute x6, waiting for transfers between devices: 9.85 us -> 7.42 us  [sum_over(): lax.ppermute(x, axis, [(i, i ^ m) for i in range(size)])]
    ppermute x13 -> x14, starting transfers between devices: 12 us -> 12.6 us  [swap(): return lax.ppermute(x, axis, [(0, 1), (1, 0)])]
    pallas_call x15 -> x16, Pallas kernels: 19 us -> 19.5 us  [call(): pl.pallas_call(kernel, in_specs=[smem] * scalars + [vmem] * (len(args) -...]
    ppermute x13 -> x14, waiting for transfers between devices: 21.5 us -> 21.7 us  [swap(): return lax.ppermute(x, axis, [(0, 1), (1, 0)])]
  transfers between devices with their start and end apart: 20 -> 21, of which waited for: 15 -> 15; matrix products, arithmetic and copies ran while one was open for 1% -> 1% of each run, Pallas kernels for 26% -> 27%
where the time goes in v3:
time: 81 us; the launch traced here: 80.8 us
  waiting for transfers between devices  29.2 us (36%)
  Pallas kernels  27.6 us (34%)
  starting transfers between devices  22.3 us (28%)
  between operations  1.09 us (1%)
    ppermute x14, waiting for transfers between devices, swap(): return lax.ppermute(x, axis, [(0, 1), (1, 0)])  21.7 us
    pallas_call x16, Pallas kernels, call(): pl.pallas_call(kernel, in_specs=[smem] * scalars + [vmem] * (len(args) -...  19.5 us
    ppermute x14, starting transfers between devices, swap(): return lax.ppermute(x, axis, [(0, 1), (1, 0)])  12.6 us
    ppermute x6, starting transfers between devices, sum_over(): lax.ppermute(x, axis, [(i, i ^ m) for i in range(size)])  8.84 us
    ppermute x6, waiting for transfers between devices, sum_over(): lax.ppermute(x, axis, [(i, i ^ m) for i in range(size)])  7.42 us
    pallas_call x1, Pallas kernels, own_coefs(): pl.pallas_call(kernel, in_specs=[hbm] * 4, out_specs=[vmem] * 5, out_shap...  5.91 us
    pallas_call x1, Pallas kernels, new_columns(): pl.pallas_call(kernel, in_specs=[pl.BlockSpec(memory_space=pltpu.SMEM)] +...  2.2 us
  transfers between devices with their start and end apart: 21, of which 15 were waited for; matrix products, arithmetic and copies ran while one was open for 1% of the time, Pallas kernels for 27%

profile of v3, /device:TPU:0, one launch (start us, length us, event | category | flops | bytes accessed | tf_op | source)
XLA Modules:
  0.0 80.8 jit_solution(14032830456903007001)
XLA Ops:
  0.6 3.0 %collective-permute-start = (bf16[64,256]{1,0:T(8,128)(2,1)}, bf16[64,256]{1,0:T(8,128)(2,1)S(1)}, u32[]{:S(2)}, u32[]{:S(2)}) collective-permute-start(bf16[64,256]{1,0:T(8,128)(2,1)} %points.1), channel_id=1, source_target_pairs={{0,2},{2,0},{1,3},{3,1},{4,6},{6,4},{5,7},{7,5},{8,10},{10,8},{9,1... | collective-permute-start | bytes 98312 | tf_op jit(solution)/shard_map/ppermute | solution.py:420
  3.7 5.9 %own_coefs.1 = (f32[64,8192]{1,0:T(8,128)S(1)}, f32[64,512]{1,0:T(8,128)S(1)}, bf16[256,8192]{1,0:T(8,128)(2,1)S(1)}, f32[1,8192]{1,0:T(1,128)S(1)}, bf16[8192,512]{1,0:T(8,128)(2,1)S(1)}) custom-call(bf16[64,256]{1,0:T(8,128)(2,1)} %points.1, bf16[256,8192]{1,0:T(8,128)(2,1)} %freqs.1, f32[1,8192]{1,0:T(1,128)} %bitcast.7, bf16[8192,512]{1,0:T(8,128)(2,1)} %basis.1), custom_call_target="tpu_custom_call" | custom-call | flops 1000 | bytes 1000 | tf_op jit(solution)/shard_map/own_coefs/pallas_call | solution.py:114
  9.6 3.4 %other_coefs.1 = (f32[64,8192]{1,0:T(8,128)S(1)}, f32[64,512]{1,0:T(8,128)S(1)}, f32[64,512]{1,0:T(8,128)S(1)}) custom-call(s32[2]{0:T(128)S(1)} %pad_add_fusion.place, bf16[64,256]{1,0:T(8,128)(2,1)S(1)} %collective-permute-done.points, bf16[256,8192]{1,0:T(8,128)(2,1)S(1)} %get-tuple-element.52.freqs, f32[1,8192]{1,0:T(1,128)S(1)} %get-tuple-element.53.phases, ...), custom_call_target="tpu_custom_call" | custom-call | flops 1000 | bytes 1000 | tf_op jit(solution)/shard_map/other_coefs/pallas_call | solution.py:54
  13.1 1.3 %collective-permute-done.1 = f32[64,512]{1,0:T(8,128)S(1)} collective-permute-done((f32[64,512]{1,0:T(8,128)S(1)}, f32[64,512]{1,0:T(8,128)S(1)}, u32[]{:S(2)}, u32[]{:S(2)}) %collective-permute-start.1) | collective-permute-done | bytes 131104 | tf_op jit(solution)/shard_map/ppermute | solution.py:420
  14.5 3.7 %collective-permute-start.4 = (f16[64,512]{1,0:T(8,128)(2,1)S(1)}, f16[64,512]{1,0:T(8,128)(2,1)S(1)}, u32[]{:S(2)}, u32[]{:S(2)}) collective-permute-start(f16[64,512]{1,0:T(8,128)(2,1)S(1)} %add_convert_fusion), channel_id=1, source_target_pairs={{0,12},{4,8},{8,4},{12,0},{1,13},{5,9},{9,5},{13,1},{2,14},{6,10},... | collective-permute-start | bytes 196616 | tf_op jit(solution)/shard_map/ppermute | solution.py:424
  18.2 0.8 collective-permute-start.2
  18.9 1.9 %collective-permute-done.4 = f16[64,512]{1,0:T(8,128)(2,1)S(1)} collective-permute-done((f16[64,512]{1,0:T(8,128)(2,1)S(1)}, f16[64,512]{1,0:T(8,128)(2,1)S(1)}, u32[]{:S(2)}, u32[]{:S(2)}) %collective-permute-start.4) | collective-permute-done | bytes 65568 | tf_op jit(solution)/shard_map/ppermute | solution.py:424
  20.8 3.2 %collective-permute-done.3 = f16[64,512]{1,0:T(8,128)(2,1)S(1)} collective-permute-done((f16[64,512]{1,0:T(8,128)(2,1)S(1)}, f16[64,512]{1,0:T(8,128)(2,1)S(1)}, u32[]{:S(2)}, u32[]{:S(2)}) %collective-permute-start.3) | collective-permute-done | bytes 65568 | tf_op jit(solution)/shard_map/ppermute | solution.py:424
  24.2 0.8 %collective-permute-start.6 = (f32[64,512]{1,0:T(8,128)S(1)}, f32[64,512]{1,0:T(8,128)S(1)}, u32[]{:S(2)}, u32[]{:S(2)}) collective-permute-start(f32[64,512]{1,0:T(8,128)S(1)} %add_add_fusion.kept), channel_id=1, source_target_pairs={{1,3},{3,1},{5,7},{7,5},{9,11},{11,9},{13,15},{15,13},{17,19},{19,... | collective-permute-start | bytes 393224 | tf_op jit(solution)/shard_map/ppermute | solution.py:452
  25.0 0.5 collective-permute-done.5.got
  25.5 1.0 %first_fit.1 = (f32[128,1024]{1,0:T(8,128)S(1)}, f32[128,1024]{1,0:T(8,128)S(1)}, f32[64,512]{1,0:T(8,128)S(1)}, bf16[256,512]{1,0:T(8,128)(2,1)S(1)}) custom-call(s32[2]{0:T(128)S(1)} %pad_add_fusion.place, f32[64,512]{1,0:T(8,128)S(1)} %add_add_fusion.kept, f32[64,512]{1,0:T(8,128)S(1)} %collective-permute-done.5.got, ...), custom_call_target="tpu_custom_call" | custom-call | flops 1000 | bytes 1000 | tf_op jit(solution)/shard_map/first_fit/pallas_call | solution.py:54
  26.6 0.6 collective-permute-start.10
  27.2 1.0 %fit.10 = (f32[128,1024]{1,0:T(8,128)S(1)}, f32[128,1024]{1,0:T(8,128)S(1)}) custom-call(s32[2]{0:T(128)S(1)} %pad_add_fusion.place, bf16[256,512]{1,0:T(8,128)(2,1)S(1)} %get-tuple-element.62.parts, f32[64,8192]{1,0:T(8,128)S(1)} %get-tuple-element.58.feats_a, f32[64,8192]{1,0:T(8,128)S(1)} %get-tuple-element.59.feats_b, ...), custom_call_target="tpu_custom_call" | custom-call | flops 1000 | bytes 1000 | tf_op jit(solution)/shard_map/fit/pallas_call | solution.py:54
  28.2 1.5 %collective-permute-start.9 = (f16[128,1024]{1,0:T(8,128)(2,1)S(1)}, f16[128,1024]{1,0:T(8,128)(2,1)S(1)}, u32[]{:S(2)}, u32[]{:S(2)}) collective-permute-start(f16[128,1024]{1,0:T(8,128)(2,1)S(1)} %convert_element_type.66), channel_id=1, source_target_pairs={{0,2},{2,0},{1,3},{3,1},{4,6},{6,4},{5,7},{7,5},{8,10},{10,8},{9,1... | collective-permute-start | bytes 786440 | tf_op jit(solution)/shard_map/ppermute | solution.py:420
  29.8 1.0 %fit.8 = (f32[128,1024]{1,0:T(8,128)S(1)}, f32[128,1024]{1,0:T(8,128)S(1)}) custom-call(s32[2]{0:T(128)S(1)} %pad_add_fusion.place, bf16[256,512]{1,0:T(8,128)(2,1)S(1)} %get-tuple-element.62.parts, f32[64,8192]{1,0:T(8,128)S(1)} %get-tuple-element.58.feats_a, f32[64,8192]{1,0:T(8,128)S(1)} %get-tuple-element.59.feats_b, ...), custom_call_target="tpu_custom_call" | custom-call | flops 1000 | bytes 1000 | tf_op jit(solution)/shard_map/fit/pallas_call | solution.py:54
  30.8 0.6 collective-permute-start.8
  31.5 1.0 %fit.7 = (f32[128,1024]{1,0:T(8,128)S(1)}, f32[128,1024]{1,0:T(8,128)S(1)}) custom-call(s32[2]{0:T(128)S(1)} %pad_add_fusion.place, bf16[256,512]{1,0:T(8,128)(2,1)S(1)} %get-tuple-element.62.parts, f32[64,8192]{1,0:T(8,128)S(1)} %get-tuple-element.58.feats_a, f32[64,8192]{1,0:T(8,128)S(1)} %get-tuple-element.59.feats_b, ...), custom_call_target="tpu_custom_call" | custom-call | flops 1000 | bytes 1000 | tf_op jit(solution)/shard_map/fit/pallas_call | solution.py:54
  32.5 1.5 %collective-permute-start.7 = (f16[128,1024]{1,0:T(8,128)(2,1)S(1)}, f16[128,1024]{1,0:T(8,128)(2,1)S(1)}, u32[]{:S(2)}, u32[]{:S(2)}) collective-permute-start(f16[128,1024]{1,0:T(8,128)(2,1)S(1)} %convert_element_type.62), channel_id=1, source_target_pairs={{0,2},{2,0},{1,3},{3,1},{4,6},{6,4},{5,7},{7,5},{8,10},{10,8},{9,1... | collective-permute-start | bytes 786440 | tf_op jit(solution)/shard_map/ppermute | solution.py:420
  34.1 1.0 %fit.11 = (f32[128,1024]{1,0:T(8,128)S(1)}, f32[128,1024]{1,0:T(8,128)S(1)}) custom-call(s32[2]{0:T(128)S(1)} %pad_add_fusion.place, bf16[256,512]{1,0:T(8,128)(2,1)S(1)} %get-tuple-element.62.parts, f32[64,8192]{1,0:T(8,128)S(1)} %get-tuple-element.58.feats_a, f32[64,8192]{1,0:T(8,128)S(1)} %get-tuple-element.59.feats_b, ...), custom_call_target="tpu_custom_call" | custom-call | flops 1000 | bytes 1000 | tf_op jit(solution)/shard_map/fit/pallas_call | solution.py:54
  35.1 0.6 collective-permute-start.13
  35.7 1.0 %fit.9 = (f32[128,1024]{1,0:T(8,128)S(1)}, f32[128,1024]{1,0:T(8,128)S(1)}) custom-call(s32[2]{0:T(128)S(1)} %pad_add_fusion.place, bf16[256,512]{1,0:T(8,128)(2,1)S(1)} %get-tuple-element.62.parts, f32[64,8192]{1,0:T(8,128)S(1)} %get-tuple-element.58.feats_a, f32[64,8192]{1,0:T(8,128)S(1)} %get-tuple-element.59.feats_b, ...), custom_call_target="tpu_custom_call" | custom-call | flops 1000 | bytes 1000 | tf_op jit(solution)/shard_map/fit/pallas_call | solution.py:54
  36.8 1.3 %fit.6 = (f32[128,2048]{1,0:T(8,128)S(1)}, f32[128,2048]{1,0:T(8,128)S(1)}) custom-call(s32[2]{0:T(128)S(1)} %pad_add_fusion.place, bf16[256,512]{1,0:T(8,128)(2,1)S(1)} %get-tuple-element.62.parts, f32[64,8192]{1,0:T(8,128)S(1)} %get-tuple-element.58.feats_a, f32[64,8192]{1,0:T(8,128)S(1)} %get-tuple-element.59.feats_b, ...), custom_call_target="tpu_custom_call" | custom-call | flops 1000 | bytes 1000 | tf_op jit(solution)/shard_map/fit/pallas_call | solution.py:54
  38.3 0.4 gram.3
  38.6 2.8 %collective-permute-done.9 = f16[128,1024]{1,0:T(8,128)(2,1)S(1)} collective-permute-done((f16[128,1024]{1,0:T(8,128)(2,1)S(1)}, f16[128,1024]{1,0:T(8,128)(2,1)S(1)}, u32[]{:S(2)}, u32[]{:S(2)}) %collective-permute-start.9) | collective-permute-done | bytes 262176 | tf_op jit(solution)/shard_map/ppermute | solution.py:420
  41.5 0.4 gram.4
  41.8 5.2 %collective-permute-done.8 = f16[128,1024]{1,0:T(8,128)(2,1)S(1)} collective-permute-done((f16[128,1024]{1,0:T(8,128)(2,1)S(1)}, f16[128,1024]{1,0:T(8,128)(2,1)S(1)}, u32[]{:S(2)}, u32[]{:S(2)}) %collective-permute-start.8) | collective-permute-done | bytes 262176 | tf_op jit(solution)/shard_map/ppermute | solution.py:420
  47.1 0.4 gram.5
  47.5 5.2 %collective-permute-done.7 = f16[128,1024]{1,0:T(8,128)(2,1)S(1)} collective-permute-done((f16[128,1024]{1,0:T(8,128)(2,1)S(1)}, f16[128,1024]{1,0:T(8,128)(2,1)S(1)}, u32[]{:S(2)}, u32[]{:S(2)}) %collective-permute-start.7) | collective-permute-done | bytes 262176 | tf_op jit(solution)/shard_map/ppermute | solution.py:420
  52.7 1.0 %gram_halves.1 = (bf16[256,1024]{1,0:T(8,128)(2,1)S(1)}, f32[64,128]{1,0:T(8,128)S(1)}, f32[64,128]{1,0:T(8,128)S(1)}) custom-call(s32[2]{0:T(128)S(1)} %pad_add_fusion.place, f32[128,2048]{1,0:T(8,128)S(1)} %get-tuple-element.63.refs_0_, f32[128,1024]{1,0:T(8,128)S(1)} %convert_element_type.63.refs_1_, f32[256,256]{1,0:T(8,128)S(1)} %get-tuple-element.75.refs_2_), custom_call_target="tpu_custom_call" | custom-call | flops 1000 | bytes 1000 | tf_op jit(solution)/shard_map/gram_halves/pallas_call | solution.py:54
  53.7 0.9 %collective-permute-start.11 = (f32[64,128]{1,0:T(8,128)S(1)}, f32[64,128]{1,0:T(8,128)S(1)}, u32[]{:S(2)}, u32[]{:S(2)}) collective-permute-start(f32[64,128]{1,0:T(8,128)S(1)} %get-tuple-element.77), channel_id=1, source_target_pairs={{0,1},{1,0},{2,3},{3,2},{4,5},{5,4},{6,7},{7,6},{8,9},{9,8},{10,11... | collective-permute-start | bytes 98312 | tf_op jit(solution)/shard_map/ppermute | solution.py:420
  54.6 0.9 %collective-permute-done.11 = f32[64,128]{1,0:T(8,128)S(1)} collective-permute-done((f32[64,128]{1,0:T(8,128)S(1)}, f32[64,128]{1,0:T(8,128)S(1)}, u32[]{:S(2)}, u32[]{:S(2)}) %collective-permute-start.11) | collective-permute-done | bytes 32800 | tf_op jit(solution)/shard_map/ppermute | solution.py:420
  55.4 1.4 %collective-permute-start.12 = (f32[64,128]{1,0:T(8,128)S(1)}, f32[64,128]{1,0:T(8,128)S(1)}, u32[]{:S(2)}, u32[]{:S(2)}) collective-permute-start(f32[64,128]{1,0:T(8,128)S(1)} %add.31), channel_id=1, source_target_pairs={{0,2},{2,0},{1,3},{3,1},{4,6},{6,4},{5,7},{7,5},{8,10},{10,8},{9,1... | collective-permute-start | bytes 98312 | tf_op jit(solution)/shard_map/ppermute | solution.py:420
  56.8 1.4 %collective-permute-done.13 = f16[128,1024]{1,0:T(8,128)(2,1)S(1)} collective-permute-done((f16[128,1024]{1,0:T(8,128)(2,1)S(1)}, f16[128,1024]{1,0:T(8,128)(2,1)S(1)}, u32[]{:S(2)}, u32[]{:S(2)}) %collective-permute-start.13) | collective-permute-done | bytes 262176 | tf_op jit(solution)/shard_map/ppermute | solution.py:420
  58.4 0.9 %collective-permute-done.12 = f32[64,128]{1,0:T(8,128)S(1)} collective-permute-done((f32[64,128]{1,0:T(8,128)S(1)}, f32[64,128]{1,0:T(8,128)S(1)}, u32[]{:S(2)}, u32[]{:S(2)}) %collective-permute-start.12) | collective-permute-done | bytes 32800 | tf_op jit(solution)/shard_map/ppermute | solution.py:420
  59.3 1.4 %collective-permute-start.20 = (f16[128,2048]{1,0:T(8,128)(2,1)S(1)}, f16[128,2048]{1,0:T(8,128)(2,1)S(1)}, u32[]{:S(2)}, u32[]{:S(2)}) collective-permute-start(f16[128,2048]{1,0:T(8,128)(2,1)S(1)} %convert_element_type.71), channel_id=1, source_target_pairs={{0,2},{2,0},{1,3},{3,1},{4,6},{6,4},{5,7},{7,5},{8,10},{10,8},{9,1... | collective-permute-start | bytes 1572872 | tf_op jit(solution)/shard_map/ppermute | solution.py:420
  60.8 2.5 %collective-permute-start.16 = (f32[64,128]{1,0:T(8,128)S(1)}, f32[64,128]{1,0:T(8,128)S(1)}, u32[]{:S(2)}, u32[]{:S(2)}) collective-permute-start(f32[64,128]{1,0:T(8,128)S(1)} %add.32), channel_id=1, source_target_pairs={{0,12},{4,8},{8,4},{12,0},{1,13},{5,9},{9,5},{13,1},{2,14},{6,10},... | collective-permute-start | bytes 98312 | tf_op jit(solution)/shard_map/ppermute | solution.py:424
  63.3 0.1 collective-permute-start.15
  63.4 1.8 %collective-permute-start.14 = (f32[64,128]{1,0:T(8,128)S(1)}, f32[64,128]{1,0:T(8,128)S(1)}, u32[]{:S(2)}, u32[]{:S(2)}) collective-permute-start(f32[64,128]{1,0:T(8,128)S(1)} %add.32), channel_id=1, source_target_pairs={{0,4},{4,0},{8,12},{12,8},{1,5},{5,1},{9,13},{13,9},{2,6},{6,2},{1... | collective-permute-start | bytes 98312 | tf_op jit(solution)/shard_map/ppermute | solution.py:424
  65.2 0.6 collective-permute-start.19
  65.8 0.7 collective-permute-done.16
  66.5 1.6 %collective-permute-done.15 = f32[64,128]{1,0:T(8,128)S(1)} collective-permute-done((f32[64,128]{1,0:T(8,128)S(1)}, f32[64,128]{1,0:T(8,128)S(1)}, u32[]{:S(2)}, u32[]{:S(2)}) %collective-permute-start.15) | collective-permute-done | bytes 32800 | tf_op jit(solution)/shard_map/ppermute | solution.py:424
  68.2 1.2 %collective-permute-done.17.got = f32[64,128]{1,0:T(8,128)S(1)} collective-permute-done((f32[64,128]{1,0:T(8,128)S(1)}, f32[64,128]{1,0:T(8,128)S(1)}, u32[]{:S(2)}, u32[]{:S(2)}) %collective-permute-start.17) | collective-permute-done | bytes 32800 | tf_op jit(solution)/shard_map/ppermute | solution.py:420
  69.4 5.1 %factorize.1 = (f32[64,128]{1,0:T(8,128)}, f32[64,128]{1,0:T(8,128)S(1)}) custom-call(s32[2]{0:T(128)S(1)} %pad_add_fusion.place, f32[64,128]{1,0:T(8,128)S(1)} %add_add_fusion.1.kept, f32[64,128]{1,0:T(8,128)S(1)} %collective-permute-done.17.got), custom_call_target="tpu_custom_call" | custom-call | flops 1000 | bytes 20000000 | tf_op jit(solution)/shard_map/factorize/pallas_call | solution.py:54
  74.5 0.2 collective-permute-start.18
  74.7 1.2 %collective-permute-done.18.passed = f32[64,512]{1,0:T(8,128)S(1)} collective-permute-done((f32[64,512]{1,0:T(8,128)S(1)}, f32[64,512]{1,0:T(8,128)S(1)}, u32[]{:S(2)}, u32[]{:S(2)}) %collective-permute-start.18) | collective-permute-done | bytes 131104 | tf_op jit(solution)/shard_map/ppermute | solution.py:420
  75.8 1.3 %own_columns.1 = f32[64,1024]{1,0:T(8,128)} custom-call(s32[2]{0:T(128)S(1)} %pad_add_fusion.place, f32[64,512]{1,0:T(8,128)S(1)} %get-tuple-element.60.own, f32[64,512]{1,0:T(8,128)S(1)} %collective-permute-done.6.theirs, f32[64,512]{1,0:T(8,128)S(1)} %collective-permute-done.18.passed), custom_call_target="tpu_custom_call" | custom-call | flops 1000 | bytes 1000 | tf_op jit(solution)/shard_map/own_columns/pallas_call | solution.py:54
  77.1 1.1 %collective-permute-done.19 = f16[128,1024]{1,0:T(8,128)(2,1)S(1)} collective-permute-done((f16[128,1024]{1,0:T(8,128)(2,1)S(1)}, f16[128,1024]{1,0:T(8,128)(2,1)S(1)}, u32[]{:S(2)}, u32[]{:S(2)}) %collective-permute-start.19) | collective-permute-done | bytes 262176 | tf_op jit(solution)/shard_map/ppermute | solution.py:420
  78.5 2.2 %new_basis.1 = f32[64,8192]{1,0:T(8,128)} custom-call(s32[2]{0:T(128)S(1)} %pad_add_fusion.place, f32[64,128]{1,0:T(8,128)S(1)} %get-tuple-element.90.weights, bf16[256,1024]{1,0:T(8,128)(2,1)S(1)} %get-tuple-element.91.refs_0_, bf16[256,1024]{1,0:T(8,128)(2,1)S(1)} %get-tuple-element.92.refs_1_, bf16[256,1024]{1,0:T(8,128)(2,1)S(1)} %get-tuple-element.93.refs_2_, ...), custom_call_target="tpu_custom_call" | custom-call | flops 1000 | bytes 1000 | tf_op jit(solution)/shard_map/new_basis/pallas_call | solution.py:404
  (32 shorter events, 1.1 us)
Async XLA Ops:
  0.6 9.0 %collective-permute-start = (bf16[64,256]{1,0:T(8,128)(2,1)}, bf16[64,256]{1,0:T(8,128)(2,1)S(1)}, u32[]{:S(2)}, u32[]{:S(2)}) collective-permute-start(bf16[64,256]{1,0:T(8,128)(2,1)} %points.1), channel_id=1, source_target_pairs={{0,2},{2,0},{1,3},{3,1},{4,6},{6,4},{5,7},{7,5},{8,10},{10,8},{9,1... | collective-permute-start | bytes 98312 | tf_op jit(solution)/shard_map/ppermute | solution.py:420
  13.0 1.4 %collective-permute-start.1 = (f32[64,512]{1,0:T(8,128)S(1)}, f32[64,512]{1,0:T(8,128)S(1)}, u32[]{:S(2)}, u32[]{:S(2)}) collective-permute-start(f32[64,512]{1,0:T(8,128)S(1)} %get-tuple-element.57), channel_id=1, source_target_pairs={{0,1},{1,0},{2,3},{3,2},{4,5},{5,4},{6,7},{7,6},{8,9},{9,8},{10,11... | collective-permute-start | bytes 393224 | tf_op jit(solution)/shard_map/ppermute | solution.py:420
  14.5 6.4 %collective-permute-start.4 = (f16[64,512]{1,0:T(8,128)(2,1)S(1)}, f16[64,512]{1,0:T(8,128)(2,1)S(1)}, u32[]{:S(2)}, u32[]{:S(2)}) collective-permute-start(f16[64,512]{1,0:T(8,128)(2,1)S(1)} %add_convert_fusion), channel_id=1, source_target_pairs={{0,12},{4,8},{8,4},{12,0},{1,13},{5,9},{9,5},{13,1},{2,14},{6,10},... | collective-permute-start | bytes 196616 | tf_op jit(solution)/shard_map/ppermute | solution.py:424
  18.2 5.9 %collective-permute-start.3 = (f16[64,512]{1,0:T(8,128)(2,1)S(1)}, f16[64,512]{1,0:T(8,128)(2,1)S(1)}, u32[]{:S(2)}, u32[]{:S(2)}) collective-permute-start(f16[64,512]{1,0:T(8,128)(2,1)S(1)} %add_convert_fusion), channel_id=1, source_target_pairs={{0,8},{4,12},{8,0},{12,4},{1,9},{5,13},{9,1},{13,5},{2,10},{6,14},... | collective-permute-start | bytes 196616 | tf_op jit(solution)/shard_map/ppermute | solution.py:424
  18.2 5.9 %collective-permute-start.2 = (f16[64,512]{1,0:T(8,128)(2,1)S(1)}, f16[64,512]{1,0:T(8,128)(2,1)S(1)}, u32[]{:S(2)}, u32[]{:S(2)}) collective-permute-start(f16[64,512]{1,0:T(8,128)(2,1)S(1)} %add_convert_fusion), channel_id=1, source_target_pairs={{0,4},{4,0},{8,12},{12,8},{1,5},{5,1},{9,13},{13,9},{2,6},{6,2},{1... | collective-permute-start | bytes 196616 | tf_op jit(solution)/shard_map/ppermute | solution.py:424
  24.1 1.4 %collective-permute-start.5 = (f32[64,512]{1,0:T(8,128)S(1)}, f32[64,512]{1,0:T(8,128)S(1)}, u32[]{:S(2)}, u32[]{:S(2)}) collective-permute-start(f32[64,512]{1,0:T(8,128)S(1)} %add_add_fusion.kept), channel_id=1, source_target_pairs={{0,1},{1,0},{2,3},{3,2},{4,5},{5,4},{6,7},{7,6},{8,9},{9,8},{10,11... | collective-permute-start | bytes 393224 | tf_op jit(solution)/shard_map/ppermute | solution.py:420
  24.2 9.9 %collective-permute-start.6 = (f32[64,512]{1,0:T(8,128)S(1)}, f32[64,512]{1,0:T(8,128)S(1)}, u32[]{:S(2)}, u32[]{:S(2)}) collective-permute-start(f32[64,512]{1,0:T(8,128)S(1)} %add_add_fusion.kept), channel_id=1, source_target_pairs={{1,3},{3,1},{5,7},{7,5},{9,11},{11,9},{13,15},{15,13},{17,19},{19,... | collective-permute-start | bytes 393224 | tf_op jit(solution)/shard_map/ppermute | solution.py:452
  26.6 11.6 %collective-permute-start.10 = (f16[128,1024]{1,0:T(8,128)(2,1)S(1)}, f16[128,1024]{1,0:T(8,128)(2,1)S(1)}, u32[]{:S(2)}, u32[]{:S(2)}) collective-permute-start(f16[128,1024]{1,0:T(8,128)(2,1)S(1)} %convert_element_type.68), channel_id=1, source_target_pairs={{0,2},{2,0},{1,3},{3,1},{4,6},{6,4},{5,7},{7,5},{8,10},{10,8},{9,1... | collective-permute-start | bytes 786440 | tf_op jit(solution)/shard_map/ppermute | solution.py:420
  28.2 13.2 %collective-permute-start.9 = (f16[128,1024]{1,0:T(8,128)(2,1)S(1)}, f16[128,1024]{1,0:T(8,128)(2,1)S(1)}, u32[]{:S(2)}, u32[]{:S(2)}) collective-permute-start(f16[128,1024]{1,0:T(8,128)(2,1)S(1)} %convert_element_type.66), channel_id=1, source_target_pairs={{0,2},{2,0},{1,3},{3,1},{4,6},{6,4},{5,7},{7,5},{8,10},{10,8},{9,1... | collective-permute-start | bytes 786440 | tf_op jit(solution)/shard_map/ppermute | solution.py:420
  30.8 16.2 %collective-permute-start.8 = (f16[128,1024]{1,0:T(8,128)(2,1)S(1)}, f16[128,1024]{1,0:T(8,128)(2,1)S(1)}, u32[]{:S(2)}, u32[]{:S(2)}) collective-permute-start(f16[128,1024]{1,0:T(8,128)(2,1)S(1)} %convert_element_type.64), channel_id=1, source_target_pairs={{0,2},{2,0},{1,3},{3,1},{4,6},{6,4},{5,7},{7,5},{8,10},{10,8},{9,1... | collective-permute-start | bytes 786440 | tf_op jit(solution)/shard_map/ppermute | solution.py:420
  32.5 20.1 %collective-permute-start.7 = (f16[128,1024]{1,0:T(8,128)(2,1)S(1)}, f16[128,1024]{1,0:T(8,128)(2,1)S(1)}, u32[]{:S(2)}, u32[]{:S(2)}) collective-permute-start(f16[128,1024]{1,0:T(8,128)(2,1)S(1)} %convert_element_type.62), channel_id=1, source_target_pairs={{0,2},{2,0},{1,3},{3,1},{4,6},{6,4},{5,7},{7,5},{8,10},{10,8},{9,1... | collective-permute-start | bytes 786440 | tf_op jit(solution)/shard_map/ppermute | solution.py:420
  35.1 23.2 %collective-permute-start.13 = (f16[128,1024]{1,0:T(8,128)(2,1)S(1)}, f16[128,1024]{1,0:T(8,128)(2,1)S(1)}, u32[]{:S(2)}, u32[]{:S(2)}) collective-permute-start(f16[128,1024]{1,0:T(8,128)(2,1)S(1)} %convert_element_type.72), channel_id=1, source_target_pairs={{0,2},{2,0},{1,3},{3,1},{4,6},{6,4},{5,7},{7,5},{8,10},{10,8},{9,1... | collective-permute-start | bytes 786440 | tf_op jit(solution)/shard_map/ppermute | solution.py:420
  53.7 1.7 %collective-permute-start.11 = (f32[64,128]{1,0:T(8,128)S(1)}, f32[64,128]{1,0:T(8,128)S(1)}, u32[]{:S(2)}, u32[]{:S(2)}) collective-permute-start(f32[64,128]{1,0:T(8,128)S(1)} %get-tuple-element.77), channel_id=1, source_target_pairs={{0,1},{1,0},{2,3},{3,2},{4,5},{5,4},{6,7},{7,6},{8,9},{9,8},{10,11... | collective-permute-start | bytes 98312 | tf_op jit(solution)/shard_map/ppermute | solution.py:420
  55.4 3.9 %collective-permute-start.12 = (f32[64,128]{1,0:T(8,128)S(1)}, f32[64,128]{1,0:T(8,128)S(1)}, u32[]{:S(2)}, u32[]{:S(2)}) collective-permute-start(f32[64,128]{1,0:T(8,128)S(1)} %add.31), channel_id=1, source_target_pairs={{0,2},{2,0},{1,3},{3,1},{4,6},{6,4},{5,7},{7,5},{8,10},{10,8},{9,1... | collective-permute-start | bytes 98312 | tf_op jit(solution)/shard_map/ppermute | solution.py:420
  59.3 19.0 %collective-permute-start.20 = (f16[128,2048]{1,0:T(8,128)(2,1)S(1)}, f16[128,2048]{1,0:T(8,128)(2,1)S(1)}, u32[]{:S(2)}, u32[]{:S(2)}) collective-permute-start(f16[128,2048]{1,0:T(8,128)(2,1)S(1)} %convert_element_type.71), channel_id=1, source_target_pairs={{0,2},{2,0},{1,3},{3,1},{4,6},{6,4},{5,7},{7,5},{8,10},{10,8},{9,1... | collective-permute-start | bytes 1572872 | tf_op jit(solution)/shard_map/ppermute | solution.py:420
  60.8 5.7 %collective-permute-start.16 = (f32[64,128]{1,0:T(8,128)S(1)}, f32[64,128]{1,0:T(8,128)S(1)}, u32[]{:S(2)}, u32[]{:S(2)}) collective-permute-start(f32[64,128]{1,0:T(8,128)S(1)} %add.32), channel_id=1, source_target_pairs={{0,12},{4,8},{8,4},{12,0},{1,13},{5,9},{9,5},{13,1},{2,14},{6,10},... | collective-permute-start | bytes 98312 | tf_op jit(solution)/shard_map/ppermute | solution.py:424
  63.3 4.8 %collective-permute-start.15 = (f32[64,128]{1,0:T(8,128)S(1)}, f32[64,128]{1,0:T(8,128)S(1)}, u32[]{:S(2)}, u32[]{:S(2)}) collective-permute-start(f32[64,128]{1,0:T(8,128)S(1)} %add.32), channel_id=1, source_target_pairs={{0,8},{4,12},{8,0},{12,4},{1,9},{5,13},{9,1},{13,5},{2,10},{6,14},... | collective-permute-start | bytes 98312 | tf_op jit(solution)/shard_map/ppermute | solution.py:424
  63.4 4.7 %collective-permute-start.14 = (f32[64,128]{1,0:T(8,128)S(1)}, f32[64,128]{1,0:T(8,128)S(1)}, u32[]{:S(2)}, u32[]{:S(2)}) collective-permute-start(f32[64,128]{1,0:T(8,128)S(1)} %add.32), channel_id=1, source_target_pairs={{0,4},{4,0},{8,12},{12,8},{1,5},{5,1},{9,13},{13,9},{2,6},{6,2},{1... | collective-permute-start | bytes 98312 | tf_op jit(solution)/shard_map/ppermute | solution.py:424
  65.2 13.1 %collective-permute-start.19 = (f16[128,1024]{1,0:T(8,128)(2,1)S(1)}, f16[128,1024]{1,0:T(8,128)(2,1)S(1)}, u32[]{:S(2)}, u32[]{:S(2)}) collective-permute-start(f16[128,1024]{1,0:T(8,128)(2,1)S(1)} %convert_element_type.70), channel_id=1, source_target_pairs={{0,2},{2,0},{1,3},{3,1},{4,6},{6,4},{5,7},{7,5},{8,10},{10,8},{9,1... | collective-permute-start | bytes 786440 | tf_op jit(solution)/shard_map/ppermute | solution.py:420
  68.1 1.3 %collective-permute-start.17 = (f32[64,128]{1,0:T(8,128)S(1)}, f32[64,128]{1,0:T(8,128)S(1)}, u32[]{:S(2)}, u32[]{:S(2)}) collective-permute-start(f32[64,128]{1,0:T(8,128)S(1)} %add_add_fusion.1.kept), channel_id=1, source_target_pairs={{0,1},{1,0},{2,3},{3,2},{4,5},{5,4},{6,7},{7,6},{8,9},{9,8},{10,11... | collective-permute-start | bytes 98312 | tf_op jit(solution)/shard_map/ppermute | solution.py:420
  74.5 1.3 %collective-permute-start.18 = (f32[64,512]{1,0:T(8,128)S(1)}, f32[64,512]{1,0:T(8,128)S(1)}, u32[]{:S(2)}, u32[]{:S(2)}) collective-permute-start(f32[64,512]{1,0:T(8,128)S(1)} %collective-permute-done.6.theirs), channel_id=1, source_target_pairs={{0,1},{1,0},{2,3},{3,2},{4,5},{5,4},{6,7},{7,6},{8,9},{9,8},{10,11... | collective-permute-start | bytes 393224 | tf_op jit(solution)/shard_map/ppermute | solution.py:420

commit v4 on v3

--- a/solution.py
+++ b/solution.py
@@ -224,6 +224,18 @@
 def residual(refs, cuts, got):
     left = [ref[:, low:high] for ref, (low, high) in zip(refs, cuts)]
     return halves(jnp.concatenate(left, axis=1) - got[...])
+
+
+def residual_span(refs, cuts, got, start, size):
+    spans, at = [], 0
+    for low, high in cuts:
+        spans.append((at, high - low))
+        at += high - low
+    index, inner = overlap(range(len(refs)), spans, (start, size))
+    left = [
+        refs[i][:, cuts[i][0] + low : cuts[i][0] + high] for i, (low, high) in zip(index, inner)
+    ]
+    return halves(jnp.concatenate(left, axis=1) - got[:, start : start + size])
 
 
 def add_gram(left, got, total=None):
@@ -368,7 +380,7 @@
     )(place, kept, got)
 
 
-def new_columns(place, weights, near, far, left, got):
+def new_columns(place, weights, near, far, left, got, block=1024):
     rows = weights.shape[0]
     pieces, cuts = left
     half = sum(part.shape[1] for part in near)
@@ -376,19 +388,30 @@
     for flip, group in ((0, near), (1, far + [got])):
         start = 0
         for part in group:
-            tasks.append((flip, start, part.shape[1]))
+            for low in range(0, part.shape[1], block):
+                size = min(block, part.shape[1] - low)
+                tasks.append((part is got, len(tasks), low, size, flip, start + low))
             start += part.shape[1]
+    parts_of = [index for index, part in enumerate(near + far) for _ in range(0, part.shape[1], block)]
 
     def kernel(place, weights, *refs):
         refs, (out, whole, sems) = refs[:-3], refs[-3:]
-        parts, lefts, got = refs[: len(tasks) - 1], refs[len(tasks) - 1 : -1], refs[-1]
-        high, low = split(weights[...])
+        number = len(near) + len(far)
+        parts, lefts, got = refs[:number], refs[number:-1], refs[-1]
+        high, low_part = split(weights[...])
         lhs = jnp.concatenate(
-            [jnp.concatenate([high, high], axis=1), jnp.concatenate([low, low], axis=1)], axis=0
+            [
+                jnp.concatenate([high, high], axis=1),
+                jnp.concatenate([low_part, low_part], axis=1),
+            ],
+            axis=0,
         )
         copies = []
-        for index, (flip, start, size) in enumerate(tasks):
-            part = parts[index][...] if index < len(parts) else residual(lefts, cuts, got)
+        for is_last, index, low, size, flip, start in tasks:
+            if is_last:
+                part = residual_span(lefts, cuts, got, low, size)
+            else:
+                part = parts[parts_of[index]][:, low : low + size]
             value = jnp.dot(lhs, part, preferred_element_type=F32)
             side = 1 - place[0] if flip else place[0]
             at = pl.ds(pl.multiple_of(side * half + start, 128), size)

time: 81 us -> 80.9 us (level)
  no operation moved by 1% of the time
where the time goes in v4:
time: 80.9 us; the launch traced here: 80.8 us
  waiting for transfers between devices  29.2 us (36%)
  Pallas kernels  27.5 us (34%)
  starting transfers between devices  22.3 us (28%)
  between operations  1.09 us (1%)
    ppermute x14, waiting for transfers between devices, swap(): return lax.ppermute(x, axis, [(0, 1), (1, 0)])  21.7 us
    pallas_call x16, Pallas kernels, call(): pl.pallas_call(kernel, in_specs=[smem] * scalars + [vmem] * (len(args) -...  19.5 us
    ppermute x14, starting transfers between devices, swap(): return lax.ppermute(x, axis, [(0, 1), (1, 0)])  12.6 us
    ppermute x6, starting transfers between devices, sum_over(): lax.ppermute(x, axis, [(i, i ^ m) for i in range(size)])  8.84 us
    ppermute x6, waiting for transfers between devices, sum_over(): lax.ppermute(x, axis, [(i, i ^ m) for i in range(size)])  7.42 us
    pallas_call x1, Pallas kernels, own_coefs(): pl.pallas_call(kernel, in_specs=[hbm] * 4, out_specs=[vmem] * 5, out_shap...  5.91 us
    pallas_call x1, Pallas kernels, new_columns(): pl.pallas_call(kernel, in_specs=[pl.BlockSpec(memory_space=pltpu.SMEM)] +...  2.16 us
  transfers between devices with their start and end apart: 21, of which 15 were waited for; matrix products, arithmetic and copies ran while one was open for 1% of the time, Pallas kernels for 27%

profile of v4, /device:TPU:0, one launch (start us, length us, event | category | flops | bytes accessed | tf_op | source)
XLA Modules:
  0.0 80.8 jit_solution(6436745628780606892)
XLA Ops:
  0.6 3.0 %collective-permute-start = (bf16[64,256]{1,0:T(8,128)(2,1)}, bf16[64,256]{1,0:T(8,128)(2,1)S(1)}, u32[]{:S(2)}, u32[]{:S(2)}) collective-permute-start(bf16[64,256]{1,0:T(8,128)(2,1)} %points.1), channel_id=1, source_target_pairs={{0,2},{2,0},{1,3},{3,1},{4,6},{6,4},{5,7},{7,5},{8,10},{10,8},{9,1... | collective-permute-start | bytes 98312 | tf_op jit(solution)/shard_map/ppermute | solution.py:443
  3.7 5.9 %own_coefs.1 = (f32[64,8192]{1,0:T(8,128)S(1)}, f32[64,512]{1,0:T(8,128)S(1)}, bf16[256,8192]{1,0:T(8,128)(2,1)S(1)}, f32[1,8192]{1,0:T(1,128)S(1)}, bf16[8192,512]{1,0:T(8,128)(2,1)S(1)}) custom-call(bf16[64,256]{1,0:T(8,128)(2,1)} %points.1, bf16[256,8192]{1,0:T(8,128)(2,1)} %freqs.1, f32[1,8192]{1,0:T(1,128)} %bitcast.7, bf16[8192,512]{1,0:T(8,128)(2,1)} %basis.1), custom_call_target="tpu_custom_call" | custom-call | flops 1000 | bytes 1000 | tf_op jit(solution)/shard_map/own_coefs/pallas_call | solution.py:114
  9.6 3.4 %other_coefs.1 = (f32[64,8192]{1,0:T(8,128)S(1)}, f32[64,512]{1,0:T(8,128)S(1)}, f32[64,512]{1,0:T(8,128)S(1)}) custom-call(s32[2]{0:T(128)S(1)} %pad_add_fusion.place, bf16[64,256]{1,0:T(8,128)(2,1)S(1)} %collective-permute-done.points, bf16[256,8192]{1,0:T(8,128)(2,1)S(1)} %get-tuple-element.52.freqs, f32[1,8192]{1,0:T(1,128)S(1)} %get-tuple-element.53.phases, ...), custom_call_target="tpu_custom_call" | custom-call | flops 1000 | bytes 1000 | tf_op jit(solution)/shard_map/other_coefs/pallas_call | solution.py:54
  13.1 1.3 %collective-permute-done.1 = f32[64,512]{1,0:T(8,128)S(1)} collective-permute-done((f32[64,512]{1,0:T(8,128)S(1)}, f32[64,512]{1,0:T(8,128)S(1)}, u32[]{:S(2)}, u32[]{:S(2)}) %collective-permute-start.1) | collective-permute-done | bytes 131104 | tf_op jit(solution)/shard_map/ppermute | solution.py:443
  14.5 3.7 %collective-permute-start.4 = (f16[64,512]{1,0:T(8,128)(2,1)S(1)}, f16[64,512]{1,0:T(8,128)(2,1)S(1)}, u32[]{:S(2)}, u32[]{:S(2)}) collective-permute-start(f16[64,512]{1,0:T(8,128)(2,1)S(1)} %add_convert_fusion), channel_id=1, source_target_pairs={{0,12},{4,8},{8,4},{12,0},{1,13},{5,9},{9,5},{13,1},{2,14},{6,10},... | collective-permute-start | bytes 196616 | tf_op jit(solution)/shard_map/ppermute | solution.py:447
  18.2 0.8 collective-permute-start.2
  18.9 1.9 %collective-permute-done.4 = f16[64,512]{1,0:T(8,128)(2,1)S(1)} collective-permute-done((f16[64,512]{1,0:T(8,128)(2,1)S(1)}, f16[64,512]{1,0:T(8,128)(2,1)S(1)}, u32[]{:S(2)}, u32[]{:S(2)}) %collective-permute-start.4) | collective-permute-done | bytes 65568 | tf_op jit(solution)/shard_map/ppermute | solution.py:447
  20.8 3.2 %collective-permute-done.3 = f16[64,512]{1,0:T(8,128)(2,1)S(1)} collective-permute-done((f16[64,512]{1,0:T(8,128)(2,1)S(1)}, f16[64,512]{1,0:T(8,128)(2,1)S(1)}, u32[]{:S(2)}, u32[]{:S(2)}) %collective-permute-start.3) | collective-permute-done | bytes 65568 | tf_op jit(solution)/shard_map/ppermute | solution.py:447
  24.2 0.8 %collective-permute-start.6 = (f32[64,512]{1,0:T(8,128)S(1)}, f32[64,512]{1,0:T(8,128)S(1)}, u32[]{:S(2)}, u32[]{:S(2)}) collective-permute-start(f32[64,512]{1,0:T(8,128)S(1)} %add_add_fusion.kept), channel_id=1, source_target_pairs={{1,3},{3,1},{5,7},{7,5},{9,11},{11,9},{13,15},{15,13},{17,19},{19,... | collective-permute-start | bytes 393224 | tf_op jit(solution)/shard_map/ppermute | solution.py:475
  25.0 0.5 collective-permute-done.5.got
  25.5 1.0 %first_fit.1 = (f32[128,1024]{1,0:T(8,128)S(1)}, f32[128,1024]{1,0:T(8,128)S(1)}, f32[64,512]{1,0:T(8,128)S(1)}, bf16[256,512]{1,0:T(8,128)(2,1)S(1)}) custom-call(s32[2]{0:T(128)S(1)} %pad_add_fusion.place, f32[64,512]{1,0:T(8,128)S(1)} %add_add_fusion.kept, f32[64,512]{1,0:T(8,128)S(1)} %collective-permute-done.5.got, ...), custom_call_target="tpu_custom_call" | custom-call | flops 1000 | bytes 1000 | tf_op jit(solution)/shard_map/first_fit/pallas_call | solution.py:54
  26.6 0.6 collective-permute-start.10
  27.2 1.0 %fit.10 = (f32[128,1024]{1,0:T(8,128)S(1)}, f32[128,1024]{1,0:T(8,128)S(1)}) custom-call(s32[2]{0:T(128)S(1)} %pad_add_fusion.place, bf16[256,512]{1,0:T(8,128)(2,1)S(1)} %get-tuple-element.62.parts, f32[64,8192]{1,0:T(8,128)S(1)} %get-tuple-element.58.feats_a, f32[64,8192]{1,0:T(8,128)S(1)} %get-tuple-element.59.feats_b, ...), custom_call_target="tpu_custom_call" | custom-call | flops 1000 | bytes 1000 | tf_op jit(solution)/shard_map/fit/pallas_call | solution.py:54
  28.2 1.5 %collective-permute-start.9 = (f16[128,1024]{1,0:T(8,128)(2,1)S(1)}, f16[128,1024]{1,0:T(8,128)(2,1)S(1)}, u32[]{:S(2)}, u32[]{:S(2)}) collective-permute-start(f16[128,1024]{1,0:T(8,128)(2,1)S(1)} %convert_element_type.66), channel_id=1, source_target_pairs={{0,2},{2,0},{1,3},{3,1},{4,6},{6,4},{5,7},{7,5},{8,10},{10,8},{9,1... | collective-permute-start | bytes 786440 | tf_op jit(solution)/shard_map/ppermute | solution.py:443
  29.8 1.0 %fit.8 = (f32[128,1024]{1,0:T(8,128)S(1)}, f32[128,1024]{1,0:T(8,128)S(1)}) custom-call(s32[2]{0:T(128)S(1)} %pad_add_fusion.place, bf16[256,512]{1,0:T(8,128)(2,1)S(1)} %get-tuple-element.62.parts, f32[64,8192]{1,0:T(8,128)S(1)} %get-tuple-element.58.feats_a, f32[64,8192]{1,0:T(8,128)S(1)} %get-tuple-element.59.feats_b, ...), custom_call_target="tpu_custom_call" | custom-call | flops 1000 | bytes 1000 | tf_op jit(solution)/shard_map/fit/pallas_call | solution.py:54
  30.8 0.6 collective-permute-start.8
  31.5 1.0 %fit.7 = (f32[128,1024]{1,0:T(8,128)S(1)}, f32[128,1024]{1,0:T(8,128)S(1)}) custom-call(s32[2]{0:T(128)S(1)} %pad_add_fusion.place, bf16[256,512]{1,0:T(8,128)(2,1)S(1)} %get-tuple-element.62.parts, f32[64,8192]{1,0:T(8,128)S(1)} %get-tuple-element.58.feats_a, f32[64,8192]{1,0:T(8,128)S(1)} %get-tuple-element.59.feats_b, ...), custom_call_target="tpu_custom_call" | custom-call | flops 1000 | bytes 1000 | tf_op jit(solution)/shard_map/fit/pallas_call | solution.py:54
  32.5 1.5 %collective-permute-start.7 = (f16[128,1024]{1,0:T(8,128)(2,1)S(1)}, f16[128,1024]{1,0:T(8,128)(2,1)S(1)}, u32[]{:S(2)}, u32[]{:S(2)}) collective-permute-start(f16[128,1024]{1,0:T(8,128)(2,1)S(1)} %convert_element_type.62), channel_id=1, source_target_pairs={{0,2},{2,0},{1,3},{3,1},{4,6},{6,4},{5,7},{7,5},{8,10},{10,8},{9,1... | collective-permute-start | bytes 786440 | tf_op jit(solution)/shard_map/ppermute | solution.py:443
  34.1 1.0 %fit.11 = (f32[128,1024]{1,0:T(8,128)S(1)}, f32[128,1024]{1,0:T(8,128)S(1)}) custom-call(s32[2]{0:T(128)S(1)} %pad_add_fusion.place, bf16[256,512]{1,0:T(8,128)(2,1)S(1)} %get-tuple-element.62.parts, f32[64,8192]{1,0:T(8,128)S(1)} %get-tuple-element.58.feats_a, f32[64,8192]{1,0:T(8,128)S(1)} %get-tuple-element.59.feats_b, ...), custom_call_target="tpu_custom_call" | custom-call | flops 1000 | bytes 1000 | tf_op jit(solution)/shard_map/fit/pallas_call | solution.py:54
  35.1 0.6 collective-permute-start.13
  35.7 1.0 %fit.9 = (f32[128,1024]{1,0:T(8,128)S(1)}, f32[128,1024]{1,0:T(8,128)S(1)}) custom-call(s32[2]{0:T(128)S(1)} %pad_add_fusion.place, bf16[256,512]{1,0:T(8,128)(2,1)S(1)} %get-tuple-element.62.parts, f32[64,8192]{1,0:T(8,128)S(1)} %get-tuple-element.58.feats_a, f32[64,8192]{1,0:T(8,128)S(1)} %get-tuple-element.59.feats_b, ...), custom_call_target="tpu_custom_call" | custom-call | flops 1000 | bytes 1000 | tf_op jit(solution)/shard_map/fit/pallas_call | solution.py:54
  36.8 1.3 %fit.6 = (f32[128,2048]{1,0:T(8,128)S(1)}, f32[128,2048]{1,0:T(8,128)S(1)}) custom-call(s32[2]{0:T(128)S(1)} %pad_add_fusion.place, bf16[256,512]{1,0:T(8,128)(2,1)S(1)} %get-tuple-element.62.parts, f32[64,8192]{1,0:T(8,128)S(1)} %get-tuple-element.58.feats_a, f32[64,8192]{1,0:T(8,128)S(1)} %get-tuple-element.59.feats_b, ...), custom_call_target="tpu_custom_call" | custom-call | flops 1000 | bytes 1000 | tf_op jit(solution)/shard_map/fit/pallas_call | solution.py:54
  38.3 0.4 gram.3
  38.6 2.8 %collective-permute-done.9 = f16[128,1024]{1,0:T(8,128)(2,1)S(1)} collective-permute-done((f16[128,1024]{1,0:T(8,128)(2,1)S(1)}, f16[128,1024]{1,0:T(8,128)(2,1)S(1)}, u32[]{:S(2)}, u32[]{:S(2)}) %collective-permute-start.9) | collective-permute-done | bytes 262176 | tf_op jit(solution)/shard_map/ppermute | solution.py:443
  41.5 0.4 gram.4
  41.8 5.2 %collective-permute-done.8 = f16[128,1024]{1,0:T(8,128)(2,1)S(1)} collective-permute-done((f16[128,1024]{1,0:T(8,128)(2,1)S(1)}, f16[128,1024]{1,0:T(8,128)(2,1)S(1)}, u32[]{:S(2)}, u32[]{:S(2)}) %collective-permute-start.8) | collective-permute-done | bytes 262176 | tf_op jit(solution)/shard_map/ppermute | solution.py:443
  47.1 0.4 gram.5
  47.5 5.2 %collective-permute-done.7 = f16[128,1024]{1,0:T(8,128)(2,1)S(1)} collective-permute-done((f16[128,1024]{1,0:T(8,128)(2,1)S(1)}, f16[128,1024]{1,0:T(8,128)(2,1)S(1)}, u32[]{:S(2)}, u32[]{:S(2)}) %collective-permute-start.7) | collective-permute-done | bytes 262176 | tf_op jit(solution)/shard_map/ppermute | solution.py:443
  52.7 1.0 %gram_halves.1 = (bf16[256,1024]{1,0:T(8,128)(2,1)S(1)}, f32[64,128]{1,0:T(8,128)S(1)}, f32[64,128]{1,0:T(8,128)S(1)}) custom-call(s32[2]{0:T(128)S(1)} %pad_add_fusion.place, f32[128,2048]{1,0:T(8,128)S(1)} %get-tuple-element.63.refs_0_, f32[128,1024]{1,0:T(8,128)S(1)} %convert_element_type.63.refs_1_, f32[256,256]{1,0:T(8,128)S(1)} %get-tuple-element.75.refs_2_), custom_call_target="tpu_custom_call" | custom-call | flops 1000 | bytes 1000 | tf_op jit(solution)/shard_map/gram_halves/pallas_call | solution.py:54
  53.7 0.9 %collective-permute-start.11 = (f32[64,128]{1,0:T(8,128)S(1)}, f32[64,128]{1,0:T(8,128)S(1)}, u32[]{:S(2)}, u32[]{:S(2)}) collective-permute-start(f32[64,128]{1,0:T(8,128)S(1)} %get-tuple-element.77), channel_id=1, source_target_pairs={{0,1},{1,0},{2,3},{3,2},{4,5},{5,4},{6,7},{7,6},{8,9},{9,8},{10,11... | collective-permute-start | bytes 98312 | tf_op jit(solution)/shard_map/ppermute | solution.py:443
  54.6 0.9 %collective-permute-done.11 = f32[64,128]{1,0:T(8,128)S(1)} collective-permute-done((f32[64,128]{1,0:T(8,128)S(1)}, f32[64,128]{1,0:T(8,128)S(1)}, u32[]{:S(2)}, u32[]{:S(2)}) %collective-permute-start.11) | collective-permute-done | bytes 32800 | tf_op jit(solution)/shard_map/ppermute | solution.py:443
  55.4 1.4 %collective-permute-start.12 = (f32[64,128]{1,0:T(8,128)S(1)}, f32[64,128]{1,0:T(8,128)S(1)}, u32[]{:S(2)}, u32[]{:S(2)}) collective-permute-start(f32[64,128]{1,0:T(8,128)S(1)} %add.31), channel_id=1, source_target_pairs={{0,2},{2,0},{1,3},{3,1},{4,6},{6,4},{5,7},{7,5},{8,10},{10,8},{9,1... | collective-permute-start | bytes 98312 | tf_op jit(solution)/shard_map/ppermute | solution.py:443
  56.8 1.4 %collective-permute-done.13 = f16[128,1024]{1,0:T(8,128)(2,1)S(1)} collective-permute-done((f16[128,1024]{1,0:T(8,128)(2,1)S(1)}, f16[128,1024]{1,0:T(8,128)(2,1)S(1)}, u32[]{:S(2)}, u32[]{:S(2)}) %collective-permute-start.13) | collective-permute-done | bytes 262176 | tf_op jit(solution)/shard_map/ppermute | solution.py:443
  58.4 0.9 %collective-permute-done.12 = f32[64,128]{1,0:T(8,128)S(1)} collective-permute-done((f32[64,128]{1,0:T(8,128)S(1)}, f32[64,128]{1,0:T(8,128)S(1)}, u32[]{:S(2)}, u32[]{:S(2)}) %collective-permute-start.12) | collective-permute-done | bytes 32800 | tf_op jit(solution)/shard_map/ppermute | solution.py:443
  59.3 1.4 %collective-permute-start.20 = (f16[128,2048]{1,0:T(8,128)(2,1)S(1)}, f16[128,2048]{1,0:T(8,128)(2,1)S(1)}, u32[]{:S(2)}, u32[]{:S(2)}) collective-permute-start(f16[128,2048]{1,0:T(8,128)(2,1)S(1)} %convert_element_type.71), channel_id=1, source_target_pairs={{0,2},{2,0},{1,3},{3,1},{4,6},{6,4},{5,7},{7,5},{8,10},{10,8},{9,1... | collective-permute-start | bytes 1572872 | tf_op jit(solution)/shard_map/ppermute | solution.py:443
  60.8 2.5 %collective-permute-start.16 = (f32[64,128]{1,0:T(8,128)S(1)}, f32[64,128]{1,0:T(8,128)S(1)}, u32[]{:S(2)}, u32[]{:S(2)}) collective-permute-start(f32[64,128]{1,0:T(8,128)S(1)} %add.32), channel_id=1, source_target_pairs={{0,12},{4,8},{8,4},{12,0},{1,13},{5,9},{9,5},{13,1},{2,14},{6,10},... | collective-permute-start | bytes 98312 | tf_op jit(solution)/shard_map/ppermute | solution.py:447
  63.3 0.1 collective-permute-start.15
  63.4 1.8 %collective-permute-start.14 = (f32[64,128]{1,0:T(8,128)S(1)}, f32[64,128]{1,0:T(8,128)S(1)}, u32[]{:S(2)}, u32[]{:S(2)}) collective-permute-start(f32[64,128]{1,0:T(8,128)S(1)} %add.32), channel_id=1, source_target_pairs={{0,4},{4,0},{8,12},{12,8},{1,5},{5,1},{9,13},{13,9},{2,6},{6,2},{1... | collective-permute-start | bytes 98312 | tf_op jit(solution)/shard_map/ppermute | solution.py:447
  65.2 0.6 collective-permute-start.19
  65.8 0.7 collective-permute-done.16
  66.5 1.6 %collective-permute-done.15 = f32[64,128]{1,0:T(8,128)S(1)} collective-permute-done((f32[64,128]{1,0:T(8,128)S(1)}, f32[64,128]{1,0:T(8,128)S(1)}, u32[]{:S(2)}, u32[]{:S(2)}) %collective-permute-start.15) | collective-permute-done | bytes 32800 | tf_op jit(solution)/shard_map/ppermute | solution.py:447
  68.2 1.2 %collective-permute-done.17.got = f32[64,128]{1,0:T(8,128)S(1)} collective-permute-done((f32[64,128]{1,0:T(8,128)S(1)}, f32[64,128]{1,0:T(8,128)S(1)}, u32[]{:S(2)}, u32[]{:S(2)}) %collective-permute-start.17) | collective-permute-done | bytes 32800 | tf_op jit(solution)/shard_map/ppermute | solution.py:443
  69.4 5.1 %factorize.1 = (f32[64,128]{1,0:T(8,128)}, f32[64,128]{1,0:T(8,128)S(1)}) custom-call(s32[2]{0:T(128)S(1)} %pad_add_fusion.place, f32[64,128]{1,0:T(8,128)S(1)} %add_add_fusion.1.kept, f32[64,128]{1,0:T(8,128)S(1)} %collective-permute-done.17.got), custom_call_target="tpu_custom_call" | custom-call | flops 1000 | bytes 20000000 | tf_op jit(solution)/shard_map/factorize/pallas_call | solution.py:54
  74.5 0.2 collective-permute-start.18
  74.7 1.2 %collective-permute-done.18.passed = f32[64,512]{1,0:T(8,128)S(1)} collective-permute-done((f32[64,512]{1,0:T(8,128)S(1)}, f32[64,512]{1,0:T(8,128)S(1)}, u32[]{:S(2)}, u32[]{:S(2)}) %collective-permute-start.18) | collective-permute-done | bytes 131104 | tf_op jit(solution)/shard_map/ppermute | solution.py:443
  75.8 1.3 %own_columns.1 = f32[64,1024]{1,0:T(8,128)} custom-call(s32[2]{0:T(128)S(1)} %pad_add_fusion.place, f32[64,512]{1,0:T(8,128)S(1)} %get-tuple-element.60.own, f32[64,512]{1,0:T(8,128)S(1)} %collective-permute-done.6.theirs, f32[64,512]{1,0:T(8,128)S(1)} %collective-permute-done.18.passed), custom_call_target="tpu_custom_call" | custom-call | flops 1000 | bytes 1000 | tf_op jit(solution)/shard_map/own_columns/pallas_call | solution.py:54
  77.1 1.1 %collective-permute-done.19 = f16[128,1024]{1,0:T(8,128)(2,1)S(1)} collective-permute-done((f16[128,1024]{1,0:T(8,128)(2,1)S(1)}, f16[128,1024]{1,0:T(8,128)(2,1)S(1)}, u32[]{:S(2)}, u32[]{:S(2)}) %collective-permute-start.19) | collective-permute-done | bytes 262176 | tf_op jit(solution)/shard_map/ppermute | solution.py:443
  78.5 2.2 %new_basis.1 = f32[64,8192]{1,0:T(8,128)} custom-call(s32[2]{0:T(128)S(1)} %pad_add_fusion.place, f32[64,128]{1,0:T(8,128)S(1)} %get-tuple-element.90.weights, bf16[256,1024]{1,0:T(8,128)(2,1)S(1)} %get-tuple-element.91.refs_0_, bf16[256,1024]{1,0:T(8,128)(2,1)S(1)} %get-tuple-element.92.refs_1_, bf16[256,1024]{1,0:T(8,128)(2,1)S(1)} %get-tuple-element.93.refs_2_, ...), custom_call_target="tpu_custom_call" | custom-call | flops 1000 | bytes 1000 | tf_op jit(solution)/shard_map/new_basis/pallas_call | solution.py:427
  (32 shorter events, 1.1 us)
Async XLA Ops:
  0.6 9.0 %collective-permute-start = (bf16[64,256]{1,0:T(8,128)(2,1)}, bf16[64,256]{1,0:T(8,128)(2,1)S(1)}, u32[]{:S(2)}, u32[]{:S(2)}) collective-permute-start(bf16[64,256]{1,0:T(8,128)(2,1)} %points.1), channel_id=1, source_target_pairs={{0,2},{2,0},{1,3},{3,1},{4,6},{6,4},{5,7},{7,5},{8,10},{10,8},{9,1... | collective-permute-start | bytes 98312 | tf_op jit(solution)/shard_map/ppermute | solution.py:443
  13.0 1.4 %collective-permute-start.1 = (f32[64,512]{1,0:T(8,128)S(1)}, f32[64,512]{1,0:T(8,128)S(1)}, u32[]{:S(2)}, u32[]{:S(2)}) collective-permute-start(f32[64,512]{1,0:T(8,128)S(1)} %get-tuple-element.57), channel_id=1, source_target_pairs={{0,1},{1,0},{2,3},{3,2},{4,5},{5,4},{6,7},{7,6},{8,9},{9,8},{10,11... | collective-permute-start | bytes 393224 | tf_op jit(solution)/shard_map/ppermute | solution.py:443
  14.5 6.4 %collective-permute-start.4 = (f16[64,512]{1,0:T(8,128)(2,1)S(1)}, f16[64,512]{1,0:T(8,128)(2,1)S(1)}, u32[]{:S(2)}, u32[]{:S(2)}) collective-permute-start(f16[64,512]{1,0:T(8,128)(2,1)S(1)} %add_convert_fusion), channel_id=1, source_target_pairs={{0,12},{4,8},{8,4},{12,0},{1,13},{5,9},{9,5},{13,1},{2,14},{6,10},... | collective-permute-start | bytes 196616 | tf_op jit(solution)/shard_map/ppermute | solution.py:447
  18.2 5.9 %collective-permute-start.3 = (f16[64,512]{1,0:T(8,128)(2,1)S(1)}, f16[64,512]{1,0:T(8,128)(2,1)S(1)}, u32[]{:S(2)}, u32[]{:S(2)}) collective-permute-start(f16[64,512]{1,0:T(8,128)(2,1)S(1)} %add_convert_fusion), channel_id=1, source_target_pairs={{0,8},{4,12},{8,0},{12,4},{1,9},{5,13},{9,1},{13,5},{2,10},{6,14},... | collective-permute-start | bytes 196616 | tf_op jit(solution)/shard_map/ppermute | solution.py:447
  18.2 5.9 %collective-permute-start.2 = (f16[64,512]{1,0:T(8,128)(2,1)S(1)}, f16[64,512]{1,0:T(8,128)(2,1)S(1)}, u32[]{:S(2)}, u32[]{:S(2)}) collective-permute-start(f16[64,512]{1,0:T(8,128)(2,1)S(1)} %add_convert_fusion), channel_id=1, source_target_pairs={{0,4},{4,0},{8,12},{12,8},{1,5},{5,1},{9,13},{13,9},{2,6},{6,2},{1... | collective-permute-start | bytes 196616 | tf_op jit(solution)/shard_map/ppermute | solution.py:447
  24.1 1.4 %collective-permute-start.5 = (f32[64,512]{1,0:T(8,128)S(1)}, f32[64,512]{1,0:T(8,128)S(1)}, u32[]{:S(2)}, u32[]{:S(2)}) collective-permute-start(f32[64,512]{1,0:T(8,128)S(1)} %add_add_fusion.kept), channel_id=1, source_target_pairs={{0,1},{1,0},{2,3},{3,2},{4,5},{5,4},{6,7},{7,6},{8,9},{9,8},{10,11... | collective-permute-start | bytes 393224 | tf_op jit(solution)/shard_map/ppermute | solution.py:443
  24.2 9.9 %collective-permute-start.6 = (f32[64,512]{1,0:T(8,128)S(1)}, f32[64,512]{1,0:T(8,128)S(1)}, u32[]{:S(2)}, u32[]{:S(2)}) collective-permute-start(f32[64,512]{1,0:T(8,128)S(1)} %add_add_fusion.kept), channel_id=1, source_target_pairs={{1,3},{3,1},{5,7},{7,5},{9,11},{11,9},{13,15},{15,13},{17,19},{19,... | collective-permute-start | bytes 393224 | tf_op jit(solution)/shard_map/ppermute | solution.py:475
  26.6 11.6 %collective-permute-start.10 = (f16[128,1024]{1,0:T(8,128)(2,1)S(1)}, f16[128,1024]{1,0:T(8,128)(2,1)S(1)}, u32[]{:S(2)}, u32[]{:S(2)}) collective-permute-start(f16[128,1024]{1,0:T(8,128)(2,1)S(1)} %convert_element_type.68), channel_id=1, source_target_pairs={{0,2},{2,0},{1,3},{3,1},{4,6},{6,4},{5,7},{7,5},{8,10},{10,8},{9,1... | collective-permute-start | bytes 786440 | tf_op jit(solution)/shard_map/ppermute | solution.py:443
  28.2 13.2 %collective-permute-start.9 = (f16[128,1024]{1,0:T(8,128)(2,1)S(1)}, f16[128,1024]{1,0:T(8,128)(2,1)S(1)}, u32[]{:S(2)}, u32[]{:S(2)}) collective-permute-start(f16[128,1024]{1,0:T(8,128)(2,1)S(1)} %convert_element_type.66), channel_id=1, source_target_pairs={{0,2},{2,0},{1,3},{3,1},{4,6},{6,4},{5,7},{7,5},{8,10},{10,8},{9,1... | collective-permute-start | bytes 786440 | tf_op jit(solution)/shard_map/ppermute | solution.py:443
  30.8 16.2 %collective-permute-start.8 = (f16[128,1024]{1,0:T(8,128)(2,1)S(1)}, f16[128,1024]{1,0:T(8,128)(2,1)S(1)}, u32[]{:S(2)}, u32[]{:S(2)}) collective-permute-start(f16[128,1024]{1,0:T(8,128)(2,1)S(1)} %convert_element_type.64), channel_id=1, source_target_pairs={{0,2},{2,0},{1,3},{3,1},{4,6},{6,4},{5,7},{7,5},{8,10},{10,8},{9,1... | collective-permute-start | bytes 786440 | tf_op jit(solution)/shard_map/ppermute | solution.py:443
  32.5 20.1 %collective-permute-start.7 = (f16[128,1024]{1,0:T(8,128)(2,1)S(1)}, f16[128,1024]{1,0:T(8,128)(2,1)S(1)}, u32[]{:S(2)}, u32[]{:S(2)}) collective-permute-start(f16[128,1024]{1,0:T(8,128)(2,1)S(1)} %convert_element_type.62), channel_id=1, source_target_pairs={{0,2},{2,0},{1,3},{3,1},{4,6},{6,4},{5,7},{7,5},{8,10},{10,8},{9,1... | collective-permute-start | bytes 786440 | tf_op jit(solution)/shard_map/ppermute | solution.py:443
  35.1 23.2 %collective-permute-start.13 = (f16[128,1024]{1,0:T(8,128)(2,1)S(1)}, f16[128,1024]{1,0:T(8,128)(2,1)S(1)}, u32[]{:S(2)}, u32[]{:S(2)}) collective-permute-start(f16[128,1024]{1,0:T(8,128)(2,1)S(1)} %convert_element_type.72), channel_id=1, source_target_pairs={{0,2},{2,0},{1,3},{3,1},{4,6},{6,4},{5,7},{7,5},{8,10},{10,8},{9,1... | collective-permute-start | bytes 786440 | tf_op jit(solution)/shard_map/ppermute | solution.py:443
  53.7 1.7 %collective-permute-start.11 = (f32[64,128]{1,0:T(8,128)S(1)}, f32[64,128]{1,0:T(8,128)S(1)}, u32[]{:S(2)}, u32[]{:S(2)}) collective-permute-start(f32[64,128]{1,0:T(8,128)S(1)} %get-tuple-element.77), channel_id=1, source_target_pairs={{0,1},{1,0},{2,3},{3,2},{4,5},{5,4},{6,7},{7,6},{8,9},{9,8},{10,11... | collective-permute-start | bytes 98312 | tf_op jit(solution)/shard_map/ppermute | solution.py:443
  55.4 3.9 %collective-permute-start.12 = (f32[64,128]{1,0:T(8,128)S(1)}, f32[64,128]{1,0:T(8,128)S(1)}, u32[]{:S(2)}, u32[]{:S(2)}) collective-permute-start(f32[64,128]{1,0:T(8,128)S(1)} %add.31), channel_id=1, source_target_pairs={{0,2},{2,0},{1,3},{3,1},{4,6},{6,4},{5,7},{7,5},{8,10},{10,8},{9,1... | collective-permute-start | bytes 98312 | tf_op jit(solution)/shard_map/ppermute | solution.py:443
  59.3 19.0 %collective-permute-start.20 = (f16[128,2048]{1,0:T(8,128)(2,1)S(1)}, f16[128,2048]{1,0:T(8,128)(2,1)S(1)}, u32[]{:S(2)}, u32[]{:S(2)}) collective-permute-start(f16[128,2048]{1,0:T(8,128)(2,1)S(1)} %convert_element_type.71), channel_id=1, source_target_pairs={{0,2},{2,0},{1,3},{3,1},{4,6},{6,4},{5,7},{7,5},{8,10},{10,8},{9,1... | collective-permute-start | bytes 1572872 | tf_op jit(solution)/shard_map/ppermute | solution.py:443
  60.8 5.7 %collective-permute-start.16 = (f32[64,128]{1,0:T(8,128)S(1)}, f32[64,128]{1,0:T(8,128)S(1)}, u32[]{:S(2)}, u32[]{:S(2)}) collective-permute-start(f32[64,128]{1,0:T(8,128)S(1)} %add.32), channel_id=1, source_target_pairs={{0,12},{4,8},{8,4},{12,0},{1,13},{5,9},{9,5},{13,1},{2,14},{6,10},... | collective-permute-start | bytes 98312 | tf_op jit(solution)/shard_map/ppermute | solution.py:447
  63.3 4.8 %collective-permute-start.15 = (f32[64,128]{1,0:T(8,128)S(1)}, f32[64,128]{1,0:T(8,128)S(1)}, u32[]{:S(2)}, u32[]{:S(2)}) collective-permute-start(f32[64,128]{1,0:T(8,128)S(1)} %add.32), channel_id=1, source_target_pairs={{0,8},{4,12},{8,0},{12,4},{1,9},{5,13},{9,1},{13,5},{2,10},{6,14},... | collective-permute-start | bytes 98312 | tf_op jit(solution)/shard_map/ppermute | solution.py:447
  63.4 4.7 %collective-permute-start.14 = (f32[64,128]{1,0:T(8,128)S(1)}, f32[64,128]{1,0:T(8,128)S(1)}, u32[]{:S(2)}, u32[]{:S(2)}) collective-permute-start(f32[64,128]{1,0:T(8,128)S(1)} %add.32), channel_id=1, source_target_pairs={{0,4},{4,0},{8,12},{12,8},{1,5},{5,1},{9,13},{13,9},{2,6},{6,2},{1... | collective-permute-start | bytes 98312 | tf_op jit(solution)/shard_map/ppermute | solution.py:447
  65.2 13.1 %collective-permute-start.19 = (f16[128,1024]{1,0:T(8,128)(2,1)S(1)}, f16[128,1024]{1,0:T(8,128)(2,1)S(1)}, u32[]{:S(2)}, u32[]{:S(2)}) collective-permute-start(f16[128,1024]{1,0:T(8,128)(2,1)S(1)} %convert_element_type.70), channel_id=1, source_target_pairs={{0,2},{2,0},{1,3},{3,1},{4,6},{6,4},{5,7},{7,5},{8,10},{10,8},{9,1... | collective-permute-start | bytes 786440 | tf_op jit(solution)/shard_map/ppermute | solution.py:443
  68.1 1.3 %collective-permute-start.17 = (f32[64,128]{1,0:T(8,128)S(1)}, f32[64,128]{1,0:T(8,128)S(1)}, u32[]{:S(2)}, u32[]{:S(2)}) collective-permute-start(f32[64,128]{1,0:T(8,128)S(1)} %add_add_fusion.1.kept), channel_id=1, source_target_pairs={{0,1},{1,0},{2,3},{3,2},{4,5},{5,4},{6,7},{7,6},{8,9},{9,8},{10,11... | collective-permute-start | bytes 98312 | tf_op jit(solution)/shard_map/ppermute | solution.py:443
  74.5 1.3 %collective-permute-start.18 = (f32[64,512]{1,0:T(8,128)S(1)}, f32[64,512]{1,0:T(8,128)S(1)}, u32[]{:S(2)}, u32[]{:S(2)}) collective-permute-start(f32[64,512]{1,0:T(8,128)S(1)} %collective-permute-done.6.theirs), channel_id=1, source_target_pairs={{0,1},{1,0},{2,3},{3,2},{4,5},{5,4},{6,7},{7,6},{8,9},{9,8},{10,11... | collective-permute-start | bytes 393224 | tf_op jit(solution)/shard_map/ppermute | solution.py:443

commit v5 on v3

--- a/solution.py
+++ b/solution.py
@@ -11,21 +11,17 @@
 
 COS = (
     0.9999999889369959,
-    -0.4999998901135819,
-    0.041666488148010265,
-    -0.0013887798934755957,
-    2.4769791619676175e-05,
-    -2.7078195310289617e-07,
-    1.7242244242579268e-09,
+    -19.739204464036813,
+    64.93911579322743,
+    -85.4501108378944,
+    60.16740762749498,
+    -25.966798028642813,
+    6.527580149233599,
 )
-TURN_HEAD = 6.28125
-TURN_REST = 0.0019353071795864769
-
-
 def cosine(x):
-    turns = jnp.round(x * 0.15915494309189535)
-    x = (x - turns * TURN_HEAD) - turns * TURN_REST
-    t = x * x
+    turns = x * 0.15915494309189535
+    t = turns - jnp.round(turns)
+    t = t * t
     y = COS[-1]
     for c in COS[-2::-1]:
         y = y * t + c

time: 81 us -> 80.8 us (level)
  no operation moved by 1% of the time
where the time goes in v5:
time: 80.8 us; the launch traced here: 80.6 us
  waiting for transfers between devices  29.2 us (36%)
  Pallas kernels  27.3 us (34%)
  starting transfers between devices  22.3 us (28%)
  between operations  1.09 us (1%)
    ppermute x14, waiting for transfers between devices, swap(): return lax.ppermute(x, axis, [(0, 1), (1, 0)])  21.8 us
    pallas_call x16, Pallas kernels, call(): pl.pallas_call(kernel, in_specs=[smem] * scalars + [vmem] * (len(args) -...  19.4 us
    ppermute x14, starting transfers between devices, swap(): return lax.ppermute(x, axis, [(0, 1), (1, 0)])  12.6 us
    ppermute x6, starting transfers between devices, sum_over(): lax.ppermute(x, axis, [(i, i ^ m) for i in range(size)])  8.84 us
    ppermute x6, waiting for transfers between devices, sum_over(): lax.ppermute(x, axis, [(i, i ^ m) for i in range(size)])  7.41 us
    pallas_call x1, Pallas kernels, own_coefs(): pl.pallas_call(kernel, in_specs=[hbm] * 4, out_specs=[vmem] * 5, out_shap...  5.71 us
    pallas_call x1, Pallas kernels, new_columns(): pl.pallas_call(kernel, in_specs=[pl.BlockSpec(memory_space=pltpu.SMEM)] +...  2.2 us
  transfers between devices with their start and end apart: 21, of which 15 were waited for; matrix products, arithmetic and copies ran while one was open for 1% of the time, Pallas kernels for 27%

profile of v5, /device:TPU:0, one launch (start us, length us, event | category | flops | bytes accessed | tf_op | source)
XLA Modules:
  0.0 80.6 jit_solution(11360738385072704511)
XLA Ops:
  0.6 3.0 %collective-permute-start = (bf16[64,256]{1,0:T(8,128)(2,1)}, bf16[64,256]{1,0:T(8,128)(2,1)S(1)}, u32[]{:S(2)}, u32[]{:S(2)}) collective-permute-start(bf16[64,256]{1,0:T(8,128)(2,1)} %points.1), channel_id=1, source_target_pairs={{0,2},{2,0},{1,3},{3,1},{4,6},{6,4},{5,7},{7,5},{8,10},{10,8},{9,1... | collective-permute-start | bytes 98312 | tf_op jit(solution)/shard_map/ppermute | solution.py:416
  3.7 5.7 %own_coefs.1 = (f32[64,8192]{1,0:T(8,128)S(1)}, f32[64,512]{1,0:T(8,128)S(1)}, bf16[256,8192]{1,0:T(8,128)(2,1)S(1)}, f32[1,8192]{1,0:T(1,128)S(1)}, bf16[8192,512]{1,0:T(8,128)(2,1)S(1)}) custom-call(bf16[64,256]{1,0:T(8,128)(2,1)} %points.1, bf16[256,8192]{1,0:T(8,128)(2,1)} %freqs.1, f32[1,8192]{1,0:T(1,128)} %bitcast.7, bf16[8192,512]{1,0:T(8,128)(2,1)} %basis.1), custom_call_target="tpu_custom_call" | custom-call | flops 1000 | bytes 1000 | tf_op jit(solution)/shard_map/own_coefs/pallas_call | solution.py:110
  9.4 3.4 %other_coefs.1 = (f32[64,8192]{1,0:T(8,128)S(1)}, f32[64,512]{1,0:T(8,128)S(1)}, f32[64,512]{1,0:T(8,128)S(1)}) custom-call(s32[2]{0:T(128)S(1)} %pad_add_fusion.place, bf16[64,256]{1,0:T(8,128)(2,1)S(1)} %collective-permute-done.points, bf16[256,8192]{1,0:T(8,128)(2,1)S(1)} %get-tuple-element.52.freqs, f32[1,8192]{1,0:T(1,128)S(1)} %get-tuple-element.53.phases, ...), custom_call_target="tpu_custom_call" | custom-call | flops 1000 | bytes 1000 | tf_op jit(solution)/shard_map/other_coefs/pallas_call | solution.py:50
  12.9 1.3 %collective-permute-done.1 = f32[64,512]{1,0:T(8,128)S(1)} collective-permute-done((f32[64,512]{1,0:T(8,128)S(1)}, f32[64,512]{1,0:T(8,128)S(1)}, u32[]{:S(2)}, u32[]{:S(2)}) %collective-permute-start.1) | collective-permute-done | bytes 131104 | tf_op jit(solution)/shard_map/ppermute | solution.py:416
  14.2 3.7 %collective-permute-start.4 = (f16[64,512]{1,0:T(8,128)(2,1)S(1)}, f16[64,512]{1,0:T(8,128)(2,1)S(1)}, u32[]{:S(2)}, u32[]{:S(2)}) collective-permute-start(f16[64,512]{1,0:T(8,128)(2,1)S(1)} %add_convert_fusion), channel_id=1, source_target_pairs={{0,12},{4,8},{8,4},{12,0},{1,13},{5,9},{9,5},{13,1},{2,14},{6,10},... | collective-permute-start | bytes 196616 | tf_op jit(solution)/shard_map/ppermute | solution.py:420
  17.9 0.8 collective-permute-start.2
  18.7 1.9 %collective-permute-done.4 = f16[64,512]{1,0:T(8,128)(2,1)S(1)} collective-permute-done((f16[64,512]{1,0:T(8,128)(2,1)S(1)}, f16[64,512]{1,0:T(8,128)(2,1)S(1)}, u32[]{:S(2)}, u32[]{:S(2)}) %collective-permute-start.4) | collective-permute-done | bytes 65568 | tf_op jit(solution)/shard_map/ppermute | solution.py:420
  20.6 3.2 %collective-permute-done.3 = f16[64,512]{1,0:T(8,128)(2,1)S(1)} collective-permute-done((f16[64,512]{1,0:T(8,128)(2,1)S(1)}, f16[64,512]{1,0:T(8,128)(2,1)S(1)}, u32[]{:S(2)}, u32[]{:S(2)}) %collective-permute-start.3) | collective-permute-done | bytes 65568 | tf_op jit(solution)/shard_map/ppermute | solution.py:420
  23.9 0.8 %collective-permute-start.6 = (f32[64,512]{1,0:T(8,128)S(1)}, f32[64,512]{1,0:T(8,128)S(1)}, u32[]{:S(2)}, u32[]{:S(2)}) collective-permute-start(f32[64,512]{1,0:T(8,128)S(1)} %add_add_fusion.kept), channel_id=1, source_target_pairs={{1,3},{3,1},{5,7},{7,5},{9,11},{11,9},{13,15},{15,13},{17,19},{19,... | collective-permute-start | bytes 393224 | tf_op jit(solution)/shard_map/ppermute | solution.py:448
  24.8 0.5 collective-permute-done.5.got
  25.3 1.0 %first_fit.1 = (f32[128,1024]{1,0:T(8,128)S(1)}, f32[128,1024]{1,0:T(8,128)S(1)}, f32[64,512]{1,0:T(8,128)S(1)}, bf16[256,512]{1,0:T(8,128)(2,1)S(1)}) custom-call(s32[2]{0:T(128)S(1)} %pad_add_fusion.place, f32[64,512]{1,0:T(8,128)S(1)} %add_add_fusion.kept, f32[64,512]{1,0:T(8,128)S(1)} %collective-permute-done.5.got, ...), custom_call_target="tpu_custom_call" | custom-call | flops 1000 | bytes 1000 | tf_op jit(solution)/shard_map/first_fit/pallas_call | solution.py:50
  26.3 0.6 collective-permute-start.10
  26.9 1.0 %fit.10 = (f32[128,1024]{1,0:T(8,128)S(1)}, f32[128,1024]{1,0:T(8,128)S(1)}) custom-call(s32[2]{0:T(128)S(1)} %pad_add_fusion.place, bf16[256,512]{1,0:T(8,128)(2,1)S(1)} %get-tuple-element.62.parts, f32[64,8192]{1,0:T(8,128)S(1)} %get-tuple-element.58.feats_a, f32[64,8192]{1,0:T(8,128)S(1)} %get-tuple-element.59.feats_b, ...), custom_call_target="tpu_custom_call" | custom-call | flops 1000 | bytes 1000 | tf_op jit(solution)/shard_map/fit/pallas_call | solution.py:50
  28.0 1.6 %collective-permute-start.9 = (f16[128,1024]{1,0:T(8,128)(2,1)S(1)}, f16[128,1024]{1,0:T(8,128)(2,1)S(1)}, u32[]{:S(2)}, u32[]{:S(2)}) collective-permute-start(f16[128,1024]{1,0:T(8,128)(2,1)S(1)} %convert_element_type.66), channel_id=1, source_target_pairs={{0,2},{2,0},{1,3},{3,1},{4,6},{6,4},{5,7},{7,5},{8,10},{10,8},{9,1... | collective-permute-start | bytes 786440 | tf_op jit(solution)/shard_map/ppermute | solution.py:416
  29.6 1.0 %fit.8 = (f32[128,1024]{1,0:T(8,128)S(1)}, f32[128,1024]{1,0:T(8,128)S(1)}) custom-call(s32[2]{0:T(128)S(1)} %pad_add_fusion.place, bf16[256,512]{1,0:T(8,128)(2,1)S(1)} %get-tuple-element.62.parts, f32[64,8192]{1,0:T(8,128)S(1)} %get-tuple-element.58.feats_a, f32[64,8192]{1,0:T(8,128)S(1)} %get-tuple-element.59.feats_b, ...), custom_call_target="tpu_custom_call" | custom-call | flops 1000 | bytes 1000 | tf_op jit(solution)/shard_map/fit/pallas_call | solution.py:50
  30.6 0.6 collective-permute-start.8
  31.2 1.0 %fit.7 = (f32[128,1024]{1,0:T(8,128)S(1)}, f32[128,1024]{1,0:T(8,128)S(1)}) custom-call(s32[2]{0:T(128)S(1)} %pad_add_fusion.place, bf16[256,512]{1,0:T(8,128)(2,1)S(1)} %get-tuple-element.62.parts, f32[64,8192]{1,0:T(8,128)S(1)} %get-tuple-element.58.feats_a, f32[64,8192]{1,0:T(8,128)S(1)} %get-tuple-element.59.feats_b, ...), custom_call_target="tpu_custom_call" | custom-call | flops 1000 | bytes 1000 | tf_op jit(solution)/shard_map/fit/pallas_call | solution.py:50
  32.3 1.6 %collective-permute-start.7 = (f16[128,1024]{1,0:T(8,128)(2,1)S(1)}, f16[128,1024]{1,0:T(8,128)(2,1)S(1)}, u32[]{:S(2)}, u32[]{:S(2)}) collective-permute-start(f16[128,1024]{1,0:T(8,128)(2,1)S(1)} %convert_element_type.62), channel_id=1, source_target_pairs={{0,2},{2,0},{1,3},{3,1},{4,6},{6,4},{5,7},{7,5},{8,10},{10,8},{9,1... | collective-permute-start | bytes 786440 | tf_op jit(solution)/shard_map/ppermute | solution.py:416
  33.8 1.0 %fit.11 = (f32[128,1024]{1,0:T(8,128)S(1)}, f32[128,1024]{1,0:T(8,128)S(1)}) custom-call(s32[2]{0:T(128)S(1)} %pad_add_fusion.place, bf16[256,512]{1,0:T(8,128)(2,1)S(1)} %get-tuple-element.62.parts, f32[64,8192]{1,0:T(8,128)S(1)} %get-tuple-element.58.feats_a, f32[64,8192]{1,0:T(8,128)S(1)} %get-tuple-element.59.feats_b, ...), custom_call_target="tpu_custom_call" | custom-call | flops 1000 | bytes 1000 | tf_op jit(solution)/shard_map/fit/pallas_call | solution.py:50
  34.9 0.6 collective-permute-start.13
  35.5 1.0 %fit.9 = (f32[128,1024]{1,0:T(8,128)S(1)}, f32[128,1024]{1,0:T(8,128)S(1)}) custom-call(s32[2]{0:T(128)S(1)} %pad_add_fusion.place, bf16[256,512]{1,0:T(8,128)(2,1)S(1)} %get-tuple-element.62.parts, f32[64,8192]{1,0:T(8,128)S(1)} %get-tuple-element.58.feats_a, f32[64,8192]{1,0:T(8,128)S(1)} %get-tuple-element.59.feats_b, ...), custom_call_target="tpu_custom_call" | custom-call | flops 1000 | bytes 1000 | tf_op jit(solution)/shard_map/fit/pallas_call | solution.py:50
  36.5 1.3 %fit.6 = (f32[128,2048]{1,0:T(8,128)S(1)}, f32[128,2048]{1,0:T(8,128)S(1)}) custom-call(s32[2]{0:T(128)S(1)} %pad_add_fusion.place, bf16[256,512]{1,0:T(8,128)(2,1)S(1)} %get-tuple-element.62.parts, f32[64,8192]{1,0:T(8,128)S(1)} %get-tuple-element.58.feats_a, f32[64,8192]{1,0:T(8,128)S(1)} %get-tuple-element.59.feats_b, ...), custom_call_target="tpu_custom_call" | custom-call | flops 1000 | bytes 1000 | tf_op jit(solution)/shard_map/fit/pallas_call | solution.py:50
  38.0 0.4 gram.3
  38.4 2.8 %collective-permute-done.9 = f16[128,1024]{1,0:T(8,128)(2,1)S(1)} collective-permute-done((f16[128,1024]{1,0:T(8,128)(2,1)S(1)}, f16[128,1024]{1,0:T(8,128)(2,1)S(1)}, u32[]{:S(2)}, u32[]{:S(2)}) %collective-permute-start.9) | collective-permute-done | bytes 262176 | tf_op jit(solution)/shard_map/ppermute | solution.py:416
  41.2 0.4 gram.4
  41.6 5.2 %collective-permute-done.8 = f16[128,1024]{1,0:T(8,128)(2,1)S(1)} collective-permute-done((f16[128,1024]{1,0:T(8,128)(2,1)S(1)}, f16[128,1024]{1,0:T(8,128)(2,1)S(1)}, u32[]{:S(2)}, u32[]{:S(2)}) %collective-permute-start.8) | collective-permute-done | bytes 262176 | tf_op jit(solution)/shard_map/ppermute | solution.py:416
  46.9 0.4 gram.5
  47.2 5.2 %collective-permute-done.7 = f16[128,1024]{1,0:T(8,128)(2,1)S(1)} collective-permute-done((f16[128,1024]{1,0:T(8,128)(2,1)S(1)}, f16[128,1024]{1,0:T(8,128)(2,1)S(1)}, u32[]{:S(2)}, u32[]{:S(2)}) %collective-permute-start.7) | collective-permute-done | bytes 262176 | tf_op jit(solution)/shard_map/ppermute | solution.py:416
  52.5 1.0 %gram_halves.1 = (bf16[256,1024]{1,0:T(8,128)(2,1)S(1)}, f32[64,128]{1,0:T(8,128)S(1)}, f32[64,128]{1,0:T(8,128)S(1)}) custom-call(s32[2]{0:T(128)S(1)} %pad_add_fusion.place, f32[128,2048]{1,0:T(8,128)S(1)} %get-tuple-element.63.refs_0_, f32[128,1024]{1,0:T(8,128)S(1)} %convert_element_type.63.refs_1_, f32[256,256]{1,0:T(8,128)S(1)} %get-tuple-element.75.refs_2_), custom_call_target="tpu_custom_call" | custom-call | flops 1000 | bytes 1000 | tf_op jit(solution)/shard_map/gram_halves/pallas_call | solution.py:50
  53.5 0.9 %collective-permute-start.11 = (f32[64,128]{1,0:T(8,128)S(1)}, f32[64,128]{1,0:T(8,128)S(1)}, u32[]{:S(2)}, u32[]{:S(2)}) collective-permute-start(f32[64,128]{1,0:T(8,128)S(1)} %get-tuple-element.77), channel_id=1, source_target_pairs={{0,1},{1,0},{2,3},{3,2},{4,5},{5,4},{6,7},{7,6},{8,9},{9,8},{10,11... | collective-permute-start | bytes 98312 | tf_op jit(solution)/shard_map/ppermute | solution.py:416
  54.3 0.9 %collective-permute-done.11 = f32[64,128]{1,0:T(8,128)S(1)} collective-permute-done((f32[64,128]{1,0:T(8,128)S(1)}, f32[64,128]{1,0:T(8,128)S(1)}, u32[]{:S(2)}, u32[]{:S(2)}) %collective-permute-start.11) | collective-permute-done | bytes 32800 | tf_op jit(solution)/shard_map/ppermute | solution.py:416
  55.2 1.4 %collective-permute-start.12 = (f32[64,128]{1,0:T(8,128)S(1)}, f32[64,128]{1,0:T(8,128)S(1)}, u32[]{:S(2)}, u32[]{:S(2)}) collective-permute-start(f32[64,128]{1,0:T(8,128)S(1)} %add.31), channel_id=1, source_target_pairs={{0,2},{2,0},{1,3},{3,1},{4,6},{6,4},{5,7},{7,5},{8,10},{10,8},{9,1... | collective-permute-start | bytes 98312 | tf_op jit(solution)/shard_map/ppermute | solution.py:416
  56.6 1.4 %collective-permute-done.13 = f16[128,1024]{1,0:T(8,128)(2,1)S(1)} collective-permute-done((f16[128,1024]{1,0:T(8,128)(2,1)S(1)}, f16[128,1024]{1,0:T(8,128)(2,1)S(1)}, u32[]{:S(2)}, u32[]{:S(2)}) %collective-permute-start.13) | collective-permute-done | bytes 262176 | tf_op jit(solution)/shard_map/ppermute | solution.py:416
  58.2 0.9 %collective-permute-done.12 = f32[64,128]{1,0:T(8,128)S(1)} collective-permute-done((f32[64,128]{1,0:T(8,128)S(1)}, f32[64,128]{1,0:T(8,128)S(1)}, u32[]{:S(2)}, u32[]{:S(2)}) %collective-permute-start.12) | collective-permute-done | bytes 32800 | tf_op jit(solution)/shard_map/ppermute | solution.py:416
  59.1 1.4 %collective-permute-start.20 = (f16[128,2048]{1,0:T(8,128)(2,1)S(1)}, f16[128,2048]{1,0:T(8,128)(2,1)S(1)}, u32[]{:S(2)}, u32[]{:S(2)}) collective-permute-start(f16[128,2048]{1,0:T(8,128)(2,1)S(1)} %convert_element_type.71), channel_id=1, source_target_pairs={{0,2},{2,0},{1,3},{3,1},{4,6},{6,4},{5,7},{7,5},{8,10},{10,8},{9,1... | collective-permute-start | bytes 1572872 | tf_op jit(solution)/shard_map/ppermute | solution.py:416
  60.5 2.5 %collective-permute-start.16 = (f32[64,128]{1,0:T(8,128)S(1)}, f32[64,128]{1,0:T(8,128)S(1)}, u32[]{:S(2)}, u32[]{:S(2)}) collective-permute-start(f32[64,128]{1,0:T(8,128)S(1)} %add.32), channel_id=1, source_target_pairs={{0,12},{4,8},{8,4},{12,0},{1,13},{5,9},{9,5},{13,1},{2,14},{6,10},... | collective-permute-start | bytes 98312 | tf_op jit(solution)/shard_map/ppermute | solution.py:420
  63.0 0.1 collective-permute-start.15
  63.1 1.8 %collective-permute-start.14 = (f32[64,128]{1,0:T(8,128)S(1)}, f32[64,128]{1,0:T(8,128)S(1)}, u32[]{:S(2)}, u32[]{:S(2)}) collective-permute-start(f32[64,128]{1,0:T(8,128)S(1)} %add.32), channel_id=1, source_target_pairs={{0,4},{4,0},{8,12},{12,8},{1,5},{5,1},{9,13},{13,9},{2,6},{6,2},{1... | collective-permute-start | bytes 98312 | tf_op jit(solution)/shard_map/ppermute | solution.py:420
  64.9 0.6 collective-permute-start.19
  65.5 0.7 collective-permute-done.16
  66.3 1.6 %collective-permute-done.15 = f32[64,128]{1,0:T(8,128)S(1)} collective-permute-done((f32[64,128]{1,0:T(8,128)S(1)}, f32[64,128]{1,0:T(8,128)S(1)}, u32[]{:S(2)}, u32[]{:S(2)}) %collective-permute-start.15) | collective-permute-done | bytes 32800 | tf_op jit(solution)/shard_map/ppermute | solution.py:420
  67.9 1.2 %collective-permute-done.17.got = f32[64,128]{1,0:T(8,128)S(1)} collective-permute-done((f32[64,128]{1,0:T(8,128)S(1)}, f32[64,128]{1,0:T(8,128)S(1)}, u32[]{:S(2)}, u32[]{:S(2)}) %collective-permute-start.17) | collective-permute-done | bytes 32800 | tf_op jit(solution)/shard_map/ppermute | solution.py:416
  69.1 5.1 %factorize.1 = (f32[64,128]{1,0:T(8,128)}, f32[64,128]{1,0:T(8,128)S(1)}) custom-call(s32[2]{0:T(128)S(1)} %pad_add_fusion.place, f32[64,128]{1,0:T(8,128)S(1)} %add_add_fusion.1.kept, f32[64,128]{1,0:T(8,128)S(1)} %collective-permute-done.17.got), custom_call_target="tpu_custom_call" | custom-call | flops 1000 | bytes 20000000 | tf_op jit(solution)/shard_map/factorize/pallas_call | solution.py:50
  74.2 0.2 collective-permute-start.18
  74.4 1.2 %collective-permute-done.18.passed = f32[64,512]{1,0:T(8,128)S(1)} collective-permute-done((f32[64,512]{1,0:T(8,128)S(1)}, f32[64,512]{1,0:T(8,128)S(1)}, u32[]{:S(2)}, u32[]{:S(2)}) %collective-permute-start.18) | collective-permute-done | bytes 131104 | tf_op jit(solution)/shard_map/ppermute | solution.py:416
  75.6 1.3 %own_columns.1 = f32[64,1024]{1,0:T(8,128)} custom-call(s32[2]{0:T(128)S(1)} %pad_add_fusion.place, f32[64,512]{1,0:T(8,128)S(1)} %get-tuple-element.60.own, f32[64,512]{1,0:T(8,128)S(1)} %collective-permute-done.6.theirs, f32[64,512]{1,0:T(8,128)S(1)} %collective-permute-done.18.passed), custom_call_target="tpu_custom_call" | custom-call | flops 1000 | bytes 1000 | tf_op jit(solution)/shard_map/own_columns/pallas_call | solution.py:50
  76.9 1.2 %collective-permute-done.19 = f16[128,1024]{1,0:T(8,128)(2,1)S(1)} collective-permute-done((f16[128,1024]{1,0:T(8,128)(2,1)S(1)}, f16[128,1024]{1,0:T(8,128)(2,1)S(1)}, u32[]{:S(2)}, u32[]{:S(2)}) %collective-permute-start.19) | collective-permute-done | bytes 262176 | tf_op jit(solution)/shard_map/ppermute | solution.py:416
  78.2 2.2 %new_basis.1 = f32[64,8192]{1,0:T(8,128)} custom-call(s32[2]{0:T(128)S(1)} %pad_add_fusion.place, f32[64,128]{1,0:T(8,128)S(1)} %get-tuple-element.90.weights, bf16[256,1024]{1,0:T(8,128)(2,1)S(1)} %get-tuple-element.91.refs_0_, bf16[256,1024]{1,0:T(8,128)(2,1)S(1)} %get-tuple-element.92.refs_1_, bf16[256,1024]{1,0:T(8,128)(2,1)S(1)} %get-tuple-element.93.refs_2_, ...), custom_call_target="tpu_custom_call" | custom-call | flops 1000 | bytes 1000 | tf_op jit(solution)/shard_map/new_basis/pallas_call | solution.py:400
  (32 shorter events, 1.1 us)
Async XLA Ops:
  0.6 8.8 %collective-permute-start = (bf16[64,256]{1,0:T(8,128)(2,1)}, bf16[64,256]{1,0:T(8,128)(2,1)S(1)}, u32[]{:S(2)}, u32[]{:S(2)}) collective-permute-start(bf16[64,256]{1,0:T(8,128)(2,1)} %points.1), channel_id=1, source_target_pairs={{0,2},{2,0},{1,3},{3,1},{4,6},{6,4},{5,7},{7,5},{8,10},{10,8},{9,1... | collective-permute-start | bytes 98312 | tf_op jit(solution)/shard_map/ppermute | solution.py:416
  12.8 1.4 %collective-permute-start.1 = (f32[64,512]{1,0:T(8,128)S(1)}, f32[64,512]{1,0:T(8,128)S(1)}, u32[]{:S(2)}, u32[]{:S(2)}) collective-permute-start(f32[64,512]{1,0:T(8,128)S(1)} %get-tuple-element.57), channel_id=1, source_target_pairs={{0,1},{1,0},{2,3},{3,2},{4,5},{5,4},{6,7},{7,6},{8,9},{9,8},{10,11... | collective-permute-start | bytes 393224 | tf_op jit(solution)/shard_map/ppermute | solution.py:416
  14.2 6.4 %collective-permute-start.4 = (f16[64,512]{1,0:T(8,128)(2,1)S(1)}, f16[64,512]{1,0:T(8,128)(2,1)S(1)}, u32[]{:S(2)}, u32[]{:S(2)}) collective-permute-start(f16[64,512]{1,0:T(8,128)(2,1)S(1)} %add_convert_fusion), channel_id=1, source_target_pairs={{0,12},{4,8},{8,4},{12,0},{1,13},{5,9},{9,5},{13,1},{2,14},{6,10},... | collective-permute-start | bytes 196616 | tf_op jit(solution)/shard_map/ppermute | solution.py:420
  17.9 5.9 %collective-permute-start.3 = (f16[64,512]{1,0:T(8,128)(2,1)S(1)}, f16[64,512]{1,0:T(8,128)(2,1)S(1)}, u32[]{:S(2)}, u32[]{:S(2)}) collective-permute-start(f16[64,512]{1,0:T(8,128)(2,1)S(1)} %add_convert_fusion), channel_id=1, source_target_pairs={{0,8},{4,12},{8,0},{12,4},{1,9},{5,13},{9,1},{13,5},{2,10},{6,14},... | collective-permute-start | bytes 196616 | tf_op jit(solution)/shard_map/ppermute | solution.py:420
  17.9 5.9 %collective-permute-start.2 = (f16[64,512]{1,0:T(8,128)(2,1)S(1)}, f16[64,512]{1,0:T(8,128)(2,1)S(1)}, u32[]{:S(2)}, u32[]{:S(2)}) collective-permute-start(f16[64,512]{1,0:T(8,128)(2,1)S(1)} %add_convert_fusion), channel_id=1, source_target_pairs={{0,4},{4,0},{8,12},{12,8},{1,5},{5,1},{9,13},{13,9},{2,6},{6,2},{1... | collective-permute-start | bytes 196616 | tf_op jit(solution)/shard_map/ppermute | solution.py:420
  23.9 1.4 %collective-permute-start.5 = (f32[64,512]{1,0:T(8,128)S(1)}, f32[64,512]{1,0:T(8,128)S(1)}, u32[]{:S(2)}, u32[]{:S(2)}) collective-permute-start(f32[64,512]{1,0:T(8,128)S(1)} %add_add_fusion.kept), channel_id=1, source_target_pairs={{0,1},{1,0},{2,3},{3,2},{4,5},{5,4},{6,7},{7,6},{8,9},{9,8},{10,11... | collective-permute-start | bytes 393224 | tf_op jit(solution)/shard_map/ppermute | solution.py:416
  23.9 9.9 %collective-permute-start.6 = (f32[64,512]{1,0:T(8,128)S(1)}, f32[64,512]{1,0:T(8,128)S(1)}, u32[]{:S(2)}, u32[]{:S(2)}) collective-permute-start(f32[64,512]{1,0:T(8,128)S(1)} %add_add_fusion.kept), channel_id=1, source_target_pairs={{1,3},{3,1},{5,7},{7,5},{9,11},{11,9},{13,15},{15,13},{17,19},{19,... | collective-permute-start | bytes 393224 | tf_op jit(solution)/shard_map/ppermute | solution.py:448
  26.3 11.6 %collective-permute-start.10 = (f16[128,1024]{1,0:T(8,128)(2,1)S(1)}, f16[128,1024]{1,0:T(8,128)(2,1)S(1)}, u32[]{:S(2)}, u32[]{:S(2)}) collective-permute-start(f16[128,1024]{1,0:T(8,128)(2,1)S(1)} %convert_element_type.68), channel_id=1, source_target_pairs={{0,2},{2,0},{1,3},{3,1},{4,6},{6,4},{5,7},{7,5},{8,10},{10,8},{9,1... | collective-permute-start | bytes 786440 | tf_op jit(solution)/shard_map/ppermute | solution.py:416
  28.0 13.2 %collective-permute-start.9 = (f16[128,1024]{1,0:T(8,128)(2,1)S(1)}, f16[128,1024]{1,0:T(8,128)(2,1)S(1)}, u32[]{:S(2)}, u32[]{:S(2)}) collective-permute-start(f16[128,1024]{1,0:T(8,128)(2,1)S(1)} %convert_element_type.66), channel_id=1, source_target_pairs={{0,2},{2,0},{1,3},{3,1},{4,6},{6,4},{5,7},{7,5},{8,10},{10,8},{9,1... | collective-permute-start | bytes 786440 | tf_op jit(solution)/shard_map/ppermute | solution.py:416
  30.6 16.2 %collective-permute-start.8 = (f16[128,1024]{1,0:T(8,128)(2,1)S(1)}, f16[128,1024]{1,0:T(8,128)(2,1)S(1)}, u32[]{:S(2)}, u32[]{:S(2)}) collective-permute-start(f16[128,1024]{1,0:T(8,128)(2,1)S(1)} %convert_element_type.64), channel_id=1, source_target_pairs={{0,2},{2,0},{1,3},{3,1},{4,6},{6,4},{5,7},{7,5},{8,10},{10,8},{9,1... | collective-permute-start | bytes 786440 | tf_op jit(solution)/shard_map/ppermute | solution.py:416
  32.3 20.2 %collective-permute-start.7 = (f16[128,1024]{1,0:T(8,128)(2,1)S(1)}, f16[128,1024]{1,0:T(8,128)(2,1)S(1)}, u32[]{:S(2)}, u32[]{:S(2)}) collective-permute-start(f16[128,1024]{1,0:T(8,128)(2,1)S(1)} %convert_element_type.62), channel_id=1, source_target_pairs={{0,2},{2,0},{1,3},{3,1},{4,6},{6,4},{5,7},{7,5},{8,10},{10,8},{9,1... | collective-permute-start | bytes 786440 | tf_op jit(solution)/shard_map/ppermute | solution.py:416
  34.9 23.2 %collective-permute-start.13 = (f16[128,1024]{1,0:T(8,128)(2,1)S(1)}, f16[128,1024]{1,0:T(8,128)(2,1)S(1)}, u32[]{:S(2)}, u32[]{:S(2)}) collective-permute-start(f16[128,1024]{1,0:T(8,128)(2,1)S(1)} %convert_element_type.72), channel_id=1, source_target_pairs={{0,2},{2,0},{1,3},{3,1},{4,6},{6,4},{5,7},{7,5},{8,10},{10,8},{9,1... | collective-permute-start | bytes 786440 | tf_op jit(solution)/shard_map/ppermute | solution.py:416
  53.5 1.7 %collective-permute-start.11 = (f32[64,128]{1,0:T(8,128)S(1)}, f32[64,128]{1,0:T(8,128)S(1)}, u32[]{:S(2)}, u32[]{:S(2)}) collective-permute-start(f32[64,128]{1,0:T(8,128)S(1)} %get-tuple-element.77), channel_id=1, source_target_pairs={{0,1},{1,0},{2,3},{3,2},{4,5},{5,4},{6,7},{7,6},{8,9},{9,8},{10,11... | collective-permute-start | bytes 98312 | tf_op jit(solution)/shard_map/ppermute | solution.py:416
  55.2 3.9 %collective-permute-start.12 = (f32[64,128]{1,0:T(8,128)S(1)}, f32[64,128]{1,0:T(8,128)S(1)}, u32[]{:S(2)}, u32[]{:S(2)}) collective-permute-start(f32[64,128]{1,0:T(8,128)S(1)} %add.31), channel_id=1, source_target_pairs={{0,2},{2,0},{1,3},{3,1},{4,6},{6,4},{5,7},{7,5},{8,10},{10,8},{9,1... | collective-permute-start | bytes 98312 | tf_op jit(solution)/shard_map/ppermute | solution.py:416
  59.1 19.0 %collective-permute-start.20 = (f16[128,2048]{1,0:T(8,128)(2,1)S(1)}, f16[128,2048]{1,0:T(8,128)(2,1)S(1)}, u32[]{:S(2)}, u32[]{:S(2)}) collective-permute-start(f16[128,2048]{1,0:T(8,128)(2,1)S(1)} %convert_element_type.71), channel_id=1, source_target_pairs={{0,2},{2,0},{1,3},{3,1},{4,6},{6,4},{5,7},{7,5},{8,10},{10,8},{9,1... | collective-permute-start | bytes 1572872 | tf_op jit(solution)/shard_map/ppermute | solution.py:416
  60.5 5.7 %collective-permute-start.16 = (f32[64,128]{1,0:T(8,128)S(1)}, f32[64,128]{1,0:T(8,128)S(1)}, u32[]{:S(2)}, u32[]{:S(2)}) collective-permute-start(f32[64,128]{1,0:T(8,128)S(1)} %add.32), channel_id=1, source_target_pairs={{0,12},{4,8},{8,4},{12,0},{1,13},{5,9},{9,5},{13,1},{2,14},{6,10},... | collective-permute-start | bytes 98312 | tf_op jit(solution)/shard_map/ppermute | solution.py:420
  63.0 4.8 %collective-permute-start.15 = (f32[64,128]{1,0:T(8,128)S(1)}, f32[64,128]{1,0:T(8,128)S(1)}, u32[]{:S(2)}, u32[]{:S(2)}) collective-permute-start(f32[64,128]{1,0:T(8,128)S(1)} %add.32), channel_id=1, source_target_pairs={{0,8},{4,12},{8,0},{12,4},{1,9},{5,13},{9,1},{13,5},{2,10},{6,14},... | collective-permute-start | bytes 98312 | tf_op jit(solution)/shard_map/ppermute | solution.py:420
  63.1 4.7 %collective-permute-start.14 = (f32[64,128]{1,0:T(8,128)S(1)}, f32[64,128]{1,0:T(8,128)S(1)}, u32[]{:S(2)}, u32[]{:S(2)}) collective-permute-start(f32[64,128]{1,0:T(8,128)S(1)} %add.32), channel_id=1, source_target_pairs={{0,4},{4,0},{8,12},{12,8},{1,5},{5,1},{9,13},{13,9},{2,6},{6,2},{1... | collective-permute-start | bytes 98312 | tf_op jit(solution)/shard_map/ppermute | solution.py:420
  64.9 13.1 %collective-permute-start.19 = (f16[128,1024]{1,0:T(8,128)(2,1)S(1)}, f16[128,1024]{1,0:T(8,128)(2,1)S(1)}, u32[]{:S(2)}, u32[]{:S(2)}) collective-permute-start(f16[128,1024]{1,0:T(8,128)(2,1)S(1)} %convert_element_type.70), channel_id=1, source_target_pairs={{0,2},{2,0},{1,3},{3,1},{4,6},{6,4},{5,7},{7,5},{8,10},{10,8},{9,1... | collective-permute-start | bytes 786440 | tf_op jit(solution)/shard_map/ppermute | solution.py:416
  67.8 1.3 %collective-permute-start.17 = (f32[64,128]{1,0:T(8,128)S(1)}, f32[64,128]{1,0:T(8,128)S(1)}, u32[]{:S(2)}, u32[]{:S(2)}) collective-permute-start(f32[64,128]{1,0:T(8,128)S(1)} %add_add_fusion.1.kept), channel_id=1, source_target_pairs={{0,1},{1,0},{2,3},{3,2},{4,5},{5,4},{6,7},{7,6},{8,9},{9,8},{10,11... | collective-permute-start | bytes 98312 | tf_op jit(solution)/shard_map/ppermute | solution.py:416
  74.2 1.3 %collective-permute-start.18 = (f32[64,512]{1,0:T(8,128)S(1)}, f32[64,512]{1,0:T(8,128)S(1)}, u32[]{:S(2)}, u32[]{:S(2)}) collective-permute-start(f32[64,512]{1,0:T(8,128)S(1)} %collective-permute-done.6.theirs), channel_id=1, source_target_pairs={{0,1},{1,0},{2,3},{3,2},{4,5},{5,4},{6,7},{7,6},{8,9},{9,8},{10,11... | collective-permute-start | bytes 393224 | tf_op jit(solution)/shard_map/ppermute | solution.py:416

commit v6 on v4

--- a/solution.py
+++ b/solution.py
@@ -11,21 +11,17 @@
 
 COS = (
     0.9999999889369959,
-    -0.4999998901135819,
-    0.041666488148010265,
-    -0.0013887798934755957,
-    2.4769791619676175e-05,
-    -2.7078195310289617e-07,
-    1.7242244242579268e-09,
+    -19.739204464036813,
+    64.93911579322743,
+    -85.4501108378944,
+    60.16740762749498,
+    -25.966798028642813,
+    6.527580149233599,
 )
-TURN_HEAD = 6.28125
-TURN_REST = 0.0019353071795864769
-
-
 def cosine(x):
-    turns = jnp.round(x * 0.15915494309189535)
-    x = (x - turns * TURN_HEAD) - turns * TURN_REST
-    t = x * x
+    turns = x * 0.15915494309189535
+    t = turns - jnp.round(turns)
+    t = t * t
     y = COS[-1]
     for c in COS[-2::-1]:
         y = y * t + c

time: 80.9 us -> 80.7 us (level)
  no operation moved by 1% of the time
where the time goes in v6:
time: 80.7 us; the launch traced here: 80.6 us
  waiting for transfers between devices  29.2 us (36%)
  Pallas kernels  27.3 us (34%)
  starting transfers between devices  22.3 us (28%)
  between operations  1.09 us (1%)
    ppermute x14, waiting for transfers between devices, swap(): return lax.ppermute(x, axis, [(0, 1), (1, 0)])  21.8 us
    pallas_call x16, Pallas kernels, call(): pl.pallas_call(kernel, in_specs=[smem] * scalars + [vmem] * (len(args) -...  19.4 us
    ppermute x14, starting transfers between devices, swap(): return lax.ppermute(x, axis, [(0, 1), (1, 0)])  12.6 us
    ppermute x6, starting transfers between devices, sum_over(): lax.ppermute(x, axis, [(i, i ^ m) for i in range(size)])  8.84 us
    ppermute x6, waiting for transfers between devices, sum_over(): lax.ppermute(x, axis, [(i, i ^ m) for i in range(size)])  7.41 us
    pallas_call x1, Pallas kernels, own_coefs(): pl.pallas_call(kernel, in_specs=[hbm] * 4, out_specs=[vmem] * 5, out_shap...  5.71 us
    pallas_call x1, Pallas kernels, new_columns(): pl.pallas_call(kernel, in_specs=[pl.BlockSpec(memory_space=pltpu.SMEM)] +...  2.16 us
  transfers between devices with their start and end apart: 21, of which 15 were waited for; matrix products, arithmetic and copies ran while one was open for 1% of the time, Pallas kernels for 27%

profile of v6, /device:TPU:0, one launch (start us, length us, event | category | flops | bytes accessed | tf_op | source)
XLA Modules:
  0.0 80.6 jit_solution(4701643213200414943)
XLA Ops:
  0.6 3.0 %collective-permute-start = (bf16[64,256]{1,0:T(8,128)(2,1)}, bf16[64,256]{1,0:T(8,128)(2,1)S(1)}, u32[]{:S(2)}, u32[]{:S(2)}) collective-permute-start(bf16[64,256]{1,0:T(8,128)(2,1)} %points.1), channel_id=1, source_target_pairs={{0,2},{2,0},{1,3},{3,1},{4,6},{6,4},{5,7},{7,5},{8,10},{10,8},{9,1... | collective-permute-start | bytes 98312 | tf_op jit(solution)/shard_map/ppermute | solution.py:439
  3.7 5.7 %own_coefs.1 = (f32[64,8192]{1,0:T(8,128)S(1)}, f32[64,512]{1,0:T(8,128)S(1)}, bf16[256,8192]{1,0:T(8,128)(2,1)S(1)}, f32[1,8192]{1,0:T(1,128)S(1)}, bf16[8192,512]{1,0:T(8,128)(2,1)S(1)}) custom-call(bf16[64,256]{1,0:T(8,128)(2,1)} %points.1, bf16[256,8192]{1,0:T(8,128)(2,1)} %freqs.1, f32[1,8192]{1,0:T(1,128)} %bitcast.7, bf16[8192,512]{1,0:T(8,128)(2,1)} %basis.1), custom_call_target="tpu_custom_call" | custom-call | flops 1000 | bytes 1000 | tf_op jit(solution)/shard_map/own_coefs/pallas_call | solution.py:110
  9.4 3.4 %other_coefs.1 = (f32[64,8192]{1,0:T(8,128)S(1)}, f32[64,512]{1,0:T(8,128)S(1)}, f32[64,512]{1,0:T(8,128)S(1)}) custom-call(s32[2]{0:T(128)S(1)} %pad_add_fusion.place, bf16[64,256]{1,0:T(8,128)(2,1)S(1)} %collective-permute-done.points, bf16[256,8192]{1,0:T(8,128)(2,1)S(1)} %get-tuple-element.52.freqs, f32[1,8192]{1,0:T(1,128)S(1)} %get-tuple-element.53.phases, ...), custom_call_target="tpu_custom_call" | custom-call | flops 1000 | bytes 1000 | tf_op jit(solution)/shard_map/other_coefs/pallas_call | solution.py:50
  12.9 1.3 %collective-permute-done.1 = f32[64,512]{1,0:T(8,128)S(1)} collective-permute-done((f32[64,512]{1,0:T(8,128)S(1)}, f32[64,512]{1,0:T(8,128)S(1)}, u32[]{:S(2)}, u32[]{:S(2)}) %collective-permute-start.1) | collective-permute-done | bytes 131104 | tf_op jit(solution)/shard_map/ppermute | solution.py:439
  14.2 3.7 %collective-permute-start.4 = (f16[64,512]{1,0:T(8,128)(2,1)S(1)}, f16[64,512]{1,0:T(8,128)(2,1)S(1)}, u32[]{:S(2)}, u32[]{:S(2)}) collective-permute-start(f16[64,512]{1,0:T(8,128)(2,1)S(1)} %add_convert_fusion), channel_id=1, source_target_pairs={{0,12},{4,8},{8,4},{12,0},{1,13},{5,9},{9,5},{13,1},{2,14},{6,10},... | collective-permute-start | bytes 196616 | tf_op jit(solution)/shard_map/ppermute | solution.py:443
  17.9 0.8 collective-permute-start.2
  18.7 1.9 %collective-permute-done.4 = f16[64,512]{1,0:T(8,128)(2,1)S(1)} collective-permute-done((f16[64,512]{1,0:T(8,128)(2,1)S(1)}, f16[64,512]{1,0:T(8,128)(2,1)S(1)}, u32[]{:S(2)}, u32[]{:S(2)}) %collective-permute-start.4) | collective-permute-done | bytes 65568 | tf_op jit(solution)/shard_map/ppermute | solution.py:443
  20.6 3.2 %collective-permute-done.3 = f16[64,512]{1,0:T(8,128)(2,1)S(1)} collective-permute-done((f16[64,512]{1,0:T(8,128)(2,1)S(1)}, f16[64,512]{1,0:T(8,128)(2,1)S(1)}, u32[]{:S(2)}, u32[]{:S(2)}) %collective-permute-start.3) | collective-permute-done | bytes 65568 | tf_op jit(solution)/shard_map/ppermute | solution.py:443
  23.9 0.8 %collective-permute-start.6 = (f32[64,512]{1,0:T(8,128)S(1)}, f32[64,512]{1,0:T(8,128)S(1)}, u32[]{:S(2)}, u32[]{:S(2)}) collective-permute-start(f32[64,512]{1,0:T(8,128)S(1)} %add_add_fusion.kept), channel_id=1, source_target_pairs={{1,3},{3,1},{5,7},{7,5},{9,11},{11,9},{13,15},{15,13},{17,19},{19,... | collective-permute-start | bytes 393224 | tf_op jit(solution)/shard_map/ppermute | solution.py:471
  24.8 0.5 collective-permute-done.5.got
  25.3 1.0 %first_fit.1 = (f32[128,1024]{1,0:T(8,128)S(1)}, f32[128,1024]{1,0:T(8,128)S(1)}, f32[64,512]{1,0:T(8,128)S(1)}, bf16[256,512]{1,0:T(8,128)(2,1)S(1)}) custom-call(s32[2]{0:T(128)S(1)} %pad_add_fusion.place, f32[64,512]{1,0:T(8,128)S(1)} %add_add_fusion.kept, f32[64,512]{1,0:T(8,128)S(1)} %collective-permute-done.5.got, ...), custom_call_target="tpu_custom_call" | custom-call | flops 1000 | bytes 1000 | tf_op jit(solution)/shard_map/first_fit/pallas_call | solution.py:50
  26.3 0.6 collective-permute-start.10
  26.9 1.0 %fit.10 = (f32[128,1024]{1,0:T(8,128)S(1)}, f32[128,1024]{1,0:T(8,128)S(1)}) custom-call(s32[2]{0:T(128)S(1)} %pad_add_fusion.place, bf16[256,512]{1,0:T(8,128)(2,1)S(1)} %get-tuple-element.62.parts, f32[64,8192]{1,0:T(8,128)S(1)} %get-tuple-element.58.feats_a, f32[64,8192]{1,0:T(8,128)S(1)} %get-tuple-element.59.feats_b, ...), custom_call_target="tpu_custom_call" | custom-call | flops 1000 | bytes 1000 | tf_op jit(solution)/shard_map/fit/pallas_call | solution.py:50
  28.0 1.6 %collective-permute-start.9 = (f16[128,1024]{1,0:T(8,128)(2,1)S(1)}, f16[128,1024]{1,0:T(8,128)(2,1)S(1)}, u32[]{:S(2)}, u32[]{:S(2)}) collective-permute-start(f16[128,1024]{1,0:T(8,128)(2,1)S(1)} %convert_element_type.66), channel_id=1, source_target_pairs={{0,2},{2,0},{1,3},{3,1},{4,6},{6,4},{5,7},{7,5},{8,10},{10,8},{9,1... | collective-permute-start | bytes 786440 | tf_op jit(solution)/shard_map/ppermute | solution.py:439
  29.6 1.0 %fit.8 = (f32[128,1024]{1,0:T(8,128)S(1)}, f32[128,1024]{1,0:T(8,128)S(1)}) custom-call(s32[2]{0:T(128)S(1)} %pad_add_fusion.place, bf16[256,512]{1,0:T(8,128)(2,1)S(1)} %get-tuple-element.62.parts, f32[64,8192]{1,0:T(8,128)S(1)} %get-tuple-element.58.feats_a, f32[64,8192]{1,0:T(8,128)S(1)} %get-tuple-element.59.feats_b, ...), custom_call_target="tpu_custom_call" | custom-call | flops 1000 | bytes 1000 | tf_op jit(solution)/shard_map/fit/pallas_call | solution.py:50
  30.6 0.6 collective-permute-start.8
  31.2 1.0 %fit.7 = (f32[128,1024]{1,0:T(8,128)S(1)}, f32[128,1024]{1,0:T(8,128)S(1)}) custom-call(s32[2]{0:T(128)S(1)} %pad_add_fusion.place, bf16[256,512]{1,0:T(8,128)(2,1)S(1)} %get-tuple-element.62.parts, f32[64,8192]{1,0:T(8,128)S(1)} %get-tuple-element.58.feats_a, f32[64,8192]{1,0:T(8,128)S(1)} %get-tuple-element.59.feats_b, ...), custom_call_target="tpu_custom_call" | custom-call | flops 1000 | bytes 1000 | tf_op jit(solution)/shard_map/fit/pallas_call | solution.py:50
  32.3 1.6 %collective-permute-start.7 = (f16[128,1024]{1,0:T(8,128)(2,1)S(1)}, f16[128,1024]{1,0:T(8,128)(2,1)S(1)}, u32[]{:S(2)}, u32[]{:S(2)}) collective-permute-start(f16[128,1024]{1,0:T(8,128)(2,1)S(1)} %convert_element_type.62), channel_id=1, source_target_pairs={{0,2},{2,0},{1,3},{3,1},{4,6},{6,4},{5,7},{7,5},{8,10},{10,8},{9,1... | collective-permute-start | bytes 786440 | tf_op jit(solution)/shard_map/ppermute | solution.py:439
  33.8 1.0 %fit.11 = (f32[128,1024]{1,0:T(8,128)S(1)}, f32[128,1024]{1,0:T(8,128)S(1)}) custom-call(s32[2]{0:T(128)S(1)} %pad_add_fusion.place, bf16[256,512]{1,0:T(8,128)(2,1)S(1)} %get-tuple-element.62.parts, f32[64,8192]{1,0:T(8,128)S(1)} %get-tuple-element.58.feats_a, f32[64,8192]{1,0:T(8,128)S(1)} %get-tuple-element.59.feats_b, ...), custom_call_target="tpu_custom_call" | custom-call | flops 1000 | bytes 1000 | tf_op jit(solution)/shard_map/fit/pallas_call | solution.py:50
  34.9 0.6 collective-permute-start.13
  35.5 1.0 %fit.9 = (f32[128,1024]{1,0:T(8,128)S(1)}, f32[128,1024]{1,0:T(8,128)S(1)}) custom-call(s32[2]{0:T(128)S(1)} %pad_add_fusion.place, bf16[256,512]{1,0:T(8,128)(2,1)S(1)} %get-tuple-element.62.parts, f32[64,8192]{1,0:T(8,128)S(1)} %get-tuple-element.58.feats_a, f32[64,8192]{1,0:T(8,128)S(1)} %get-tuple-element.59.feats_b, ...), custom_call_target="tpu_custom_call" | custom-call | flops 1000 | bytes 1000 | tf_op jit(solution)/shard_map/fit/pallas_call | solution.py:50
  36.5 1.3 %fit.6 = (f32[128,2048]{1,0:T(8,128)S(1)}, f32[128,2048]{1,0:T(8,128)S(1)}) custom-call(s32[2]{0:T(128)S(1)} %pad_add_fusion.place, bf16[256,512]{1,0:T(8,128)(2,1)S(1)} %get-tuple-element.62.parts, f32[64,8192]{1,0:T(8,128)S(1)} %get-tuple-element.58.feats_a, f32[64,8192]{1,0:T(8,128)S(1)} %get-tuple-element.59.feats_b, ...), custom_call_target="tpu_custom_call" | custom-call | flops 1000 | bytes 1000 | tf_op jit(solution)/shard_map/fit/pallas_call | solution.py:50
  38.0 0.4 gram.3
  38.4 2.8 %collective-permute-done.9 = f16[128,1024]{1,0:T(8,128)(2,1)S(1)} collective-permute-done((f16[128,1024]{1,0:T(8,128)(2,1)S(1)}, f16[128,1024]{1,0:T(8,128)(2,1)S(1)}, u32[]{:S(2)}, u32[]{:S(2)}) %collective-permute-start.9) | collective-permute-done | bytes 262176 | tf_op jit(solution)/shard_map/ppermute | solution.py:439
  41.2 0.4 gram.4
  41.6 5.2 %collective-permute-done.8 = f16[128,1024]{1,0:T(8,128)(2,1)S(1)} collective-permute-done((f16[128,1024]{1,0:T(8,128)(2,1)S(1)}, f16[128,1024]{1,0:T(8,128)(2,1)S(1)}, u32[]{:S(2)}, u32[]{:S(2)}) %collective-permute-start.8) | collective-permute-done | bytes 262176 | tf_op jit(solution)/shard_map/ppermute | solution.py:439
  46.9 0.4 gram.5
  47.2 5.2 %collective-permute-done.7 = f16[128,1024]{1,0:T(8,128)(2,1)S(1)} collective-permute-done((f16[128,1024]{1,0:T(8,128)(2,1)S(1)}, f16[128,1024]{1,0:T(8,128)(2,1)S(1)}, u32[]{:S(2)}, u32[]{:S(2)}) %collective-permute-start.7) | collective-permute-done | bytes 262176 | tf_op jit(solution)/shard_map/ppermute | solution.py:439
  52.5 1.0 %gram_halves.1 = (bf16[256,1024]{1,0:T(8,128)(2,1)S(1)}, f32[64,128]{1,0:T(8,128)S(1)}, f32[64,128]{1,0:T(8,128)S(1)}) custom-call(s32[2]{0:T(128)S(1)} %pad_add_fusion.place, f32[128,2048]{1,0:T(8,128)S(1)} %get-tuple-element.63.refs_0_, f32[128,1024]{1,0:T(8,128)S(1)} %convert_element_type.63.refs_1_, f32[256,256]{1,0:T(8,128)S(1)} %get-tuple-element.75.refs_2_), custom_call_target="tpu_custom_call" | custom-call | flops 1000 | bytes 1000 | tf_op jit(solution)/shard_map/gram_halves/pallas_call | solution.py:50
  53.5 0.9 %collective-permute-start.11 = (f32[64,128]{1,0:T(8,128)S(1)}, f32[64,128]{1,0:T(8,128)S(1)}, u32[]{:S(2)}, u32[]{:S(2)}) collective-permute-start(f32[64,128]{1,0:T(8,128)S(1)} %get-tuple-element.77), channel_id=1, source_target_pairs={{0,1},{1,0},{2,3},{3,2},{4,5},{5,4},{6,7},{7,6},{8,9},{9,8},{10,11... | collective-permute-start | bytes 98312 | tf_op jit(solution)/shard_map/ppermute | solution.py:439
  54.3 0.9 %collective-permute-done.11 = f32[64,128]{1,0:T(8,128)S(1)} collective-permute-done((f32[64,128]{1,0:T(8,128)S(1)}, f32[64,128]{1,0:T(8,128)S(1)}, u32[]{:S(2)}, u32[]{:S(2)}) %collective-permute-start.11) | collective-permute-done | bytes 32800 | tf_op jit(solution)/shard_map/ppermute | solution.py:439
  55.2 1.4 %collective-permute-start.12 = (f32[64,128]{1,0:T(8,128)S(1)}, f32[64,128]{1,0:T(8,128)S(1)}, u32[]{:S(2)}, u32[]{:S(2)}) collective-permute-start(f32[64,128]{1,0:T(8,128)S(1)} %add.31), channel_id=1, source_target_pairs={{0,2},{2,0},{1,3},{3,1},{4,6},{6,4},{5,7},{7,5},{8,10},{10,8},{9,1... | collective-permute-start | bytes 98312 | tf_op jit(solution)/shard_map/ppermute | solution.py:439
  56.6 1.4 %collective-permute-done.13 = f16[128,1024]{1,0:T(8,128)(2,1)S(1)} collective-permute-done((f16[128,1024]{1,0:T(8,128)(2,1)S(1)}, f16[128,1024]{1,0:T(8,128)(2,1)S(1)}, u32[]{:S(2)}, u32[]{:S(2)}) %collective-permute-start.13) | collective-permute-done | bytes 262176 | tf_op jit(solution)/shard_map/ppermute | solution.py:439
  58.2 0.9 %collective-permute-done.12 = f32[64,128]{1,0:T(8,128)S(1)} collective-permute-done((f32[64,128]{1,0:T(8,128)S(1)}, f32[64,128]{1,0:T(8,128)S(1)}, u32[]{:S(2)}, u32[]{:S(2)}) %collective-permute-start.12) | collective-permute-done | bytes 32800 | tf_op jit(solution)/shard_map/ppermute | solution.py:439
  59.1 1.4 %collective-permute-start.20 = (f16[128,2048]{1,0:T(8,128)(2,1)S(1)}, f16[128,2048]{1,0:T(8,128)(2,1)S(1)}, u32[]{:S(2)}, u32[]{:S(2)}) collective-permute-start(f16[128,2048]{1,0:T(8,128)(2,1)S(1)} %convert_element_type.71), channel_id=1, source_target_pairs={{0,2},{2,0},{1,3},{3,1},{4,6},{6,4},{5,7},{7,5},{8,10},{10,8},{9,1... | collective-permute-start | bytes 1572872 | tf_op jit(solution)/shard_map/ppermute | solution.py:439
  60.5 2.5 %collective-permute-start.16 = (f32[64,128]{1,0:T(8,128)S(1)}, f32[64,128]{1,0:T(8,128)S(1)}, u32[]{:S(2)}, u32[]{:S(2)}) collective-permute-start(f32[64,128]{1,0:T(8,128)S(1)} %add.32), channel_id=1, source_target_pairs={{0,12},{4,8},{8,4},{12,0},{1,13},{5,9},{9,5},{13,1},{2,14},{6,10},... | collective-permute-start | bytes 98312 | tf_op jit(solution)/shard_map/ppermute | solution.py:443
  63.0 0.1 collective-permute-start.15
  63.1 1.8 %collective-permute-start.14 = (f32[64,128]{1,0:T(8,128)S(1)}, f32[64,128]{1,0:T(8,128)S(1)}, u32[]{:S(2)}, u32[]{:S(2)}) collective-permute-start(f32[64,128]{1,0:T(8,128)S(1)} %add.32), channel_id=1, source_target_pairs={{0,4},{4,0},{8,12},{12,8},{1,5},{5,1},{9,13},{13,9},{2,6},{6,2},{1... | collective-permute-start | bytes 98312 | tf_op jit(solution)/shard_map/ppermute | solution.py:443
  64.9 0.6 collective-permute-start.19
  65.5 0.7 collective-permute-done.16
  66.3 1.6 %collective-permute-done.15 = f32[64,128]{1,0:T(8,128)S(1)} collective-permute-done((f32[64,128]{1,0:T(8,128)S(1)}, f32[64,128]{1,0:T(8,128)S(1)}, u32[]{:S(2)}, u32[]{:S(2)}) %collective-permute-start.15) | collective-permute-done | bytes 32800 | tf_op jit(solution)/shard_map/ppermute | solution.py:443
  67.9 1.2 %collective-permute-done.17.got = f32[64,128]{1,0:T(8,128)S(1)} collective-permute-done((f32[64,128]{1,0:T(8,128)S(1)}, f32[64,128]{1,0:T(8,128)S(1)}, u32[]{:S(2)}, u32[]{:S(2)}) %collective-permute-start.17) | collective-permute-done | bytes 32800 | tf_op jit(solution)/shard_map/ppermute | solution.py:439
  69.1 5.1 %factorize.1 = (f32[64,128]{1,0:T(8,128)}, f32[64,128]{1,0:T(8,128)S(1)}) custom-call(s32[2]{0:T(128)S(1)} %pad_add_fusion.place, f32[64,128]{1,0:T(8,128)S(1)} %add_add_fusion.1.kept, f32[64,128]{1,0:T(8,128)S(1)} %collective-permute-done.17.got), custom_call_target="tpu_custom_call" | custom-call | flops 1000 | bytes 20000000 | tf_op jit(solution)/shard_map/factorize/pallas_call | solution.py:50
  74.2 0.2 collective-permute-start.18
  74.4 1.2 %collective-permute-done.18.passed = f32[64,512]{1,0:T(8,128)S(1)} collective-permute-done((f32[64,512]{1,0:T(8,128)S(1)}, f32[64,512]{1,0:T(8,128)S(1)}, u32[]{:S(2)}, u32[]{:S(2)}) %collective-permute-start.18) | collective-permute-done | bytes 131104 | tf_op jit(solution)/shard_map/ppermute | solution.py:439
  75.6 1.3 %own_columns.1 = f32[64,1024]{1,0:T(8,128)} custom-call(s32[2]{0:T(128)S(1)} %pad_add_fusion.place, f32[64,512]{1,0:T(8,128)S(1)} %get-tuple-element.60.own, f32[64,512]{1,0:T(8,128)S(1)} %collective-permute-done.6.theirs, f32[64,512]{1,0:T(8,128)S(1)} %collective-permute-done.18.passed), custom_call_target="tpu_custom_call" | custom-call | flops 1000 | bytes 1000 | tf_op jit(solution)/shard_map/own_columns/pallas_call | solution.py:50
  76.9 1.2 %collective-permute-done.19 = f16[128,1024]{1,0:T(8,128)(2,1)S(1)} collective-permute-done((f16[128,1024]{1,0:T(8,128)(2,1)S(1)}, f16[128,1024]{1,0:T(8,128)(2,1)S(1)}, u32[]{:S(2)}, u32[]{:S(2)}) %collective-permute-start.19) | collective-permute-done | bytes 262176 | tf_op jit(solution)/shard_map/ppermute | solution.py:439
  78.2 2.2 %new_basis.1 = f32[64,8192]{1,0:T(8,128)} custom-call(s32[2]{0:T(128)S(1)} %pad_add_fusion.place, f32[64,128]{1,0:T(8,128)S(1)} %get-tuple-element.90.weights, bf16[256,1024]{1,0:T(8,128)(2,1)S(1)} %get-tuple-element.91.refs_0_, bf16[256,1024]{1,0:T(8,128)(2,1)S(1)} %get-tuple-element.92.refs_1_, bf16[256,1024]{1,0:T(8,128)(2,1)S(1)} %get-tuple-element.93.refs_2_, ...), custom_call_target="tpu_custom_call" | custom-call | flops 1000 | bytes 1000 | tf_op jit(solution)/shard_map/new_basis/pallas_call | solution.py:423
  (32 shorter events, 1.1 us)
Async XLA Ops:
  0.6 8.8 %collective-permute-start = (bf16[64,256]{1,0:T(8,128)(2,1)}, bf16[64,256]{1,0:T(8,128)(2,1)S(1)}, u32[]{:S(2)}, u32[]{:S(2)}) collective-permute-start(bf16[64,256]{1,0:T(8,128)(2,1)} %points.1), channel_id=1, source_target_pairs={{0,2},{2,0},{1,3},{3,1},{4,6},{6,4},{5,7},{7,5},{8,10},{10,8},{9,1... | collective-permute-start | bytes 98312 | tf_op jit(solution)/shard_map/ppermute | solution.py:439
  12.8 1.4 %collective-permute-start.1 = (f32[64,512]{1,0:T(8,128)S(1)}, f32[64,512]{1,0:T(8,128)S(1)}, u32[]{:S(2)}, u32[]{:S(2)}) collective-permute-start(f32[64,512]{1,0:T(8,128)S(1)} %get-tuple-element.57), channel_id=1, source_target_pairs={{0,1},{1,0},{2,3},{3,2},{4,5},{5,4},{6,7},{7,6},{8,9},{9,8},{10,11... | collective-permute-start | bytes 393224 | tf_op jit(solution)/shard_map/ppermute | solution.py:439
  14.2 6.4 %collective-permute-start.4 = (f16[64,512]{1,0:T(8,128)(2,1)S(1)}, f16[64,512]{1,0:T(8,128)(2,1)S(1)}, u32[]{:S(2)}, u32[]{:S(2)}) collective-permute-start(f16[64,512]{1,0:T(8,128)(2,1)S(1)} %add_convert_fusion), channel_id=1, source_target_pairs={{0,12},{4,8},{8,4},{12,0},{1,13},{5,9},{9,5},{13,1},{2,14},{6,10},... | collective-permute-start | bytes 196616 | tf_op jit(solution)/shard_map/ppermute | solution.py:443
  17.9 5.9 %collective-permute-start.3 = (f16[64,512]{1,0:T(8,128)(2,1)S(1)}, f16[64,512]{1,0:T(8,128)(2,1)S(1)}, u32[]{:S(2)}, u32[]{:S(2)}) collective-permute-start(f16[64,512]{1,0:T(8,128)(2,1)S(1)} %add_convert_fusion), channel_id=1, source_target_pairs={{0,8},{4,12},{8,0},{12,4},{1,9},{5,13},{9,1},{13,5},{2,10},{6,14},... | collective-permute-start | bytes 196616 | tf_op jit(solution)/shard_map/ppermute | solution.py:443
  17.9 5.9 %collective-permute-start.2 = (f16[64,512]{1,0:T(8,128)(2,1)S(1)}, f16[64,512]{1,0:T(8,128)(2,1)S(1)}, u32[]{:S(2)}, u32[]{:S(2)}) collective-permute-start(f16[64,512]{1,0:T(8,128)(2,1)S(1)} %add_convert_fusion), channel_id=1, source_target_pairs={{0,4},{4,0},{8,12},{12,8},{1,5},{5,1},{9,13},{13,9},{2,6},{6,2},{1... | collective-permute-start | bytes 196616 | tf_op jit(solution)/shard_map/ppermute | solution.py:443
  23.9 1.4 %collective-permute-start.5 = (f32[64,512]{1,0:T(8,128)S(1)}, f32[64,512]{1,0:T(8,128)S(1)}, u32[]{:S(2)}, u32[]{:S(2)}) collective-permute-start(f32[64,512]{1,0:T(8,128)S(1)} %add_add_fusion.kept), channel_id=1, source_target_pairs={{0,1},{1,0},{2,3},{3,2},{4,5},{5,4},{6,7},{7,6},{8,9},{9,8},{10,11... | collective-permute-start | bytes 393224 | tf_op jit(solution)/shard_map/ppermute | solution.py:439
  23.9 9.9 %collective-permute-start.6 = (f32[64,512]{1,0:T(8,128)S(1)}, f32[64,512]{1,0:T(8,128)S(1)}, u32[]{:S(2)}, u32[]{:S(2)}) collective-permute-start(f32[64,512]{1,0:T(8,128)S(1)} %add_add_fusion.kept), channel_id=1, source_target_pairs={{1,3},{3,1},{5,7},{7,5},{9,11},{11,9},{13,15},{15,13},{17,19},{19,... | collective-permute-start | bytes 393224 | tf_op jit(solution)/shard_map/ppermute | solution.py:471
  26.3 11.6 %collective-permute-start.10 = (f16[128,1024]{1,0:T(8,128)(2,1)S(1)}, f16[128,1024]{1,0:T(8,128)(2,1)S(1)}, u32[]{:S(2)}, u32[]{:S(2)}) collective-permute-start(f16[128,1024]{1,0:T(8,128)(2,1)S(1)} %convert_element_type.68), channel_id=1, source_target_pairs={{0,2},{2,0},{1,3},{3,1},{4,6},{6,4},{5,7},{7,5},{8,10},{10,8},{9,1... | collective-permute-start | bytes 786440 | tf_op jit(solution)/shard_map/ppermute | solution.py:439
  28.0 13.2 %collective-permute-start.9 = (f16[128,1024]{1,0:T(8,128)(2,1)S(1)}, f16[128,1024]{1,0:T(8,128)(2,1)S(1)}, u32[]{:S(2)}, u32[]{:S(2)}) collective-permute-start(f16[128,1024]{1,0:T(8,128)(2,1)S(1)} %convert_element_type.66), channel_id=1, source_target_pairs={{0,2},{2,0},{1,3},{3,1},{4,6},{6,4},{5,7},{7,5},{8,10},{10,8},{9,1... | collective-permute-start | bytes 786440 | tf_op jit(solution)/shard_map/ppermute | solution.py:439
  30.6 16.2 %collective-permute-start.8 = (f16[128,1024]{1,0:T(8,128)(2,1)S(1)}, f16[128,1024]{1,0:T(8,128)(2,1)S(1)}, u32[]{:S(2)}, u32[]{:S(2)}) collective-permute-start(f16[128,1024]{1,0:T(8,128)(2,1)S(1)} %convert_element_type.64), channel_id=1, source_target_pairs={{0,2},{2,0},{1,3},{3,1},{4,6},{6,4},{5,7},{7,5},{8,10},{10,8},{9,1... | collective-permute-start | bytes 786440 | tf_op jit(solution)/shard_map/ppermute | solution.py:439
  32.3 20.2 %collective-permute-start.7 = (f16[128,1024]{1,0:T(8,128)(2,1)S(1)}, f16[128,1024]{1,0:T(8,128)(2,1)S(1)}, u32[]{:S(2)}, u32[]{:S(2)}) collective-permute-start(f16[128,1024]{1,0:T(8,128)(2,1)S(1)} %convert_element_type.62), channel_id=1, source_target_pairs={{0,2},{2,0},{1,3},{3,1},{4,6},{6,4},{5,7},{7,5},{8,10},{10,8},{9,1... | collective-permute-start | bytes 786440 | tf_op jit(solution)/shard_map/ppermute | solution.py:439
  34.9 23.2 %collective-permute-start.13 = (f16[128,1024]{1,0:T(8,128)(2,1)S(1)}, f16[128,1024]{1,0:T(8,128)(2,1)S(1)}, u32[]{:S(2)}, u32[]{:S(2)}) collective-permute-start(f16[128,1024]{1,0:T(8,128)(2,1)S(1)} %convert_element_type.72), channel_id=1, source_target_pairs={{0,2},{2,0},{1,3},{3,1},{4,6},{6,4},{5,7},{7,5},{8,10},{10,8},{9,1... | collective-permute-start | bytes 786440 | tf_op jit(solution)/shard_map/ppermute | solution.py:439
  53.5 1.7 %collective-permute-start.11 = (f32[64,128]{1,0:T(8,128)S(1)}, f32[64,128]{1,0:T(8,128)S(1)}, u32[]{:S(2)}, u32[]{:S(2)}) collective-permute-start(f32[64,128]{1,0:T(8,128)S(1)} %get-tuple-element.77), channel_id=1, source_target_pairs={{0,1},{1,0},{2,3},{3,2},{4,5},{5,4},{6,7},{7,6},{8,9},{9,8},{10,11... | collective-permute-start | bytes 98312 | tf_op jit(solution)/shard_map/ppermute | solution.py:439
  55.2 3.9 %collective-permute-start.12 = (f32[64,128]{1,0:T(8,128)S(1)}, f32[64,128]{1,0:T(8,128)S(1)}, u32[]{:S(2)}, u32[]{:S(2)}) collective-permute-start(f32[64,128]{1,0:T(8,128)S(1)} %add.31), channel_id=1, source_target_pairs={{0,2},{2,0},{1,3},{3,1},{4,6},{6,4},{5,7},{7,5},{8,10},{10,8},{9,1... | collective-permute-start | bytes 98312 | tf_op jit(solution)/shard_map/ppermute | solution.py:439
  59.1 19.0 %collective-permute-start.20 = (f16[128,2048]{1,0:T(8,128)(2,1)S(1)}, f16[128,2048]{1,0:T(8,128)(2,1)S(1)}, u32[]{:S(2)}, u32[]{:S(2)}) collective-permute-start(f16[128,2048]{1,0:T(8,128)(2,1)S(1)} %convert_element_type.71), channel_id=1, source_target_pairs={{0,2},{2,0},{1,3},{3,1},{4,6},{6,4},{5,7},{7,5},{8,10},{10,8},{9,1... | collective-permute-start | bytes 1572872 | tf_op jit(solution)/shard_map/ppermute | solution.py:439
  60.5 5.7 %collective-permute-start.16 = (f32[64,128]{1,0:T(8,128)S(1)}, f32[64,128]{1,0:T(8,128)S(1)}, u32[]{:S(2)}, u32[]{:S(2)}) collective-permute-start(f32[64,128]{1,0:T(8,128)S(1)} %add.32), channel_id=1, source_target_pairs={{0,12},{4,8},{8,4},{12,0},{1,13},{5,9},{9,5},{13,1},{2,14},{6,10},... | collective-permute-start | bytes 98312 | tf_op jit(solution)/shard_map/ppermute | solution.py:443
  63.0 4.8 %collective-permute-start.15 = (f32[64,128]{1,0:T(8,128)S(1)}, f32[64,128]{1,0:T(8,128)S(1)}, u32[]{:S(2)}, u32[]{:S(2)}) collective-permute-start(f32[64,128]{1,0:T(8,128)S(1)} %add.32), channel_id=1, source_target_pairs={{0,8},{4,12},{8,0},{12,4},{1,9},{5,13},{9,1},{13,5},{2,10},{6,14},... | collective-permute-start | bytes 98312 | tf_op jit(solution)/shard_map/ppermute | solution.py:443
  63.1 4.7 %collective-permute-start.14 = (f32[64,128]{1,0:T(8,128)S(1)}, f32[64,128]{1,0:T(8,128)S(1)}, u32[]{:S(2)}, u32[]{:S(2)}) collective-permute-start(f32[64,128]{1,0:T(8,128)S(1)} %add.32), channel_id=1, source_target_pairs={{0,4},{4,0},{8,12},{12,8},{1,5},{5,1},{9,13},{13,9},{2,6},{6,2},{1... | collective-permute-start | bytes 98312 | tf_op jit(solution)/shard_map/ppermute | solution.py:443
  64.9 13.1 %collective-permute-start.19 = (f16[128,1024]{1,0:T(8,128)(2,1)S(1)}, f16[128,1024]{1,0:T(8,128)(2,1)S(1)}, u32[]{:S(2)}, u32[]{:S(2)}) collective-permute-start(f16[128,1024]{1,0:T(8,128)(2,1)S(1)} %convert_element_type.70), channel_id=1, source_target_pairs={{0,2},{2,0},{1,3},{3,1},{4,6},{6,4},{5,7},{7,5},{8,10},{10,8},{9,1... | collective-permute-start | bytes 786440 | tf_op jit(solution)/shard_map/ppermute | solution.py:439
  67.8 1.3 %collective-permute-start.17 = (f32[64,128]{1,0:T(8,128)S(1)}, f32[64,128]{1,0:T(8,128)S(1)}, u32[]{:S(2)}, u32[]{:S(2)}) collective-permute-start(f32[64,128]{1,0:T(8,128)S(1)} %add_add_fusion.1.kept), channel_id=1, source_target_pairs={{0,1},{1,0},{2,3},{3,2},{4,5},{5,4},{6,7},{7,6},{8,9},{9,8},{10,11... | collective-permute-start | bytes 98312 | tf_op jit(solution)/shard_map/ppermute | solution.py:439
  74.2 1.3 %collective-permute-start.18 = (f32[64,512]{1,0:T(8,128)S(1)}, f32[64,512]{1,0:T(8,128)S(1)}, u32[]{:S(2)}, u32[]{:S(2)}) collective-permute-start(f32[64,512]{1,0:T(8,128)S(1)} %collective-permute-done.6.theirs), channel_id=1, source_target_pairs={{0,1},{1,0},{2,3},{3,2},{4,5},{5,4},{6,7},{7,6},{8,9},{9,8},{10,11... | collective-permute-start | bytes 393224 | tf_op jit(solution)/shard_map/ppermute | solution.py:439
